TPU v7x, 128 devices: a whole 4x4x4 slice. The times are simulated.
128 devices in a mesh: row: 4 (over y), col: 32 (over z, x, core).
Axes of the slice: x: 4, y: 4, z: 4, core: 2. Of those that a mesh axis runs over, the one named last changes fastest.
Arguments:
- hidden: bfloat16 [24576, 1536], P('col'), may hold values from -6 to 6
- w_zx: bfloat16 [1536, 4096], P('col', 'row'), may hold values from -0.15625 to 0.15625
- w_bc: bfloat16 [1536, 256], P('col'), may hold values from -0.15625 to 0.15625
- w_dt: bfloat16 [1536, 32], P('col', 'row'), may hold values from -0.15625 to 0.15625
- w_out: bfloat16 [1536, 2048], P('col', 'row'), may hold values from -0.125 to 0.125
- dt_bias: float32 [32], P('row'), may hold values from -4 to -1
- a_log: float32 [32], P('row'), may hold values from -3 to 1
- d_skip: float32 [32], P('row'), may hold values from 0.5 to 1.5
- conv_x_w: float32 [4, 2048], P(None, 'row'), may hold values from -2 to 2
- conv_x_b: float32 [2048], P('row'), may hold values from -1.5 to 1.5
- conv_bc_w: float32 [4, 256], replicated, may hold values from -2 to 2
- conv_bc_b: float32 [256], replicated, may hold values from -1.5 to 1.5
- norm_gain: float32 [2048], P('row'), may hold values from 0.1 to 1.9
- prev_state: bfloat16 [768, 32, 64, 128], P('col', 'row'), may hold values from -3 to 3
- prev_edge_x: bfloat16 [768, 3, 2048], P('col', None, 'row'), may hold values from -6 to 6
- prev_edge_bc: bfloat16 [768, 3, 256], P('col'), may hold values from -6 to 6
- holder: int32 [1536], replicated, may hold values from 0 to 31, as said below
- continued: int32 [1536], replicated, may hold values from 0 to 1, as said below
- owner: int32 [1536], replicated, may hold values from 0 to 31, as said below
- accepted: int32 [1536], replicated, may hold values from 0 to 16
Outputs:
- mixed: bfloat16 [24576, 1536], P('col', 'row')
- new_state: bfloat16 [1536, 32, 64, 128], P('col', 'row')
- new_edge_x: bfloat16 [1536, 3, 2048], P('col', None, 'row')
- new_edge_bc: bfloat16 [1536, 3, 256], P('col')
Inputs may be any that keep to these rules, and one draw needn't show every extreme that they name: Only read where continued is 1. Each holder holds exactly 24 continued requests, in request order in its slots; one holder holds at most 2 continued requests of one aligned block of 48 requests, and some holder holds that many. Exactly 24 requests of each aligned block of 48 requests are continued. Where continued is 1, owner equals holder. Each owner receives exactly 48 requests; of one aligned block of 48 requests at most 2 continued and at most 2 others go to one owner, at most 4 in all, and that many in some block.
All inputs are finite; a program needn't handle non-finite values.
Results may differ from a plain program's by a relative error of at most 0.0072.
Values may be sent and summed in bfloat16 or wider, within the bound.
A program may use at most 192 MiB of HBM per device.

v0:
```python
import jax
import jax.numpy as jnp
from jax import lax
from jax.sharding import PartitionSpec as P

HEAD_DIM = 64
STATE = 128
KCONV = 4
LEN = 16
INNER = 2048


def ranks_of(values, live, count):
    onehot = (
        (values[:, None] == jnp.arange(count, dtype=jnp.int32)[None, :]) & live[:, None]
    ).astype(jnp.int32)
    before = jnp.cumsum(onehot, axis=0) - onehot
    return jnp.sum(before * onehot, axis=1)


def conv_silu(edge, fresh, weight, bias):
    length = fresh.shape[1]
    series = jnp.concatenate([edge, fresh], axis=1).astype(jnp.float32)
    total = bias + weight[0] * series[:, 0:length]
    for shift in range(1, weight.shape[0]):
        total = total + weight[shift] * series[:, shift : shift + length]
    return jax.nn.silu(total).astype(jnp.bfloat16)


def last_rows(edge, fresh, accepted):
    keep = edge.shape[1]
    series = jnp.concatenate([edge, fresh], axis=1)
    return jax.vmap(lambda rows, start: lax.dynamic_slice_in_dim(rows, start, keep, 0))(
        series, accepted
    )


def pack_rows(source, index, valid):
    picked = jnp.take(source, index, axis=0)
    shape = (valid.shape[0],) + (1,) * (source.ndim - 1)
    return jnp.where(valid.reshape(shape), picked, jnp.zeros((), source.dtype))


def per_device(
    hidden,
    w_zx,
    w_bc,
    w_dt,
    w_out,
    dt_bias,
    a_log,
    d_skip,
    conv_x_w,
    conv_x_b,
    conv_bc_w,
    conv_bc_b,
    norm_gain,
    prev_state,
    prev_edge_x,
    prev_edge_bc,
    holder,
    continued,
    owner,
    accepted,
):
    highest = lax.Precision.HIGHEST
    col_count = lax.axis_size("col")
    col_index = lax.axis_index("col")
    token_count = hidden.shape[0]
    request_count = token_count // LEN
    heads_here = dt_bias.shape[0]
    inner_here = heads_here * HEAD_DIM
    total_requests = holder.shape[0]
    decay_rate = -jnp.exp(a_log)
    full_zx, full_bc, full_dt, full_out = (
        lax.all_gather(w_zx, "col", axis=0, tiled=True),
        lax.all_gather(w_bc, "col", axis=0, tiled=True),
        lax.all_gather(w_dt, "col", axis=0, tiled=True),
        lax.all_gather(w_out, "col", axis=0, tiled=True),
    )
    proj_zx = jnp.dot(hidden, full_zx, preferred_element_type=jnp.float32).astype(jnp.bfloat16)
    proj_zx = proj_zx.reshape(request_count, LEN, heads_here, 2 * HEAD_DIM)
    gate_in = proj_zx[..., :HEAD_DIM]
    x_in = proj_zx[..., HEAD_DIM:].reshape(request_count, LEN, inner_here)
    bc_flat = jnp.dot(hidden, full_bc, preferred_element_type=jnp.float32).astype(jnp.bfloat16)
    proj_bc = bc_flat.reshape(request_count, LEN, 2 * STATE)
    dt_raw = jnp.dot(hidden, full_dt, preferred_element_type=jnp.float32).reshape(
        request_count, LEN, heads_here
    )
    live_all = continued == 1
    group_of = jnp.arange(total_requests, dtype=jnp.int32) // request_count
    cap_fetch = 2 * ((request_count // 4 + col_count - 1) // col_count)
    mine_held = live_all & (holder == col_index)
    held_int = mine_held.astype(jnp.int32)
    cache_slot = jnp.cumsum(held_int) - held_int
    held_grid = held_int.reshape(col_count, request_count)
    group_rank = (jnp.cumsum(held_grid, axis=1) - held_grid).reshape(total_requests)
    send_key = group_of * cap_fetch + group_rank
    slot_ids = jnp.arange(col_count * cap_fetch, dtype=jnp.int32)
    send_match = ((send_key[None, :] == slot_ids[:, None]) & mine_held[None, :]).astype(jnp.int32)
    send_from = jnp.sum(send_match * cache_slot[None, :], axis=1)
    send_live = jnp.sum(send_match, axis=1) > 0
    my_holder = lax.dynamic_slice_in_dim(holder, col_index * request_count, request_count)
    my_live = lax.dynamic_slice_in_dim(live_all, col_index * request_count, request_count)
    my_accepted = lax.dynamic_slice_in_dim(accepted, col_index * request_count, request_count)
    my_owner = lax.dynamic_slice_in_dim(owner, col_index * request_count, request_count)
    recv_index = jnp.where(
        my_live, my_holder * cap_fetch + ranks_of(my_holder, my_live, col_count), 0
    )
    local_ids = jnp.arange(request_count, dtype=jnp.int32)
    owned = owner == col_index
    owned_int = owned.astype(jnp.int32)
    owned_slot = jnp.cumsum(owned_int) - owned_int
    out_state = pack_rows(prev_state, send_from, send_live).reshape(
        col_count, cap_fetch, heads_here, HEAD_DIM, STATE
    )
    out_edge_x = pack_rows(prev_edge_x, send_from, send_live).reshape(
        col_count, cap_fetch, KCONV - 1, inner_here
    )
    out_edge_bc = pack_rows(prev_edge_bc, send_from, send_live).reshape(
        col_count, cap_fetch, KCONV - 1, 2 * STATE
    )
    got_state, got_edge_x, got_edge_bc = (
        lax.all_to_all(out_state, "col", split_axis=0, concat_axis=0, tiled=True),
        lax.all_to_all(out_edge_x, "col", split_axis=0, concat_axis=0, tiled=True),
        lax.all_to_all(out_edge_bc, "col", split_axis=0, concat_axis=0, tiled=True),
    )
    start_state = pack_rows(
        got_state.reshape(col_count * cap_fetch, heads_here, HEAD_DIM, STATE), recv_index, my_live
    ).astype(jnp.float32)
    edge_x = pack_rows(
        got_edge_x.reshape(col_count * cap_fetch, KCONV - 1, inner_here), recv_index, my_live
    )
    edge_bc = pack_rows(
        got_edge_bc.reshape(col_count * cap_fetch, KCONV - 1, 2 * STATE), recv_index, my_live
    )
    number = x_in.shape[0]
    x_conv = (
        conv_silu(edge_x, x_in, conv_x_w, conv_x_b)
        .astype(jnp.float32)
        .reshape(number, LEN, heads_here, HEAD_DIM)
    )
    bc_conv = conv_silu(edge_bc, proj_bc, conv_bc_w, conv_bc_b).astype(jnp.float32)
    b_in = bc_conv[..., :STATE]
    c_in = bc_conv[..., STATE:]
    step_size = jax.nn.softplus(dt_raw + dt_bias)
    log_decay = jnp.cumsum(step_size * decay_rate, axis=1)
    positions = jnp.arange(LEN, dtype=jnp.int32)
    later = positions[:, None] >= positions[None, :]
    spread = log_decay[:, :, None, :] - log_decay[:, None, :, :]
    within = jnp.where(later[None, :, :, None], jnp.exp(jnp.minimum(spread, 0.0)), 0.0)
    scores = jnp.einsum("rtn,rsn->rts", c_in, b_in, precision=highest)
    mixing = within * scores[..., None] * step_size[:, None, :, :]
    scan_out = jnp.einsum("rtsh,rshp->rthp", mixing, x_conv, precision=highest)
    scan_out = scan_out + jnp.exp(log_decay)[..., None] * jnp.einsum(
        "rhpn,rtn->rthp", start_state, c_in, precision=highest
    )
    scan_out = scan_out + d_skip[None, None, :, None] * x_conv
    padded_decay = jnp.concatenate(
        [jnp.zeros((number, 1, heads_here), jnp.float32), log_decay], axis=1
    )
    pick_mask = (jnp.arange(LEN + 1, dtype=jnp.int32)[None, :] == my_accepted[:, None]).astype(
        jnp.float32
    )
    reach = jnp.sum(pick_mask[:, :, None] * padded_decay, axis=1)
    before = positions[None, :] < my_accepted[:, None]
    weight_s = (
        jnp.where(before[:, :, None], jnp.exp(jnp.minimum(reach[:, None, :] - log_decay, 0.0)), 0.0)
        * step_size
    )
    chosen = jnp.exp(reach)[:, :, None, None] * start_state + jnp.einsum(
        "rsh,rshp,rsn->rhpn", weight_s, x_conv, b_in, precision=highest
    )
    scan_out, chosen_state, chosen_edge_x, chosen_edge_bc = (
        scan_out,
        chosen.astype(jnp.bfloat16),
        last_rows(edge_x, x_in, my_accepted),
        last_rows(edge_bc, proj_bc, my_accepted),
    )
    cap_return = 4 * ((request_count // 4 + col_count - 1) // col_count)
    everyone = jnp.ones((request_count,), dtype=bool)
    return_key = my_owner * cap_return + ranks_of(my_owner, everyone, col_count)
    return_ids = jnp.arange(col_count * cap_return, dtype=jnp.int32)
    return_match = (return_key[None, :] == return_ids[:, None]).astype(jnp.int32)
    return_from = jnp.sum(return_match * local_ids[None, :], axis=1)
    return_live = jnp.sum(return_match, axis=1) > 0
    back_state = pack_rows(chosen_state, return_from, return_live).reshape(
        col_count, cap_return, heads_here, HEAD_DIM, STATE
    )
    back_edge_x = pack_rows(chosen_edge_x, return_from, return_live).reshape(
        col_count, cap_return, KCONV - 1, inner_here
    )
    back_edge_bc = pack_rows(chosen_edge_bc, return_from, return_live).reshape(
        col_count, cap_return, KCONV - 1, 2 * STATE
    )
    came_state, came_edge_x, came_edge_bc = (
        lax.all_to_all(back_state, "col", split_axis=0, concat_axis=0, tiled=True),
        lax.all_to_all(back_edge_x, "col", split_axis=0, concat_axis=0, tiled=True),
        lax.all_to_all(back_edge_bc, "col", split_axis=0, concat_axis=0, tiled=True),
    )
    pool_state = came_state.reshape(col_count * cap_return, heads_here, HEAD_DIM, STATE)
    pool_edge_x = came_edge_x.reshape(col_count * cap_return, KCONV - 1, inner_here)
    pool_edge_bc = came_edge_bc.reshape(col_count * cap_return, KCONV - 1, 2 * STATE)
    owned_grid = owned_int.reshape(col_count, request_count)
    group_owned = (jnp.cumsum(owned_grid, axis=1) - owned_grid).reshape(total_requests)
    source_flat = group_of * cap_return + group_owned
    pick_match = ((owned_slot[None, :] == local_ids[:, None]) & owned[None, :]).astype(jnp.int32)
    pick = jnp.sum(pick_match * source_flat[None, :], axis=1)
    new_state = jnp.take(pool_state, pick, axis=0)
    new_edge_x = jnp.take(pool_edge_x, pick, axis=0)
    new_edge_bc = jnp.take(pool_edge_bc, pick, axis=0)
    gated = (scan_out * jax.nn.silu(gate_in.astype(jnp.float32))).reshape(token_count, inner_here)
    totals = lax.psum(jnp.sum(gated * gated, axis=1), "row")
    normed = (gated * lax.rsqrt(totals / INNER + 1e-05)[:, None] * norm_gain).astype(jnp.bfloat16)
    partial_out = lax.dot_general(
        normed, full_out, (((1,), (1,)), ((), ())), preferred_element_type=jnp.float32
    )
    mixed = lax.psum_scatter(partial_out, "row", scatter_dimension=1, tiled=True).astype(
        jnp.bfloat16
    )
    return (mixed, new_state, new_edge_x, new_edge_bc)


def solution(mesh):
    return jax.shard_map(
        per_device,
        mesh=mesh,
        in_specs=(
            P("col", None),
            P("col", "row"),
            P("col", None),
            P("col", "row"),
            P("col", "row"),
            P("row"),
            P("row"),
            P("row"),
            P(None, "row"),
            P("row"),
            P(),
            P(),
            P("row"),
            P("col", "row", None, None),
            P("col", None, "row"),
            P("col", None, None),
            P(),
            P(),
            P(),
            P(),
        ),
        out_specs=(
            P("col", "row"),
            P("col", "row", None, None),
            P("col", None, "row"),
            P("col", None, None),
        ),
        check_vma=False,
    )
```

profile of v0, /device:TPU:1, one launch (start us, length us, event | category | flops | bytes accessed | tf_op | source)
XLA Modules:
  0.0 580.7 jit_solution(11812744949949448263)
XLA Ops:
  7.2 0.7 all-gather.4.cloned.1.call-update
  7.9 1.4 convert_bitcast_fusion
  10.8 1.7 gather_fusion.2
  12.5 0.9 broadcast_select_fusion.5
  13.4 9.4 %all-to-all-start.1 = ((bf16[32,2,3,256]{3,1,2,0:T(2,128)(2,1)}), bf16[32,2,3,256]{3,1,2,0:T(2,128)(2,1)S(1)}, u32[]{:S(2)}, u32[]{:S(2)}) async-start(bf16[32,2,3,256]{3,1,2,0:T(2,128)(2,1)} %broadcast_select_fusion.5), calls=%async_computation.1 | async-start | bytes 196608 | tf_op jit(solution)/shard_map/all_to_all | solution.py:126
  22.9 1.2 gather_fusion
  24.1 0.8 gather.67
  24.8 1.9 broadcast_select_fusion.2
  26.8 5.4 gather_fusion.4
  32.1 7.4 %all-to-all-start = ((bf16[32,2,3,512]{3,1,2,0:T(2,128)(2,1)}), bf16[32,2,3,512]{3,1,2,0:T(2,128)(2,1)S(1)}, u32[]{:S(2)}, u32[]{:S(2)}) async-start(bf16[32,2,3,512]{3,1,2,0:T(2,128)(2,1)} %broadcast_select_fusion.2), calls=%async_computation | async-start | bytes 393216 | tf_op jit(solution)/shard_map/all_to_all | solution.py:125
  39.6 7.6 %select_select_fusion.1 = bf16[32,2,8,64,128]{4,3,2,1,0:T(8,128)(2,1)} fusion(bf16[32,2,8,64,128]{4,3,2,1,0:T(8,128)(2,1)} %bitcast.91, pred[32,2]{1,0:T(8,128)(4,1)S(1)} %compare_and_fusion.1, pred[32,2]{1,0:T(8,128)(4,1)S(1)} %gt.44), kind=kLoop, calls=%fused_computation.16 | loop fusion | flops 8388608 | bytes 16777344 | tf_op jit(solution)/shard_map/jit(_where)/select_n | solution.py:41
  47.2 24.5 %all-gather = bf16[32,48,8]{1,2,0:T(8,128)(2,1)S(1)} all-gather(bf16[1,48,8]{1,2,0:T(8,128)(2,1)S(1)} %bitcast.108), channel_id=1, replica_groups=mesh['row'=4,'col'=32] {'col'}, dimensions={0}, use_global_device_ids=true | all-gather | bytes 25344 | tf_op jit(solution)/shard_map/all_gather | solution.py:78
  71.9 5.4 all-to-all-start.2
  77.3 0.7 fusion.68
  78.0 0.8 dynamic_slice.13
  78.8 0.8 dynamic_slice.14
  80.2 0.8 fusion.60
  80.9 1.0 fusion.67
  83.5 0.8 multiply_add_fusion
  84.7 0.8 copy.159
  85.7 0.8 compare_and_fusion.4
  86.5 110.1 %all_gather.14 = bf16[1536,256]{1,0:T(8,128)(2,1)S(1)} all-gather(bf16[48,256]{1,0:T(8,128)(2,1)S(1)} %copy-done.11), channel_id=1, replica_groups=mesh['row'=4,'col'=32] {'col'}, dimensions={0}, use_global_device_ids=true | all-gather | bytes 811008 | tf_op jit(solution)/shard_map/all_gather | solution.py:77
  196.7 2.4 convolution_convert_fusion.1
  200.3 1.2 gather_fusion.13
  201.6 0.8 gather_fusion.10
  202.4 0.9 fusion.38
  203.9 0.7 gather_fusion.1
  204.8 0.7 copy_dynamic-update-slice_fusion.1
  205.5 5.2 fusion.23
  211.2 2.4 fusion.64
  213.6 2.7 reshape.449
  216.3 1.3 copy_dynamic-update-slice_fusion
  217.6 2.3 gather_fusion.12
  219.9 1.4 convert_element_type.65
  221.5 1.8 gather_fusion.8
  223.3 1.4 multiply_convert_fusion.1
  224.6 0.8 reshape.450
  225.5 2.1 fusion.33
  227.6 6.7 %all-to-all-start.5 = ((bf16[32,4,3,256]{3,1,2,0:T(4,128)(2,1)}), bf16[32,4,3,256]{3,1,2,0:T(4,128)(2,1)S(1)}, u32[]{:S(2)}, u32[]{:S(2)}) async-start(bf16[32,4,3,256]{3,1,2,0:T(4,128)(2,1)} %fusion.38), calls=%async_computation.6 | async-start | bytes 393216 | tf_op jit(solution)/shard_map/all_to_all | solution.py:199
  234.3 8.4 %gather_fusion.5 = bf16[48,8,64,128]{3,2,1,0:T(8,128)(2,1)} fusion(bf16[64,8,64,128]{3,2,1,0:T(8,128)(2,1)} %bitcast.20, s32[1024]{0:T(1024)S(1)} %pad_clamp_fusion.2), kind=kCustom, calls=%fused_computation.5 | custom fusion | bytes 12583104 | tf_op jit(solution)/shard_map/jit(_take)/gather | solution.py:39
  242.7 16.3 %add_convert_fusion = bf16[48,8,64,128]{3,2,1,0:T(8,128)(2,1)} fusion(f32[48,8]{1,0:T(8,128)S(1)} %copy-done.12, f32[48,16,8]{1,2,0:T(8,128)S(1)} %copy-done.9, bf16[48,16,8,64]{3,2,0,1:T(8,128)(2,1)S(1)} %reshape.450, bf16[48,16,256]{2,1,0:T(8,128)(2,1)S(1)} %multiply_convert_fusion.3, bf16[48,8,64,128]{3,2,1,0:T(8,128)(2,1)} %gather_fusion.5, ...), kind=kOutput, calls=%fused_computation.15 | convolution fusion | flops 623640576 | bytes 14574592 | tf_op jit(solution)/shard_map/rsh,rshp,rsn->rhpn/dot_general | solution.py:171
  259.1 10.8 %gather_fusion.6 = bf16[128,8,64,128]{3,2,1,0:T(8,128)(2,1)} fusion(bf16[48,8,64,128]{3,2,1,0:T(8,128)(2,1)} %add_convert_fusion, s32[1024]{0:T(1024)S(1)} %pad_clamp_fusion.1), kind=kCustom, calls=%fused_computation.6 | custom fusion | bytes 33554944 | tf_op jit(solution)/shard_map/jit(_take)/gather | solution.py:39
  269.8 7.4 %all-to-all-start.4 = ((bf16[32,4,3,512]{3,1,2,0:T(4,128)(2,1)}), bf16[32,4,3,512]{3,1,2,0:T(4,128)(2,1)S(1)}, u32[]{:S(2)}, u32[]{:S(2)}) async-start(bf16[32,4,3,512]{3,1,2,0:T(4,128)(2,1)} %fusion.33), calls=%async_computation.5 | async-start | bytes 786432 | tf_op jit(solution)/shard_map/all_to_all | solution.py:198
  277.2 14.3 %select_select_fusion = bf16[32,4,8,64,128]{4,3,2,1,0:T(8,128)(2,1)} fusion(bf16[32,4,8,64,128]{4,3,2,1,0:T(8,128)(2,1)} %bitcast.90, pred[32,4]{1,0:T(8,128)(4,1)S(1)} %compare_and_fusion, pred[32,4]{1,0:T(8,128)(4,1)S(1)} %gt.49), kind=kLoop, calls=%fused_computation.14 | loop fusion | flops 16777216 | bytes 33554688 | tf_op jit(solution)/shard_map/jit(_where)/select_n | solution.py:41
  291.6 0.7 copy-done.4
  292.3 7.4 %all-to-all-start.3 = ((bf16[32,4,8,64,128]{4,3,2,1,0:T(8,128)(2,1)}), bf16[32,4,8,64,128]{4,3,2,1,0:T(8,128)(2,1)}, u32[]{:S(2)}, u32[]{:S(2)}) async-start(bf16[32,4,8,64,128]{4,3,2,1,0:T(8,128)(2,1)} %select_select_fusion), calls=%async_computation.4 | async-start | bytes 33554432 | tf_op jit(solution)/shard_map/all_to_all | solution.py:197
  299.8 0.7 all-gather.6.cloned.1.call-update
  300.8 0.8 copy.151
  301.6 0.9 copy.147
  302.5 0.9 copy.153
  303.7 4.3 fusion.5
  308.0 9.0 %multiply_reduce_fusion = (f32[48,16]{1,0:T(8,128)}, f32[48,16,8,64]{3,1,2,0:T(8,128)}) fusion(bf16[48,16,8,64]{3,2,1,0:T(8,128)(2,1)S(1)} %copy-done.6, bf16[48,16,8,64]{3,2,0,1:T(8,128)(2,1)S(1)} %reshape.450, f32[8]{0:T(128)S(1)} %copy-done.24, bf16[48,8,64,128]{3,2,1,0:T(8,128)(2,1)} %gather_fusion.5, pred[48]{0:T(512)(128)(4,1)S(1)} %copy-done.17, ...), kind=kOutput, calls=%fused_computation.29 | convolution fusion | flops 112065792 | bytes 14553600 | tf_op jit(solution)/shard_map/rhpn,rtn->rthp/dot_general | solution.py:155
  317.0 0.8 reduce_sum.99
  317.9 3.3 copy.156
  321.2 1.7 reshape.322
  322.9 9.7 %psum.7 = f32[768]{0:T(1024)S(1)} all-reduce(f32[768]{0:T(1024)S(1)} %reduce_sum.99), channel_id=1, replica_groups=mesh['row'=4,'col'=32] {'row'}, use_global_device_ids=true, to_apply=%region_9.10 | all-reduce | flops 768 | bytes 6144 | tf_op jit(solution)/shard_map/psum | solution.py:213
  332.6 160.2 %all-gather.6.cloned.1.call-done = bf16[1536,512]{1,0:T(8,128)(2,1)} async-done(((bf16[48,512]{1,0:T(8,128)(2,1)}), bf16[1536,512]{1,0:T(8,128)(2,1)}) %all-gather.6.cloned.1.call-update) | async-done | bytes 1572880 | tf_op jit(solution)/shard_map/all_gather | solution.py:79
  492.8 5.5 fusion.26
  501.3 0.7 gather_fusion.9
  502.3 0.7 copy.167
  502.9 51.7 %reduce-scatter.2.cloned.1.call-done = f32[768,384]{1,0:T(8,128)} async-done(((f32[768,1536]{1,0:T(8,128)}), f32[768,384]{1,0:T(8,128)}) %reduce-scatter.2.cloned.1.call-update) | async-done | bytes 1179664 | tf_op jit(solution)/shard_map/reduce_scatter | solution.py:218
  554.6 2.1 convert_element_type.72
  556.8 10.8 %gather_fusion.7 = bf16[48,8,64,128]{3,2,1,0:T(8,128)(2,1)} fusion(bf16[128,8,64,128]{3,2,1,0:T(8,128)(2,1)} %bitcast.28, s32[1024]{0:T(1024)S(1)} %pad_clamp_fusion), kind=kCustom, calls=%fused_computation.7 | custom fusion | bytes 12583104 | tf_op jit(solution)/shard_map/jit(_take)/gather | solution.py:209
  567.6 6.3 %broadcast_select_fusion = bf16[48,8,64,128]{3,2,1,0:T(8,128)(2,1)} fusion(bf16[48,8,64,128]{3,2,1,0:T(8,128)(2,1)} %gather_fusion.7, pred[48]{0:T(512)(128)(4,1)S(1)} %compare_and_fusion.3), kind=kLoop, calls=%fused_computation.18 | loop fusion | flops 3145728 | bytes 12582960 | tf_op jit(solution)/shard_map/jit(_take)/select_n | solution.py:209
  (142 shorter events, 10.7 us)
Async XLA Ops:
  7.2 19.6 %copy-start = (bf16[24,8,64,128]{3,2,1,0:T(8,128)(2,1)S(1)}, bf16[24,8,64,128]{3,2,1,0:T(8,128)(2,1)}, u32[]{:S(2)}) copy-start(bf16[24,8,64,128]{3,2,1,0:T(8,128)(2,1)} %param.33) | copy-start | bytes 9437188
  7.2 15.7 %copy-start.2 = (bf16[24,3,512]{2,0,1:T(8,128)(2,1)S(1)}, bf16[24,3,512]{2,0,1:T(8,128)(2,1)}, u32[]{:S(2)}) copy-start(bf16[24,3,512]{2,0,1:T(8,128)(2,1)} %param.34) | copy-start | bytes 221188
  7.2 198.3 %all-gather.4.cloned.1.call-start = ((), (), s32[]{:S(2)}) async-start(), calls=%async_computation.7 | async-start | bytes 3244032 | tf_op jit(solution)/shard_map/all_gather | solution.py:76
  13.4 18.7 %all-to-all-start.1 = ((bf16[32,2,3,256]{3,1,2,0:T(2,128)(2,1)}), bf16[32,2,3,256]{3,1,2,0:T(2,128)(2,1)S(1)}, u32[]{:S(2)}, u32[]{:S(2)}) async-start(bf16[32,2,3,256]{3,1,2,0:T(2,128)(2,1)} %broadcast_select_fusion.5), calls=%async_computation.1 | async-start | bytes 196608 | tf_op jit(solution)/shard_map/all_to_all | solution.py:126
  32.1 39.8 %all-to-all-start = ((bf16[32,2,3,512]{3,1,2,0:T(2,128)(2,1)}), bf16[32,2,3,512]{3,1,2,0:T(2,128)(2,1)S(1)}, u32[]{:S(2)}, u32[]{:S(2)}) async-start(bf16[32,2,3,512]{3,1,2,0:T(2,128)(2,1)} %broadcast_select_fusion.2), calls=%async_computation | async-start | bytes 393216 | tf_op jit(solution)/shard_map/all_to_all | solution.py:125
  39.6 7.6 %copy-start.20 = (bf16[48,8]{0,1:T(8,128)(2,1)S(1)}, bf16[48,8]{0,1:T(8,128)(2,1)}, u32[]{:S(2)}) copy-start(bf16[48,8]{0,1:T(8,128)(2,1)} %param.23) | copy-start | bytes 2308
  71.9 5.4 copy-start.3
  71.9 8.0 %copy-start.23 = (f32[8]{0:T(128)S(1)}, f32[8]{0:T(128)}, u32[]{:S(2)}) copy-start(f32[8]{0:T(128)} %param.26) | copy-start | bytes 100
  71.9 8.0 %copy-start.22 = (f32[8]{0:T(128)S(1)}, f32[8]{0:T(128)}, u32[]{:S(2)}) copy-start(f32[8]{0:T(128)} %param.25) | copy-start | bytes 100
  71.9 155.7 %all-to-all-start.2 = ((bf16[32,2,8,64,128]{4,3,2,1,0:T(8,128)(2,1)}), bf16[32,2,8,64,128]{4,3,2,1,0:T(8,128)(2,1)}, u32[]{:S(2)}, u32[]{:S(2)}) async-start(bf16[32,2,8,64,128]{4,3,2,1,0:T(8,128)(2,1)} %select_select_fusion.1), calls=%async_computation.2 | async-start | bytes 16777216 | tf_op jit(solution)/shard_map/all_to_all | solution.py:124
  77.3 5.7 copy-start.19
  77.3 9.2 %copy-start.11 = (bf16[48,256]{1,0:T(8,128)(2,1)S(1)}, bf16[48,256]{1,0:T(8,128)(2,1)}, u32[]{:S(2)}) copy-start(bf16[48,256]{1,0:T(8,128)(2,1)} %param.22) | copy-start | bytes 73732
  77.3 119.3 %copy-start.18 = (f32[4,256]{1,0:T(4,128)S(1)}, f32[4,256]{1,0:T(4,128)}, u32[]{:S(2)}) copy-start(f32[4,256]{1,0:T(4,128)} %param.30) | copy-start | bytes 12292
  77.3 119.3 %copy-start.14 = (f32[4,512]{1,0:T(4,128)S(1)}, f32[4,512]{1,0:T(4,128)}, u32[]{:S(2)}) copy-start(f32[4,512]{1,0:T(4,128)} %param.28) | copy-start | bytes 24580
  86.5 118.2 %copy-start.15 = (pred[48]{0:T(512)(128)(4,1)}, pred[48]{0:T(512)(128)(4,1)S(1)}, u32[]{:S(2)}) copy-start(pred[48]{0:T(512)(128)(4,1)S(1)} %get-tuple-element.38) | copy-start | bytes 148
  199.1 4.1 copy-start.21
  227.6 42.2 %all-to-all-start.5 = ((bf16[32,4,3,256]{3,1,2,0:T(4,128)(2,1)}), bf16[32,4,3,256]{3,1,2,0:T(4,128)(2,1)S(1)}, u32[]{:S(2)}, u32[]{:S(2)}) async-start(bf16[32,4,3,256]{3,1,2,0:T(4,128)(2,1)} %fusion.38), calls=%async_computation.6 | async-start | bytes 393216 | tf_op jit(solution)/shard_map/all_to_all | solution.py:199
  234.3 8.4 %copy-start.9 = (f32[48,16,8]{1,2,0:T(8,128)S(1)}, f32[48,16,8]{1,2,0:T(8,128)}, u32[]{:S(2)}) copy-start(f32[48,16,8]{1,2,0:T(8,128)} %copy.159) | copy-start | bytes 73732
  234.3 8.4 %copy-start.12 = (f32[48,8]{1,0:T(8,128)S(1)}, f32[48,8]{1,0:T(8,128)}, u32[]{:S(2)}) copy-start(f32[48,8]{1,0:T(8,128)} %exp.50) | copy-start | bytes 4612
  234.3 8.4 %copy-start.16 = (pred[48]{0:T(512)(128)(4,1)S(1)}, pred[48]{0:T(512)(128)(4,1)}, u32[]{:S(2)}) copy-start(pred[48]{0:T(512)(128)(4,1)} %copy-done.15) | copy-start | bytes 148
  269.8 21.8 %copy-start.7 = (bf16[32,4,3,256]{3,1,2,0:T(4,128)(2,1)}, bf16[32,4,3,256]{3,1,2,0:T(4,128)(2,1)S(1)}, u32[]{:S(2)}) copy-start(bf16[32,4,3,256]{3,1,2,0:T(4,128)(2,1)S(1)} %all-to-all-done.5) | copy-start | bytes 589828
  269.8 21.8 %all-to-all-start.4 = ((bf16[32,4,3,512]{3,1,2,0:T(4,128)(2,1)}), bf16[32,4,3,512]{3,1,2,0:T(4,128)(2,1)S(1)}, u32[]{:S(2)}, u32[]{:S(2)}) async-start(bf16[32,4,3,512]{3,1,2,0:T(4,128)(2,1)} %fusion.33), calls=%async_computation.5 | async-start | bytes 786432 | tf_op jit(solution)/shard_map/all_to_all | solution.py:198
  291.6 0.7 copy-start.4
  292.3 264.5 %all-to-all-start.3 = ((bf16[32,4,8,64,128]{4,3,2,1,0:T(8,128)(2,1)}), bf16[32,4,8,64,128]{4,3,2,1,0:T(8,128)(2,1)}, u32[]{:S(2)}, u32[]{:S(2)}) async-start(bf16[32,4,8,64,128]{4,3,2,1,0:T(8,128)(2,1)} %select_select_fusion), calls=%async_computation.4 | async-start | bytes 33554432 | tf_op jit(solution)/shard_map/all_to_all | solution.py:197
  299.8 193.1 %all-gather.6.cloned.1.call-start = ((), (), s32[]{:S(2)}) async-start(), calls=%async_computation.8 | async-start | bytes 1622016 | tf_op jit(solution)/shard_map/all_gather | solution.py:79
  300.5 254.1 %reduce-scatter.2.cloned.1.call-start = ((), (), s32[]{:S(2)}) async-start(), calls=%async_computation.9 | async-start | bytes 5898240 | tf_op jit(solution)/shard_map/reduce_scatter | solution.py:218
  303.6 4.3 copy-start.6
  303.6 4.3 copy-start.10
  303.6 4.3 copy-start.17
  303.7 4.3 copy-start.24
  321.2 171.7 %copy-start.13 = (f32[512]{0:T(512)S(1)}, f32[512]{0:T(512)}, u32[]{:S(2)}) copy-start(f32[512]{0:T(512)} %param.32) | copy-start | bytes 6148
  498.3 1.2 copy-start.8
  498.3 2.7 copy-start.5
  567.6 6.3 %copy-start.1 = (bf16[24,8,64,128]{3,2,1,0:T(8,128)(2,1)S(1)}, bf16[24,8,64,128]{3,2,1,0:T(8,128)(2,1)}, u32[]{:S(2)}) copy-start(bf16[24,8,64,128]{3,2,1,0:T(8,128)(2,1)} %param.33) | copy-start | bytes 9437188
Sparse Core Ops, SparseCore 0:
  10.3 48.9 all-gather.3
  302.9 189.9 all-gather.5
  498.5 56.1 reduce-scatter.1
where the time goes:
time: 588 us; the launch traced here: 581 us
  waiting for transfers between devices  213 us (36%)
  blocking collectives  144 us (24%)
  local copies, waits for them, and re-layouts  72.5 us (12%)
  other arithmetic  47.9 us (8%)
  starting transfers between devices  44.1 us (8%)
  matrix products  43.7 us (7%)
  between operations  14.8 us (3%)
    all_gather x1, waiting for transfers between devices, per_device(): lax.all_gather(w_out, 'col', axis=0, tiled=True)  160 us
    all_gather x1, blocking collectives, per_device(): lax.all_gather(w_bc, 'col', axis=0, tiled=True)  110 us
    reduce_scatter x1, waiting for transfers between devices, per_device(): lax.psum_scatter(partial_out, 'row', scatter_dimension=1, tiled=True)  51.7 us
    gather x11, local copies, waits for them, and re-layouts, pack_rows(): picked = jnp.take(source, index, axis=0)  32.2 us
    select_n x8, other arithmetic, pack_rows(): return jnp.where(valid.reshape(shape), picked, jnp.zeros((), source.dtype))  28.1 us
    all_gather x1, blocking collectives, per_device(): lax.all_gather(w_dt, 'col', axis=0, tiled=True)  24.5 us
    dot_general x1, matrix products, per_device(): jnp.einsum('rsh,rshp,rsn->rhpn', weight_s, x_conv, b_in, precision=highest)  16.3 us
  transfers between devices with their start and end apart: 9, of which 2 were waited for; matrix products, arithmetic and copies ran while one was open for 25% of the time, Pallas kernels for 0%

commit v1 on v0

v1 whole, which is shorter than its diff:
```python
import jax
import jax.numpy as jnp
from jax import lax
from jax.sharding import PartitionSpec as P

HEAD_DIM = 64
STATE = 128
KCONV = 4
LEN = 16
INNER = 2048


def routing(owner, accepted, continued, col_index, request_count, cap):
    total = owner.shape[0]
    groups = total // request_count
    local = jnp.arange(request_count, dtype=jnp.int32)
    slots = jnp.arange(groups * cap, dtype=jnp.int32)
    mine = lax.dynamic_slice_in_dim(owner, col_index * request_count, request_count)
    earlier = local[None, :] < local[:, None]
    rank = jnp.sum(((mine[None, :] == mine[:, None]) & earlier).astype(jnp.int32), axis=1)
    home_key = mine * cap + rank
    send_from = jnp.sum(jnp.where(home_key[None, :] == slots[:, None], local[None, :], 0), axis=1)
    owned = (owner == col_index).reshape(groups, request_count)
    owned_int = owned.astype(jnp.int32)
    in_group = jnp.sum(jnp.where(earlier[None], owned_int[:, None, :], 0), axis=2)
    counts = jnp.sum(owned_int, axis=1)
    group = jnp.arange(groups, dtype=jnp.int32)
    before = jnp.sum(jnp.where(group[None, :] < group[:, None], counts[None, :], 0), axis=1)
    slot = jnp.where(owned, in_group + before[:, None], -1)
    match = slot[None] == local[:, None, None]

    def picked(values):
        return jnp.sum(jnp.where(match, values[None], 0), axis=(1, 2))

    pick = picked(group[:, None] * cap + in_group)
    own_accepted = picked(accepted.reshape(groups, request_count))
    own_cont = picked((continued == 1).astype(jnp.int32).reshape(groups, request_count))
    own_prev = jnp.sum(jnp.where(earlier, own_cont[None, :], 0), axis=1)
    back_from = jnp.sum(jnp.where(pick[None, :] == slots[:, None], local[None, :], 0), axis=1)
    return home_key, send_from, pick, own_accepted, own_cont, own_prev, back_from


def rows_of(source, index, live=None):
    ids = jnp.arange(source.shape[0], dtype=jnp.int32)
    hot = index[:, None] == ids[None, :]
    if live is not None:
        hot = hot & live[:, None]
    flat = source.reshape(source.shape[0], -1)
    out = jnp.dot(hot.astype(source.dtype), flat, preferred_element_type=jnp.float32)
    return out.astype(source.dtype).reshape((index.shape[0],) + source.shape[1:])


def conv_silu(edge, fresh, weight, bias):
    length = fresh.shape[1]
    series = jnp.concatenate([edge, fresh], axis=1).astype(jnp.float32)
    total = bias + weight[0] * series[:, 0:length]
    for shift in range(1, weight.shape[0]):
        total = total + weight[shift] * series[:, shift : shift + length]
    return jax.nn.silu(total).astype(jnp.bfloat16)


def last_rows(edge, fresh, accepted):
    keep = edge.shape[1]
    series = jnp.concatenate([edge, fresh], axis=1)
    ids = jnp.arange(series.shape[1], dtype=jnp.int32)
    picks = []
    for row in range(keep):
        hot = (ids[None, :] == accepted[:, None] + row)[:, :, None]
        picks.append(jnp.sum(jnp.where(hot, series, 0).astype(jnp.float32), axis=1))
    return jnp.stack(picks, axis=1).astype(edge.dtype)


def per_device(
    hidden,
    w_zx,
    w_bc,
    w_dt,
    w_out,
    dt_bias,
    a_log,
    d_skip,
    conv_x_w,
    conv_x_b,
    conv_bc_w,
    conv_bc_b,
    norm_gain,
    prev_state,
    prev_edge_x,
    prev_edge_bc,
    holder,
    continued,
    owner,
    accepted,
):
    highest = lax.Precision.HIGHEST
    col_count = lax.axis_size("col")
    col_index = lax.axis_index("col")
    row_index = lax.axis_index("row")
    row_count = lax.axis_size("row")
    token_count = hidden.shape[0]
    request_count = token_count // LEN
    heads_here = dt_bias.shape[0]
    inner_here = heads_here * HEAD_DIM
    slice_width = hidden.shape[1] // row_count
    decay_rate = -jnp.exp(a_log)
    cap = 4 * ((request_count // 4 + col_count - 1) // col_count)
    home_key, send_from, pick, my_accepted, own_cont, own_prev, back_from = routing(
        owner, accepted, continued, col_index, request_count, cap
    )
    own_live = own_cont > 0
    my_slice = lax.dynamic_slice_in_dim(hidden, row_index * slice_width, slice_width, 1)
    packed = rows_of(my_slice.reshape(request_count, LEN, slice_width), send_from)
    packed = packed.reshape(col_count, cap, LEN, slice_width)
    got = lax.all_to_all(packed, "col", split_axis=0, concat_axis=0, tiled=True)
    own_slice = rows_of(got.reshape(col_count * cap, LEN, slice_width), pick)
    own_slice = own_slice.reshape(token_count, slice_width)
    hidden = lax.all_gather(own_slice, "row", axis=1, tiled=True)

    rest = jnp.concatenate(
        [w_out, w_bc, w_dt, jnp.zeros((w_dt.shape[0], 128 - w_dt.shape[1]), w_dt.dtype)], axis=1
    )
    full_zx = lax.all_gather(w_zx, "col", axis=0, tiled=True)
    full_rest = lax.all_gather(rest, "col", axis=0, tiled=True)
    full_out = full_rest[:, :inner_here]
    full_bc = full_rest[:, inner_here : inner_here + 2 * STATE]
    full_dt = full_rest[:, inner_here + 2 * STATE : inner_here + 2 * STATE + heads_here]
    proj_zx = jnp.dot(hidden, full_zx, preferred_element_type=jnp.float32).astype(jnp.bfloat16)
    proj_zx = proj_zx.reshape(request_count, LEN, heads_here, 2 * HEAD_DIM)
    gate_in = proj_zx[..., :HEAD_DIM]
    x_in = proj_zx[..., HEAD_DIM:].reshape(request_count, LEN, inner_here)
    bc_flat = jnp.dot(hidden, full_bc, preferred_element_type=jnp.float32).astype(jnp.bfloat16)
    proj_bc = bc_flat.reshape(request_count, LEN, 2 * STATE)
    dt_raw = jnp.dot(hidden, full_dt, preferred_element_type=jnp.float32).reshape(
        request_count, LEN, heads_here
    )
    start_state = rows_of(prev_state, own_prev, own_live).astype(jnp.float32)
    edge_x = rows_of(prev_edge_x, own_prev, own_live)
    edge_bc = rows_of(prev_edge_bc, own_prev, own_live)
    number = x_in.shape[0]
    x_conv = (
        conv_silu(edge_x, x_in, conv_x_w, conv_x_b)
        .astype(jnp.float32)
        .reshape(number, LEN, heads_here, HEAD_DIM)
    )
    bc_conv = conv_silu(edge_bc, proj_bc, conv_bc_w, conv_bc_b).astype(jnp.float32)
    b_in = bc_conv[..., :STATE]
    c_in = bc_conv[..., STATE:]
    step_size = jax.nn.softplus(dt_raw + dt_bias)
    log_decay = jnp.stack(
        [jnp.sum((step_size * decay_rate)[:, : t + 1], axis=1) for t in range(LEN)], axis=1
    )
    positions = jnp.arange(LEN, dtype=jnp.int32)
    later = positions[:, None] >= positions[None, :]
    spread = log_decay[:, :, None, :] - log_decay[:, None, :, :]
    within = jnp.where(later[None, :, :, None], jnp.exp(jnp.minimum(spread, 0.0)), 0.0)
    scores = jnp.einsum("rtn,rsn->rts", c_in, b_in, precision=highest)
    mixing = within * scores[..., None] * step_size[:, None, :, :]
    scan_out = jnp.einsum("rtsh,rshp->rthp", mixing, x_conv, precision=highest)
    scan_out = scan_out + jnp.exp(log_decay)[..., None] * jnp.einsum(
        "rhpn,rtn->rthp", start_state, c_in, precision=highest
    )
    scan_out = scan_out + d_skip[None, None, :, None] * x_conv
    padded_decay = jnp.concatenate(
        [jnp.zeros((number, 1, heads_here), jnp.float32), log_decay], axis=1
    )
    pick_mask = (jnp.arange(LEN + 1, dtype=jnp.int32)[None, :] == my_accepted[:, None]).astype(
        jnp.float32
    )
    reach = jnp.sum(pick_mask[:, :, None] * padded_decay, axis=1)
    before = positions[None, :] < my_accepted[:, None]
    weight_s = (
        jnp.where(before[:, :, None], jnp.exp(jnp.minimum(reach[:, None, :] - log_decay, 0.0)), 0.0)
        * step_size
    )
    chosen = jnp.exp(reach)[:, :, None, None] * start_state + jnp.einsum(
        "rsh,rshp,rsn->rhpn", weight_s, x_conv, b_in, precision=highest
    )
    new_state, new_edge_x, new_edge_bc = (
        chosen.astype(jnp.bfloat16),
        last_rows(edge_x, x_in, my_accepted),
        last_rows(edge_bc, proj_bc, my_accepted),
    )
    gated = (scan_out * jax.nn.silu(gate_in.astype(jnp.float32))).reshape(token_count, inner_here)
    totals = lax.psum(jnp.sum(gated * gated, axis=1), "row")
    normed = (gated * lax.rsqrt(totals / INNER + 1e-05)[:, None] * norm_gain).astype(jnp.bfloat16)
    partial_out = lax.dot_general(
        normed, full_out, (((1,), (1,)), ((), ())), preferred_element_type=jnp.float32
    )
    own_mixed = lax.psum_scatter(partial_out, "row", scatter_dimension=1, tiled=True).astype(
        jnp.bfloat16
    )
    back = rows_of(own_mixed.reshape(request_count, LEN, slice_width), back_from)
    back = back.reshape(col_count, cap, LEN, slice_width)
    came = lax.all_to_all(back, "col", split_axis=0, concat_axis=0, tiled=True)
    mixed = rows_of(came.reshape(col_count * cap, LEN, slice_width), home_key)
    return (mixed.reshape(token_count, slice_width), new_state, new_edge_x, new_edge_bc)


def solution(mesh):
    return jax.shard_map(
        per_device,
        mesh=mesh,
        in_specs=(
            P("col", None),
            P("col", "row"),
            P("col", None),
            P("col", "row"),
            P("col", "row"),
            P("row"),
            P("row"),
            P("row"),
            P(None, "row"),
            P("row"),
            P(),
            P(),
            P("row"),
            P("col", "row", None, None),
            P("col", None, "row"),
            P("col", None, None),
            P(),
            P(),
            P(),
            P(),
        ),
        out_specs=(
            P("col", "row"),
            P("col", "row", None, None),
            P("col", None, "row"),
            P("col", None, None),
        ),
        check_vma=False,
    )
```

time: 588 us -> 313 us (0.53); the launches traced: 581 us -> 312 us
  blocking collectives: 144 us -> 8.43 us
  local copies, waits for them, and re-layouts: 72.5 us -> 32.3 us
  waiting for transfers between devices: 213 us -> 175 us
  other arithmetic: 47.9 us -> 16 us
  starting transfers between devices: 44.1 us -> 17.5 us
    all_gather x2 -> x0, blocking collectives: 135 us -> none  [the longest x1 110 us: per_device(): lax.all_gather(w_bc, 'col', axis=0, tiled=True)]
    all_gather x2 -> x3, waiting for transfers between devices: 160 us -> 101 us  [the longest x1 48.1 us: per_device(): full_rest = lax.all_gather(rest, 'col', axis=0, tiled=True)]
    gather x18 -> x0, local copies, waits for them, and re-layouts: 48 us -> none  [the longest x11 32.2 us: pack_rows(): picked = jnp.take(source, index, axis=0)]
    select_n x14 -> x0, other arithmetic: 34.7 us -> none  [the longest x8 28.1 us: pack_rows(): return jnp.where(valid.reshape(shape), picked, jnp.zeros((), source.dtype))]
    all_to_all x6 -> x2, starting transfers between devices: 43.8 us -> 17.4 us  [the longest x1 9.57 us: per_device(): got = lax.all_to_all(packed, 'col', split_axis=0, concat_axis=0, tiled=True)]
    all_to_all x6 -> x2, waiting for transfers between devices: 0.02 us -> 23.5 us  [the longest x1 18.2 us: per_device(): got = lax.all_to_all(packed, 'col', split_axis=0, concat_axis=0, tiled=True)]
    unnamed x55 -> x111, local copies, waits for them, and re-layouts: 3.47 us -> 12.9 us
    reduce_sum x5 -> x25, other arithmetic: 0.83 us -> 9.45 us  [the longest x2 5.18 us: last_rows(): picks.append(jnp.sum(jnp.where(hot, series, 0).astype(jnp.float32), axis=1))]
  transfers between devices with their start and end apart: 9 -> 6, of which waited for: 2 -> 6; matrix products, arithmetic and copies ran while one was open for 25% -> 14% of each run, Pallas kernels for 0% -> 0%
where the time goes in v1:
time: 313 us; the launch traced here: 312 us
  waiting for transfers between devices  175 us (56%)
  matrix products  48.1 us (15%)
  local copies, waits for them, and re-layouts  32.3 us (10%)
  starting transfers between devices  17.5 us (6%)
  other arithmetic  16 us (5%)
  between operations  14.7 us (5%)
  blocking collectives  8.43 us (3%)
    reduce_scatter x1, waiting for transfers between devices, per_device(): lax.psum_scatter(partial_out, 'row', scatter_dimension=1, tiled=True)  49.4 us
    all_gather x1, waiting for transfers between devices, per_device(): full_rest = lax.all_gather(rest, 'col', axis=0, tiled=True)  48.1 us
    all_gather x1, waiting for transfers between devices, per_device(): full_zx = lax.all_gather(w_zx, 'col', axis=0, tiled=True)  34.7 us
    all_gather x1, waiting for transfers between devices, per_device(): hidden = lax.all_gather(own_slice, 'row', axis=1, tiled=True)  18.2 us
    all_to_all x1, waiting for transfers between devices, per_device(): got = lax.all_to_all(packed, 'col', split_axis=0, concat_axis=0, tiled=True)  18.2 us
    dot_general x1, matrix products, per_device(): jnp.einsum('rsh,rshp,rsn->rhpn', weight_s, x_conv, b_in, precision=highest)  15.3 us
    unnamed x111, local copies, waits for them, and re-layouts  12.9 us
    all_to_all x1, starting transfers between devices, per_device(): got = lax.all_to_all(packed, 'col', split_axis=0, concat_axis=0, tiled=True)  9.57 us
  transfers between devices with their start and end apart: 6, of which 6 were waited for; matrix products, arithmetic and copies ran while one was open for 14% of the time, Pallas kernels for 0%

profile of v1, /device:TPU:1, one launch (start us, length us, event | category | flops | bytes accessed | tf_op | source)
XLA Modules:
  0.0 311.7 jit_solution(2899129266878916183)
XLA Ops:
  7.2 1.6 copy-done
  8.9 0.3 reshape_reshape.24
  9.3 0.2 convert_reduce_fusion
  9.6 0.6 convolution_convert_fusion.2
  10.3 1.5 copy.142
  11.7 9.6 %all-to-all-start = ((bf16[32,4,16,384]{3,2,1,0:T(8,128)(2,1)}), bf16[32,4,16,384]{3,2,1,0:T(8,128)(2,1)S(1)}, u32[]{:S(2)}, u32[]{:S(2)}) async-start(bf16[32,4,16,384]{3,2,1,0:T(8,128)(2,1)} %bitcast.128), calls=%async_computation | async-start | bytes 3145728 | tf_op jit(solution)/shard_map/all_to_all | solution.py:114
  21.9 0.6 select_reduce_fusion.6
  22.6 2.7 select_reduce_fusion.3
  25.3 18.2 %all-to-all-done = bf16[32,4,16,384]{3,2,1,0:T(8,128)(2,1)S(1)} async-done(((bf16[32,4,16,384]{3,2,1,0:T(8,128)(2,1)}), bf16[32,4,16,384]{3,2,1,0:T(8,128)(2,1)S(1)}, u32[]{:S(2)}, u32[]{:S(2)}) %all-to-all-start) | async-done | bytes 1572896 | tf_op jit(solution)/shard_map/all_to_all | solution.py:114
  43.5 0.4 copy.143
  43.9 0.4 convolution_convert_fusion.4
  44.4 1.1 reshape_reshape.27
  45.7 0.7 maximum_maximum_fusion
  46.4 0.7 all-gather.6.cloned.1.call-update
  47.4 0.6 iota_compare_fusion.19
  48.0 0.2 convolution_convert_fusion.5
  48.3 0.8 reshape.411
  49.0 0.6 fusion.69
  49.6 4.4 %fusion.14 = bf16[6,8,512,128]{3,1,2,0:T(8,128)(2,1)S(1)} fusion(bf16[3,8,512,128]{3,2,1,0:T(8,128)(2,1)} %bitcast.133, s32[48]{0:T(128)S(1)} %select_reduce_fusion.11, pred[48]{0:T(512)(128)(4,1)S(1)} %broadcast_compare_fusion.1), kind=kOutput, calls=%fused_computation.26 | convolution fusion | flops 154142976 | bytes 9437424 | tf_op jit(solution)/shard_map/dot_general | solution.py:49
  54.1 4.3 %copy.146 = bf16[6,8,512,128]{3,2,1,0:T(8,128)(2,1)} copy(bf16[6,8,512,128]{3,1,2,0:T(8,128)(2,1)S(1)} %fusion.14) | data formatting | bytes 12582912
  58.4 0.2 convolution_convert_fusion.8
  58.8 18.2 %all-gather.4.cloned.1.call-done = bf16[768,1536]{1,0:T(8,128)(2,1)} async-done(((bf16[768,384]{1,0:T(8,128)(2,1)}), bf16[768,1536]{1,0:T(8,128)(2,1)}) %all-gather.4.cloned.1.call-update) | async-done | bytes 2359312 | tf_op jit(solution)/shard_map/all_gather | solution.py:117
  77.1 48.1 %all-gather.8.cloned.1.call-done = bf16[1536,896]{1,0:T(8,128)(2,1)} async-done(((bf16[48,896]{1,0:T(8,128)(2,1)}), bf16[1536,896]{1,0:T(8,128)(2,1)}) %all-gather.8.cloned.1.call-update) | async-done | bytes 2752528 | tf_op jit(solution)/shard_map/all_gather | solution.py:123
  125.2 2.4 fusion.40
  127.6 0.1 reshape.415
  127.9 0.1 fusion.67
  128.1 0.8 copy.127
  129.2 0.8 copy.124
  130.0 0.7 select_multiply_fusion
  130.7 0.8 copy.129
  131.5 2.6 convolution_convert_fusion.7
  134.2 1.8 select_reduce_fusion.9
  135.9 0.5 multiply_convert_fusion.3
  136.5 1.0 fusion.46
  137.4 34.7 %all-gather.6.cloned.1.call-done = bf16[1536,1024]{1,0:T(8,128)(2,1)} async-done(((bf16[48,1024]{1,0:T(8,128)(2,1)}), bf16[1536,1024]{1,0:T(8,128)(2,1)}) %all-gather.6.cloned.1.call-update) | async-done | bytes 3145744 | tf_op jit(solution)/shard_map/all_gather | solution.py:122
  172.1 5.2 %fusion.30 = bf16[96,8,8,128]{3,1,2,0:T(8,128)(2,1)S(1)} fusion(bf16[768,1536]{1,0:T(8,128)(2,1)} %all-gather.4.cloned.1.call-done, bf16[1536,1024]{1,0:T(8,128)(2,1)} %all-gather.6.cloned.1.call-done), kind=kOutput, calls=%fused_computation.48 | convolution fusion | flops 2416705536 | bytes 7077888 | tf_op jit(solution)/shard_map/dot_general | solution.py:127
  177.3 0.4 copy.144
  177.8 2.4 fusion.68
  180.2 2.7 reshape.413
  182.9 3.4 %select_reduce_fusion.2 = (bf16[48,512]{1,0:T(8,128)(2,1)}, bf16[48,512]{1,0:T(8,128)(2,1)}, bf16[48,512]{1,0:T(8,128)(2,1)}, f32[48,19,512]{2,1,0:T(8,128)S(1)}) fusion(pred[48,19]{1,0:T(8,128)(4,1)S(1)} %iota_compare_fusion.7, bf16[48,16,512]{2,1,0:T(8,128)(2,1)S(1)} %reshape.413, bf16[48,3,512]{2,1,0:T(4,128)(2,1)} %reshape.411, ...), kind=kLoop, calls=%fused_computation.55 | loop fusion | flops 5062656 | bytes 2951856 | tf_op jit(solution)/shard_map/reduce_sum | solution.py:69
  186.4 1.0 multiply_convert_fusion.1
  187.4 0.8 reshape.414
  188.2 0.1 copy-done.5
  188.5 2.5 fusion.7
  191.1 7.1 %multiply_reduce_fusion = (f32[48,16]{1,0:T(8,128)S(1)}, f32[48,16,8,64]{3,1,2,0:T(8,128)S(1)}) fusion(bf16[48,16,8,64]{3,2,1,0:T(8,128)(2,1)S(1)} %copy-done.4, bf16[48,16,8,64]{3,2,1,0:T(8,128)(2,1)S(1)} %reshape.414, f32[8]{0:T(128)S(1)} %copy-done.43, bf16[48,8,64,128]{3,2,1,0:T(8,128)(2,1)} %bitcast.124, ...), kind=kOutput, calls=%fused_computation.18 | convolution fusion | flops 105774336 | bytes 14552576 | tf_op jit(solution)/shard_map/rhpn,rtn->rthp/dot_general | solution.py:159
  198.3 3.1 copy.132
  201.4 2.9 reshape.422
  204.3 8.4 %psum.7 = f32[768]{0:T(1024)S(1)} all-reduce(f32[768]{0:T(1024)S(1)} %reduce_sum.328), channel_id=1, replica_groups=mesh['row'=4,'col'=32] {'row'}, use_global_device_ids=true, to_apply=%region_25.26 | all-reduce | flops 768 | bytes 6144 | tf_op jit(solution)/shard_map/psum | solution.py:184
  212.7 5.0 %fusion.17 = f32[768,1536]{1,0:T(8,128)} fusion(bf16[1536,896]{1,0:T(8,128)(2,1)} %all-gather.8.cloned.1.call-done, f32[768,512]{1,0:T(8,128)S(1)} %reshape.422, f32[512]{0:T(512)S(1)} %copy-done.24, f32[768]{0:T(1024)S(1)} %add_rsqrt_fusion), kind=kOutput, calls=%fused_computation.29 | convolution fusion | flops 1209139200 | bytes 7869440 | tf_op jit(solution)/shard_map/dot_general | solution.py:186
  217.8 0.6 copy-done.35
  218.5 49.4 %reduce-scatter.2.cloned.1.call-done = f32[768,384]{1,0:T(8,128)} async-done(((f32[768,1536]{1,0:T(8,128)}), f32[768,384]{1,0:T(8,128)}) %reduce-scatter.2.cloned.1.call-update) | async-done | bytes 1179664 | tf_op jit(solution)/shard_map/reduce_scatter | solution.py:189
  267.8 1.3 convert_element_type.124
  269.2 0.3 reshape_reshape.28
  269.4 0.6 convolution_convert_fusion.1
  270.1 1.5 copy.147
  271.6 7.8 %all-to-all-start.1 = ((bf16[32,4,16,384]{3,2,1,0:T(8,128)(2,1)}), bf16[32,4,16,384]{3,2,1,0:T(8,128)(2,1)}, u32[]{:S(2)}, u32[]{:S(2)}) async-start(bf16[32,4,16,384]{3,2,1,0:T(8,128)(2,1)} %bitcast.61), calls=%async_computation.2 | async-start | bytes 3145728 | tf_op jit(solution)/shard_map/all_to_all | solution.py:194
  279.5 0.1 copy.135
  279.7 0.6 pad_maximum_fusion.3
  280.4 0.7 pad_maximum_fusion.2
  281.0 15.3 %add_convert_fusion = bf16[48,8,64,128]{3,2,1,0:T(8,128)(2,1)} fusion(bf16[48,8,64,128]{3,2,1,0:T(8,128)(2,1)} %bitcast.125, f32[48,8]{1,0:T(8,128)S(1)} %copy.134, f32[48,16,8]{1,2,0:T(8,128)S(1)} %copy.135, bf16[48,16,8,64]{3,2,1,0:T(8,128)(2,1)S(1)} %copy-done.3, bf16[48,16,256]{2,1,0:T(8,128)(2,1)S(1)} %multiply_convert_fusion.3), kind=kOutput, calls=%fused_computation.1 | convolution fusion | flops 617349120 | bytes 14573568 | tf_op jit(solution)/shard_map/rsh,rshp,rsn->rhpn/dot_general | solution.py:175
  296.4 5.3 %all-to-all-done.1 = bf16[32,4,16,384]{3,2,1,0:T(8,128)(2,1)} async-done(((bf16[32,4,16,384]{3,2,1,0:T(8,128)(2,1)}), bf16[32,4,16,384]{3,2,1,0:T(8,128)(2,1)}, u32[]{:S(2)}, u32[]{:S(2)}) %all-to-all-start.1) | async-done | bytes 1572896 | tf_op jit(solution)/shard_map/all_to_all | solution.py:194
  301.7 1.9 copy.148
  303.6 0.4 convolution_convert_fusion.3
  304.0 1.1 reshape_reshape.31
  (160 shorter events, 2.6 us)
Async XLA Ops:
  7.2 1.7 copy-start
  7.2 2.0 copy-start.23
  9.5 2.2 copy-start.36
  11.7 9.6 %copy-start.29 = (s32[1536]{0:T(1024)S(1)}, s32[1536]{0:T(1024)}, u32[]{:S(2)}) copy-start(s32[1536]{0:T(1024)} %param.38) | copy-start | bytes 18436
  11.7 9.8 %copy-start.30 = (s32[1536]{0:T(1024)S(1)}, s32[1536]{0:T(1024)}, u32[]{:S(2)}) copy-start(s32[1536]{0:T(1024)} %param.36) | copy-start | bytes 18436
  11.7 31.8 %all-to-all-start = ((bf16[32,4,16,384]{3,2,1,0:T(8,128)(2,1)}), bf16[32,4,16,384]{3,2,1,0:T(8,128)(2,1)S(1)}, u32[]{:S(2)}, u32[]{:S(2)}) async-start(bf16[32,4,16,384]{3,2,1,0:T(8,128)(2,1)} %bitcast.128), calls=%async_computation | async-start | bytes 3145728 | tf_op jit(solution)/shard_map/all_to_all | solution.py:114
  21.3 55.8 %all-gather.4.cloned.1.call-start = ((), (), s32[]{:S(2)}) async-start(), calls=%async_computation.3 | async-start | bytes 2949120 | tf_op jit(solution)/shard_map/all_gather | solution.py:117
  25.2 19.1 %copy-start.34 = (s32[48]{0:T(128)}, s32[48]{0:T(128)S(1)}, u32[]{:S(2)}) copy-start(s32[48]{0:T(128)S(1)} %get-tuple-element.12) | copy-start | bytes 580
  43.9 1.6 copy-start.38
  43.9 1.8 copy-start.18
  43.9 1.8 copy-start.22
  43.9 4.1 %copy-start.16 = (bf16[24,3,512]{2,0,1:T(8,128)(2,1)S(1)}, bf16[24,3,512]{2,0,1:T(8,128)(2,1)}, u32[]{:S(2)}) copy-start(bf16[24,3,512]{2,0,1:T(8,128)(2,1)} %param.34) | copy-start | bytes 221188
  43.9 5.1 %copy-start.31 = (f32[4,512]{1,0:T(4,128)S(1)}, f32[4,512]{1,0:T(4,128)}, u32[]{:S(2)}) copy-start(f32[4,512]{1,0:T(4,128)} %param.28) | copy-start | bytes 24580
  45.5 79.7 %all-gather.8.cloned.1.call-start = ((), (), s32[]{:S(2)}) async-start(), calls=%async_computation.5 | async-start | bytes 2838528 | tf_op jit(solution)/shard_map/all_gather | solution.py:123
  46.4 125.7 %all-gather.6.cloned.1.call-start = ((), (), s32[]{:S(2)}) async-start(), calls=%async_computation.4 | async-start | bytes 3244032 | tf_op jit(solution)/shard_map/all_gather | solution.py:122
  47.1 220.7 %reduce-scatter.2.cloned.1.call-start = ((), (), s32[]{:S(2)}) async-start(), calls=%async_computation.6 | async-start | bytes 5898240 | tf_op jit(solution)/shard_map/reduce_scatter | solution.py:189
  54.0 4.4 %copy-start.21 = (bf16[24,3,256]{2,0,1:T(8,128)(2,1)S(1)}, bf16[24,3,256]{2,0,1:T(8,128)(2,1)}, u32[]{:S(2)}) copy-start(bf16[24,3,256]{2,0,1:T(8,128)(2,1)} %param.35) | copy-start | bytes 110596
  54.1 4.6 %copy-start.32 = (f32[4,256]{1,0:T(4,128)S(1)}, f32[4,256]{1,0:T(4,128)}, u32[]{:S(2)}) copy-start(f32[4,256]{1,0:T(4,128)} %param.30) | copy-start | bytes 12292
  54.1 4.7 %copy-start.42 = (f32[8]{0:T(128)S(1)}, f32[8]{0:T(128)}, u32[]{:S(2)}) copy-start(f32[8]{0:T(128)} %param.26) | copy-start | bytes 100
  58.4 69.5 %copy-start.41 = (f32[8]{0:T(128)S(1)}, f32[8]{0:T(128)}, u32[]{:S(2)}) copy-start(f32[8]{0:T(128)} %param.25) | copy-start | bytes 100
  58.8 75.3 %copy-start.17 = (pred[48,19]{1,0:T(8,128)(4,1)}, pred[48,19]{1,0:T(8,128)(4,1)S(1)}, u32[]{:S(2)}) copy-start(pred[48,19]{1,0:T(8,128)(4,1)S(1)} %get-tuple-element.69) | copy-start | bytes 2740
  130.0 4.1 %copy-start.19 = (f32[48,8]{0,1:T(8,128)}, f32[48,8]{0,1:T(8,128)S(1)}, u32[]{:S(2)}) copy-start(f32[48,8]{0,1:T(8,128)S(1)} %multiply_reduce_fusion.1) | copy-start | bytes 4612
  131.5 4.4 %copy-start.40 = (f32[256]{0:T(256)S(1)}, f32[256]{0:T(256)}, u32[]{:S(2)}) copy-start(f32[256]{0:T(256)} %param.31) | copy-start | bytes 3076
  182.9 3.5 %copy-start.25 = (f32[1,512]{1,0:T(1,128)S(1)}, f32[1,512]{1,0:T(1,128)}, u32[]{:S(2)}) copy-start(f32[1,512]{1,0:T(1,128)} %get-tuple-element.26) | copy-start | bytes 6148
  182.9 3.5 %copy-start.26 = (f32[1,512]{1,0:T(1,128)S(1)}, f32[1,512]{1,0:T(1,128)}, u32[]{:S(2)}) copy-start(f32[1,512]{1,0:T(1,128)} %get-tuple-element.27) | copy-start | bytes 6148
  182.9 3.5 %copy-start.27 = (f32[1,512]{1,0:T(1,128)S(1)}, f32[1,512]{1,0:T(1,128)}, u32[]{:S(2)}) copy-start(f32[1,512]{1,0:T(1,128)} %get-tuple-element.28) | copy-start | bytes 6148
  182.9 3.4 %copy-start.28 = (f32[1,512]{1,0:T(1,128)S(1)}, f32[1,512]{1,0:T(1,128)}, u32[]{:S(2)}) copy-start(f32[1,512]{1,0:T(1,128)} %get-tuple-element.29) | copy-start | bytes 6148
  182.9 3.4 %copy-start.33 = (f32[512]{0:T(512)S(1)}, f32[512]{0:T(512)}, u32[]{:S(2)}) copy-start(f32[512]{0:T(512)} %param.29) | copy-start | bytes 6148
  187.4 1.0 copy-start.5
  187.4 1.0 copy-start.7
  187.4 1.1 copy-start.8
  187.4 1.1 copy-start.39
  188.5 2.6 copy-start.2
  188.5 2.6 copy-start.4
  188.5 2.6 copy-start.9
  188.5 2.6 copy-start.43
  201.4 11.4 %copy-start.24 = (f32[512]{0:T(512)S(1)}, f32[512]{0:T(512)}, u32[]{:S(2)}) copy-start(f32[512]{0:T(512)} %param.32) | copy-start | bytes 6148
  217.8 0.6 copy-start.35
  271.5 7.9 %copy-start.20 = (f32[48,8]{0,1:T(8,128)S(1)}, f32[48,8]{0,1:T(8,128)}, u32[]{:S(2)}) copy-start(f32[48,8]{0,1:T(8,128)} %copy-done.19) | copy-start | bytes 4612
  271.5 8.0 %copy-start.6 = (f32[48,16,8]{0,2,1:T(8,128)S(1)}, f32[48,16,8]{0,2,1:T(8,128)}, u32[]{:S(2)}) copy-start(f32[48,16,8]{0,2,1:T(8,128)} %get-tuple-element.20) | copy-start | bytes 73732
  271.5 8.1 %copy-start.13 = (bf16[48,256]{1,0:T(8,128)(2,1)S(1)}, bf16[48,256]{1,0:T(8,128)(2,1)}, u32[]{:S(2)}) copy-start(bf16[48,256]{1,0:T(8,128)(2,1)} %get-tuple-element.7) | copy-start | bytes 73732
  271.5 8.1 %copy-start.14 = (bf16[48,256]{1,0:T(8,128)(2,1)S(1)}, bf16[48,256]{1,0:T(8,128)(2,1)}, u32[]{:S(2)}) copy-start(bf16[48,256]{1,0:T(8,128)(2,1)} %get-tuple-element.8) | copy-start | bytes 73732
  271.5 8.1 %copy-start.15 = (bf16[48,256]{1,0:T(8,128)(2,1)S(1)}, bf16[48,256]{1,0:T(8,128)(2,1)}, u32[]{:S(2)}) copy-start(bf16[48,256]{1,0:T(8,128)(2,1)} %get-tuple-element.9) | copy-start | bytes 73732
  271.6 8.8 %copy-start.10 = (bf16[48,512]{1,0:T(8,128)(2,1)S(1)}, bf16[48,512]{1,0:T(8,128)(2,1)}, u32[]{:S(2)}) copy-start(bf16[48,512]{1,0:T(8,128)(2,1)} %get-tuple-element.4) | copy-start | bytes 147460
  271.6 8.8 %copy-start.11 = (bf16[48,512]{1,0:T(8,128)(2,1)S(1)}, bf16[48,512]{1,0:T(8,128)(2,1)}, u32[]{:S(2)}) copy-start(bf16[48,512]{1,0:T(8,128)(2,1)} %get-tuple-element.5) | copy-start | bytes 147460
  271.6 8.8 %copy-start.12 = (bf16[48,512]{1,0:T(8,128)(2,1)S(1)}, bf16[48,512]{1,0:T(8,128)(2,1)}, u32[]{:S(2)}) copy-start(bf16[48,512]{1,0:T(8,128)(2,1)} %get-tuple-element.6) | copy-start | bytes 147460
  271.6 9.4 %copy-start.3 = (bf16[48,16,8,64]{3,2,1,0:T(8,128)(2,1)S(1)}, bf16[48,16,8,64]{3,2,1,0:T(8,128)(2,1)}, u32[]{:S(2)}) copy-start(bf16[48,16,8,64]{3,2,1,0:T(8,128)(2,1)} %copy-done.2) | copy-start | bytes 2359300
  271.6 30.1 %all-to-all-start.1 = ((bf16[32,4,16,384]{3,2,1,0:T(8,128)(2,1)}), bf16[32,4,16,384]{3,2,1,0:T(8,128)(2,1)}, u32[]{:S(2)}, u32[]{:S(2)}) async-start(bf16[32,4,16,384]{3,2,1,0:T(8,128)(2,1)} %bitcast.61), calls=%async_computation.2 | async-start | bytes 3145728 | tf_op jit(solution)/shard_map/all_to_all | solution.py:194
  296.3 7.3 %copy-start.37 = (s32[48]{0:T(128)S(1)}, s32[48]{0:T(128)}, u32[]{:S(2)}) copy-start(s32[48]{0:T(128)} %copy-done.36) | copy-start | bytes 580
  301.7 3.5 %copy-start.1 = (bf16[768,1536]{1,0:T(8,128)(2,1)S(1)}, bf16[768,1536]{1,0:T(8,128)(2,1)}, u32[]{:S(2)}) copy-start(bf16[768,1536]{1,0:T(8,128)(2,1)} %param.20) | copy-start | bytes 7077892
Sparse Core Ops, SparseCore 0:
  45.6 31.4 all-gather.3
  80.0 45.1 all-gather.7
  127.5 44.6 all-gather.5
  217.9 49.8 reduce-scatter.1

commit v2 on v1

v2 whole, which is shorter than its diff:
```python
import jax
import jax.numpy as jnp
from jax import lax
from jax.experimental import pallas as pl
from jax.experimental.pallas import tpu as pltpu
from jax.sharding import PartitionSpec as P

HEAD_DIM = 64
STATE = 128
KCONV = 4
LEN = 16
INNER = 2048
SIDE = 4
GROUP = 8
TOK = GROUP * LEN
MESH = pl.DeviceIdType.MESH
HIGHEST = lax.Precision.HIGHEST


def routing(owner, accepted, continued, col_index, request_count, cap):
    total = owner.shape[0]
    groups = total // request_count
    local = jnp.arange(request_count, dtype=jnp.int32)
    slots = jnp.arange(groups * cap, dtype=jnp.int32)
    mine = lax.dynamic_slice_in_dim(owner, col_index * request_count, request_count)
    earlier = local[None, :] < local[:, None]
    rank = jnp.sum(((mine[None, :] == mine[:, None]) & earlier).astype(jnp.int32), axis=1)
    home_key = mine * cap + rank
    send_from = jnp.sum(jnp.where(home_key[None, :] == slots[:, None], local[None, :], 0), axis=1)
    owned = (owner == col_index).reshape(groups, request_count)
    owned_int = owned.astype(jnp.int32)
    in_group = jnp.sum(jnp.where(earlier[None], owned_int[:, None, :], 0), axis=2)
    counts = jnp.sum(owned_int, axis=1)
    group = jnp.arange(groups, dtype=jnp.int32)
    before = jnp.sum(jnp.where(group[None, :] < group[:, None], counts[None, :], 0), axis=1)
    slot = jnp.where(owned, in_group + before[:, None], -1)
    match = slot[None] == local[:, None, None]

    def picked(values):
        return jnp.sum(jnp.where(match, values[None], 0), axis=(1, 2))

    pick = picked(group[:, None] * cap + in_group)
    own_accepted = picked(accepted.reshape(groups, request_count))
    own_cont = picked((continued == 1).astype(jnp.int32).reshape(groups, request_count))
    own_prev = jnp.sum(jnp.where(earlier, own_cont[None, :], 0), axis=1)
    back_from = jnp.sum(jnp.where(pick[None, :] == slots[:, None], local[None, :], 0), axis=1)
    return home_key, send_from, pick, own_accepted, own_cont, own_prev, back_from


def greet(row, me, rows, cols):
    barrier = pltpu.get_barrier_semaphore()

    def along_col(d, carry):
        pl.semaphore_signal(
            barrier, inc=1, device_id=(row, (me + d) % cols), device_id_type=MESH
        )
        return carry

    lax.fori_loop(1, cols, along_col, 0)

    def along_row(d, carry):
        pl.semaphore_signal(
            barrier, inc=1, device_id=((row + d) % rows, me), device_id_type=MESH
        )
        return carry

    lax.fori_loop(1, rows, along_row, 0)
    return barrier


def gather_kernel(
    rows, cols, cap, send_from, pick, hidden, wa, wb, hid_full, fa, fb,
    sl, packed, got, own, loc, a2a_s, a2a_r, was, wbs, war, wbr, y_s, y_r,
):
    row, me = lax.axis_index("row"), lax.axis_index("col")
    barrier = greet(row, me, rows, cols)
    width = sl.shape[2]
    half = sl.shape[0] // 2
    depth = wa.shape[0]

    def cols_of(r):
        return pl.ds(pl.multiple_of(r * width, 128), width)

    def block(ref, c):
        return ref.at[pl.ds(pl.multiple_of(c * depth, 16), depth), :]

    load = pltpu.make_async_copy(hidden.at[:, :, cols_of(row)], sl, loc.at[0])
    load.start()
    keep_a = pltpu.make_async_copy(wa, block(fa, me), loc.at[1])
    keep_b = pltpu.make_async_copy(wb, block(fb, me), loc.at[2])
    keep_a.start()
    keep_b.start()
    load.wait()

    def pack(s, carry):
        packed[s] = sl[send_from[s]]
        return carry

    lax.fori_loop(0, cols * cap, pack, 0)
    pl.semaphore_wait(barrier, cols - 1 + rows - 1)

    def piece(ref, c):
        return ref.at[pl.ds(c * cap, cap)]

    def push(d, carry):
        peer = (me + d) % cols
        pltpu.make_async_remote_copy(
            piece(packed, peer), piece(got, me), a2a_s.at[peer], a2a_r.at[me],
            device_id=(row, peer), device_id_type=MESH,
        ).start()
        return carry

    lax.fori_loop(1, cols, push, 0)
    keep_m = pltpu.make_async_copy(piece(packed, me), piece(got, me), loc.at[3])
    keep_m.start()

    core = me % 2
    x = (me // 2) % SIDE
    z = me // (2 * SIDE)
    a = x + core * (z - x)
    b = z + core * (x - z)

    def at(pa, pb):
        pa, pb = (pa + SIDE) % SIDE, (pb + SIDE) % SIDE
        px = pa + core * (pb - pa)
        pz = pb + core * (pa - pb)
        return (pz * SIDE + px) * 2 + core

    sibling = me + 1 - 2 * core
    sent = [0, 0]

    def send(which, src, c, dest):
        full, ss, rs = ((fa, was, war), (fb, wbs, wbr))[which]
        k = sent[which]
        sent[which] += 1
        pltpu.make_async_remote_copy(
            src, block(full, c), ss.at[k], rs.at[c],
            device_id=(row, dest), device_id_type=MESH,
        ).start()

    def forward(which, c, dest):
        send(which, block((fa, fb)[which], c), c, dest)

    def arrived(which, c):
        full, rs = ((fa, war), (fb, wbr))[which]
        pltpu.make_async_copy(block(full, c), block(full, c), rs.at[c]).wait()

    up, down = at(a + 1, b), at(a - 1, b)
    far = at(a + 2, b)
    over, under = at(a, b + 1), at(a, b - 1)
    for dest in (up, down, over, under, sibling):
        for which, src in ((0, wa), (1, wb)):
            send(which, src, me, dest)
    arrived(0, down)
    forward(0, down, up)
    arrived(1, up)
    forward(1, up, down)
    arrived(1, down)
    arrived(0, up)
    for c in (down, up):
        for which in (0, 1):
            for dest in (over, under, sibling):
                forward(which, c, dest)
    keep_m.wait()

    def took(d, carry):
        peer = (me + d) % cols
        pltpu.make_async_copy(piece(got, peer), piece(got, peer), a2a_r.at[peer]).wait()
        return carry

    lax.fori_loop(1, cols, took, 0)

    def unpack(s, carry):
        own[s] = got[pick[s]]
        return carry

    lax.fori_loop(0, own.shape[0], unpack, 0)

    def part(ref, h, r):
        return ref.at[pl.ds(h * half, half), :, cols_of(r)]

    right, left = (row + 1) % rows, (row + rows - 1) % rows
    far_row = (row + 2) % rows
    for k, dest in ((0, right), (1, left)):
        for h in (0, 1):
            pltpu.make_async_remote_copy(
                own.at[pl.ds(h * half, half)], part(hid_full, h, row),
                y_s.at[2 * k + h], y_r.at[row, h],
                device_id=(dest, me), device_id_type=MESH,
            ).start()
    keep_y = pltpu.make_async_copy(own, hid_full.at[:, :, cols_of(row)], loc.at[4])
    keep_y.start()

    for which in (0, 1):
        arrived(which, far)
        for dest in (over, under, sibling):
            forward(which, far, dest)
    for k in (0, 1, -1, 2):
        low, high = at(a + k, b - 1), at(a + k, b + 1)
        arrived(0, low)
        forward(0, low, over)
        arrived(1, high)
        forward(1, high, under)
        arrived(1, low)
        arrived(0, high)
        for which in (0, 1):
            forward(which, low, sibling)
            forward(which, high, sibling)

    def y_here(h, r):
        pltpu.make_async_copy(part(hid_full, h, r), part(hid_full, h, r), y_r.at[r, h]).wait()

    y_here(0, left)
    pltpu.make_async_remote_copy(
        part(hid_full, 0, left), part(hid_full, 0, left), y_s.at[4], y_r.at[left, 0],
        device_id=(right, me), device_id_type=MESH,
    ).start()
    y_here(1, right)
    pltpu.make_async_remote_copy(
        part(hid_full, 1, right), part(hid_full, 1, right), y_s.at[5], y_r.at[right, 1],
        device_id=(left, me), device_id_type=MESH,
    ).start()
    y_here(1, left)
    y_here(0, right)
    for k in (0, 1, -1, 2):
        opposite = at(a + k, b + 2)
        for which in (0, 1):
            arrived(which, opposite)
            forward(which, opposite, sibling)
    y_here(0, far_row)
    y_here(1, far_row)

    def from_sibling(k, carry):
        c = 2 * k + 1 - core
        pltpu.make_async_copy(block(fa, c), block(fa, c), war.at[c]).wait()
        pltpu.make_async_copy(block(fb, c), block(fb, c), wbr.at[c]).wait()
        return carry

    lax.fori_loop(0, cols // 2, from_sibling, 0)
    keep_a.wait()
    keep_b.wait()
    keep_y.wait()

    def a2a_done(d, carry):
        peer = (me + d) % cols
        pltpu.make_async_copy(piece(packed, peer), piece(packed, peer), a2a_s.at[peer]).wait()
        return carry

    lax.fori_loop(1, cols, a2a_done, 0)

    def a_done(k, carry):
        pltpu.make_async_copy(block(fa, me), block(fa, me), was.at[k]).wait()
        return carry

    lax.fori_loop(0, sent[0], a_done, 0)

    def b_done(k, carry):
        pltpu.make_async_copy(block(fb, me), block(fb, me), wbs.at[k]).wait()
        return carry

    lax.fori_loop(0, sent[1], b_done, 0)
    for k in range(6):
        h = (0, 1, 0, 1, 0, 1)[k]
        pltpu.make_async_copy(part(hid_full, h, row), part(hid_full, h, row), y_s.at[k]).wait()


def gather_all(send_from, pick, hidden, wa, wb, rows, cols, cap):
    requests, _, model = hidden.shape
    width = model // rows
    dt = hidden.dtype
    smem = pl.BlockSpec(memory_space=pltpu.SMEM)
    hbm = pl.BlockSpec(memory_space=pl.ANY)
    vmem = pl.BlockSpec(memory_space=pltpu.VMEM)
    dma = pltpu.SemaphoreType.DMA

    def body(*refs):
        gather_kernel(rows, cols, cap, *refs)

    return pl.pallas_call(
        body,
        out_shape=(
            jax.ShapeDtypeStruct(hidden.shape, dt),
            jax.ShapeDtypeStruct((wa.shape[0] * cols, wa.shape[1]), dt),
            jax.ShapeDtypeStruct((wb.shape[0] * cols, wb.shape[1]), dt),
        ),
        in_specs=[smem, smem, hbm, vmem, vmem],
        out_specs=(hbm, hbm, hbm),
        scratch_shapes=[
            pltpu.VMEM((requests, LEN, width), dt),
            pltpu.VMEM((cols * cap, LEN, width), dt),
            pltpu.VMEM((cols * cap, LEN, width), dt),
            pltpu.VMEM((requests, LEN, width), dt),
            dma((5,)), dma((cols,)), dma((cols,)),
            dma((48,)), dma((48,)), dma((cols,)), dma((cols,)),
            dma((6,)), dma((rows, 2)),
        ],
        compiler_params=pltpu.CompilerParams(
            collective_id=0, has_side_effects=True, vmem_limit_bytes=32 << 20
        ),
        name="gather_all",
    )(send_from, pick, hidden, wa, wb)


def return_kernel(
    rows, cols, cap, back_from, home_key, part, ss, mixed,
    mine, came, ss_in, scale, mix, packed, got0, got1, got2,
    loc, ss_s, ss_r, y_s, y_r, a2a_s, a2a_r,
):
    row, me = lax.axis_index("row"), lax.axis_index("col")
    barrier = greet(row, me, rows, cols)
    pieces = part.shape[0] // rows
    tokens = part.shape[1]
    keep = pltpu.make_async_copy(part.at[pl.ds(row * pieces, pieces)], mine, loc.at[0])
    keep.start()
    pl.semaphore_wait(barrier, cols - 1 + rows - 1)
    order = (1, 3, 2)
    for k, d in enumerate(order):
        peer = (row + d) % rows
        pltpu.make_async_remote_copy(
            ss, ss_in.at[row], ss_s.at[k], ss_r.at[row],
            device_id=(peer, me), device_id_type=MESH,
        ).start()
    for j in range(pieces):
        for k, d in enumerate(order):
            peer = (row + d) % rows
            pltpu.make_async_remote_copy(
                part.at[peer * pieces + j], came.at[row, j], y_s.at[j, k], y_r.at[row, j],
                device_id=(peer, me), device_id_type=MESH,
            ).start()
    total = ss[...]
    for d in order:
        peer = (row + d) % rows
        pltpu.make_async_copy(ss_in.at[peer], ss_in.at[peer], ss_r.at[peer]).wait()
        total = total + ss_in[peer]
    factor = lax.rsqrt(total / INNER + 1e-05)
    for i in range(tokens // TOK):
        line = jnp.broadcast_to(factor[i : i + 1, :], (TOK, TOK))
        scale[pl.ds(i * TOK, TOK), :] = line.T
    keep.wait()
    gots = (got0, got1, got2)

    def piece(ref, c):
        return ref.at[pl.ds(c * cap, cap)]

    for j in range(pieces):
        for d in order:
            peer = (row + d) % rows
            pltpu.make_async_copy(came.at[peer, j], came.at[peer, j], y_r.at[peer, j]).wait()

        def add(i, carry):
            at = pl.ds(pl.multiple_of(i * TOK, TOK), TOK)
            value = mine[j, at, :].astype(jnp.float32)
            for d in order:
                value = value + came[(row + d) % rows, j, at, :].astype(jnp.float32)
            value = (value * scale[at, :]).astype(mix.dtype)
            mix[pl.ds(i * GROUP, GROUP)] = value.reshape(GROUP, LEN, 128)
            return carry

        lax.fori_loop(0, tokens // TOK, add, 0)

        def pack(s, carry):
            packed[j, s] = mix[back_from[s]]
            return carry

        lax.fori_loop(0, cols * cap, pack, 0)

        def push(d, carry):
            peer = (me + d) % cols
            pltpu.make_async_remote_copy(
                piece(packed.at[j], peer), piece(gots[j], me), a2a_s.at[j, peer], a2a_r.at[j, me],
                device_id=(row, peer), device_id_type=MESH,
            ).start()
            return carry

        lax.fori_loop(1, cols, push, 0)
        pltpu.make_async_copy(piece(packed.at[j], me), piece(gots[j], me), loc.at[1 + j]).start()
    for j in range(pieces):
        got = gots[j]
        pltpu.make_async_copy(piece(packed.at[j], me), piece(got, me), loc.at[1 + j]).wait()

        def took(d, carry):
            peer = (me + d) % cols
            pltpu.make_async_copy(piece(got, peer), piece(got, peer), a2a_r.at[j, peer]).wait()
            return carry

        lax.fori_loop(1, cols, took, 0)

        def unpack(s, carry):
            mixed[s, :, j * 128 : (j + 1) * 128] = got[home_key[s]]
            return carry

        lax.fori_loop(0, mixed.shape[0], unpack, 0)
    for k in range(3):
        pltpu.make_async_copy(ss, ss, ss_s.at[k]).wait()
        for j in range(pieces):
            pltpu.make_async_copy(mine.at[j], mine.at[j], y_s.at[j, k]).wait()
    for j in range(pieces):

        def gone(d, carry):
            peer = (me + d) % cols
            pltpu.make_async_copy(
                piece(packed.at[j], peer), piece(packed.at[j], peer), a2a_s.at[j, peer]
            ).wait()
            return carry

        lax.fori_loop(1, cols, gone, 0)


def send_home(back_from, home_key, part, ss, rows, cols, cap):
    pieces = part.shape[0] // rows
    tokens = part.shape[1]
    smem = pl.BlockSpec(memory_space=pltpu.SMEM)
    hbm = pl.BlockSpec(memory_space=pl.ANY)
    vmem = pl.BlockSpec(memory_space=pltpu.VMEM)
    dma = pltpu.SemaphoreType.DMA
    slots = cols * cap
    requests = tokens // LEN
    dt = part.dtype

    def body(*refs):
        return_kernel(rows, cols, cap, *refs)

    return pl.pallas_call(
        body,
        out_shape=jax.ShapeDtypeStruct((requests, LEN, pieces * 128), dt),
        in_specs=[smem, smem, hbm, vmem],
        out_specs=vmem,
        scratch_shapes=[
            pltpu.VMEM((pieces, tokens, 128), dt),
            pltpu.VMEM((rows, pieces, tokens, 128), dt),
            pltpu.VMEM((rows,) + ss.shape, jnp.float32),
            pltpu.VMEM((tokens, 128), jnp.float32),
            pltpu.VMEM((requests, LEN, 128), dt),
            pltpu.VMEM((pieces, slots, LEN, 128), dt),
            pltpu.VMEM((slots, LEN, 128), dt),
            pltpu.VMEM((slots, LEN, 128), dt),
            pltpu.VMEM((slots, LEN, 128), dt),
            dma((1 + pieces,)), dma((3,)), dma((rows,)),
            dma((pieces, 3)), dma((rows, pieces)), dma((pieces, cols)), dma((pieces, cols)),
        ],
        compiler_params=pltpu.CompilerParams(
            collective_id=1, has_side_effects=True, vmem_limit_bytes=32 << 20
        ),
        name="send_home",
    )(back_from, home_key, part, ss)


def silu(v):
    return v / (1.0 + jnp.exp(-v))


def mixer_kernel(
    prev_slot, cont, acc, hid, fa, fb, dtb, rate, skip, cxw, cxb, cbw, cbb, gain,
    prev, pex, peb, part, ss, nst, nex, neb, zx, bc, dts, gg, cx, cb,
):
    f32, bf16 = jnp.float32, jnp.bfloat16
    inner = gain.shape[1]
    tokens = hid.shape[0]
    heads = inner // HEAD_DIM

    @pl.loop(0, 2 * inner // 256)
    def _(n):
        at = pl.ds(pl.multiple_of(n * 256, 256), 256)
        zx[:, at] = jnp.dot(hid[...], fa[:, at], preferred_element_type=f32).astype(bf16)

    bc[...] = jnp.dot(
        hid[...], fb[:, inner : inner + 2 * STATE], preferred_element_type=f32
    ).astype(bf16)
    dts[...] = jnp.dot(hid[...], fb[:, inner + 2 * STATE :], preferred_element_type=f32)

    t_ids = lax.broadcasted_iota(jnp.int32, (TOK, TOK), 0)
    s_ids = lax.broadcasted_iota(jnp.int32, (TOK, TOK), 1)
    same = (t_ids // LEN) == (s_ids // LEN)
    causal = same & (t_ids >= s_ids)
    tri = causal.astype(f32)
    spread_h = (
        lax.broadcasted_iota(jnp.int32, (TOK, inner), 1) // HEAD_DIM
        == lax.broadcasted_iota(jnp.int32, (TOK, inner), 0)
    ).astype(f32)

    @pl.loop(0, tokens // TOK)
    def _(i):
        at = pl.ds(pl.multiple_of(i * TOK, TOK), TOK)
        live, last = [], jnp.zeros((TOK, TOK), jnp.int32)
        for r in range(GROUP):
            s = i * GROUP + r
            flag = cont[s].astype(f32)
            live.append(flag)
            last = jnp.where(t_ids // LEN == r, acc[s], last)
            cx[r, 13:16, :] = pex[prev_slot[s]].astype(f32) * flag
            cb[r, 13:16, :] = peb[prev_slot[s]].astype(f32) * flag
        cx[:, 16:32, :] = zx[at, inner:].astype(f32).reshape(GROUP, LEN, inner)
        cb[:, 16:32, :] = bc[at, :].astype(f32).reshape(GROUP, LEN, 2 * STATE)
        tot_x = cxb[...].reshape(1, 1, inner) + cxw[0:1, :].reshape(1, 1, inner) * cx[:, 13:29, :]
        tot_b = cbb[...].reshape(1, 1, 2 * STATE) + cbw[0:1, :].reshape(
            1, 1, 2 * STATE
        ) * cb[:, 13:29, :]
        for k in range(1, KCONV):
            tot_x = tot_x + cxw[k : k + 1, :].reshape(1, 1, inner) * cx[:, 13 + k : 29 + k, :]
            tot_b = tot_b + cbw[k : k + 1, :].reshape(1, 1, 2 * STATE) * cb[:, 13 + k : 29 + k, :]
        xc = silu(tot_x).reshape(TOK, inner).astype(bf16)
        bcc = silu(tot_b).reshape(TOK, 2 * STATE).astype(bf16)
        for r in range(GROUP):
            s = i * GROUP + r
            nex[s] = pltpu.roll(cx[r], 19 - acc[s], 0)[0:3, :].astype(bf16)
            neb[s] = pltpu.roll(cb[r], 19 - acc[s], 0)[0:3, :].astype(bf16)
        b_in, c_in = bcc[:, :STATE], bcc[:, STATE:]
        xf = xc.astype(f32)
        raw = dts[at, :] + dtb[...]
        step = jnp.maximum(raw, 0.0) + jnp.log(1.0 + jnp.exp(-jnp.abs(raw)))
        decay = jnp.dot(tri, step * rate[...], precision=HIGHEST, preferred_element_type=f32)
        decay_t = decay.T
        step_t = step.T
        choose = (same & (s_ids % LEN == last - 1)).astype(f32)
        reach = jnp.dot(choose, decay, precision=HIGHEST, preferred_element_type=f32)
        taken = t_ids % LEN < last
        weight = jnp.where(taken, jnp.exp(jnp.minimum(reach - decay, 0.0)), 0.0) * step
        weight_x = jnp.dot(weight, spread_h, precision=HIGHEST, preferred_element_type=f32)
        grow_x = jnp.dot(jnp.exp(decay), spread_h, precision=HIGHEST, preferred_element_type=f32)
        scores = lax.dot_general(
            c_in, b_in, (((1,), (1,)), ((), ())), preferred_element_type=f32
        )
        scores = jnp.where(causal, scores, 0.0)
        half = s_ids < HEAD_DIM
        zero = jnp.zeros((TOK, 2 * HEAD_DIM), bf16)
        y = []
        for pair in range(heads // 2):
            mats = []
            for h in (2 * pair, 2 * pair + 1):
                gap = decay[:, h : h + 1] - decay_t[h : h + 1, :]
                mats.append(
                    (jnp.exp(jnp.minimum(gap, 0.0)) * scores * step_t[h : h + 1, :]).astype(bf16)
                )
            xp = xc[:, pair * 128 : (pair + 1) * 128]
            both = jnp.concatenate([jnp.where(half, xp, zero), jnp.where(half, zero, xp)], axis=0)
            y.append(
                jnp.dot(jnp.concatenate(mats, axis=1), both, preferred_element_type=f32)
            )
        y = jnp.concatenate(y, axis=1)
        carried = []
        for r in range(GROUP):
            s = i * GROUP + r
            from_state = lax.dot_general(
                c_in[r * LEN : (r + 1) * LEN, :], prev[prev_slot[s]], (((1,), (1,)), ((), ())),
                preferred_element_type=f32,
            )
            carried.append(from_state * live[r])
        y = y + grow_x * jnp.concatenate(carried, axis=0) + skip[...] * xf
        gated = y * silu(zx[at, :inner].astype(f32))
        gg[at, :] = (gated * gain[...]).astype(bf16)
        squares = jnp.sum(gated * gated, axis=1, keepdims=True)
        ss[pl.ds(i, 1), :] = jnp.broadcast_to(squares, (TOK, TOK)).T[0:1, :]

        xw = (xf * weight_x).T
        high = xw.astype(bf16)
        low = (xw - high.astype(f32)).astype(bf16)
        lhs = jnp.concatenate([high, low], axis=1)
        keep_t = jnp.exp(reach).T
        none = jnp.zeros((TOK, STATE), bf16)
        for pair in range(GROUP // 2):
            cut = jnp.concatenate(
                [
                    jnp.where(t_ids // LEN == r, b_in, none)
                    for r in (2 * pair, 2 * pair + 1)
                ],
                axis=1,
            )
            added = jnp.dot(
                lhs, jnp.concatenate([cut, cut], axis=0), preferred_element_type=f32
            )
            for k in (0, 1):
                r = 2 * pair + k
                s = i * GROUP + r
                factor = jnp.broadcast_to(keep_t[0:heads, r * LEN : r * LEN + 1], (heads, STATE))
                factor = factor * live[r]
                old = prev[prev_slot[s]].astype(f32).reshape(heads, HEAD_DIM, STATE)
                new = factor[:, None, :] * old + added[:, k * STATE : (k + 1) * STATE].reshape(
                    heads, HEAD_DIM, STATE
                )
                nst[s] = new.reshape(inner, STATE).astype(bf16)

    @pl.loop(0, part.shape[0] // 2)
    def _(q):
        at = pl.ds(pl.multiple_of(q * 256, 256), 256)
        out = lax.dot_general(
            gg[...], fb[at, :inner], (((1,), (1,)), ((), ())), preferred_element_type=f32
        ).astype(bf16)
        part[2 * q] = out[:, :128]
        part[2 * q + 1] = out[:, 128:]


def mixer(prev_slot, cont, acc, hid, fa, fb, vectors, prev, pex, peb):
    tokens, model = hid.shape
    inner = fa.shape[1] // 2
    requests = tokens // LEN
    dt = hid.dtype
    smem = pl.BlockSpec(memory_space=pltpu.SMEM)
    vmem = pl.BlockSpec(memory_space=pltpu.VMEM)
    return pl.pallas_call(
        mixer_kernel,
        out_shape=(
            jax.ShapeDtypeStruct((model // 128, tokens, 128), dt),
            jax.ShapeDtypeStruct((8, 128), jnp.float32),
            jax.ShapeDtypeStruct((requests, inner, STATE), dt),
            jax.ShapeDtypeStruct((requests, 3, inner), dt),
            jax.ShapeDtypeStruct((requests, 3, 2 * STATE), dt),
        ),
        in_specs=[smem] * 3 + [vmem] * (6 + len(vectors)),
        out_specs=(vmem,) * 5,
        scratch_shapes=[
            pltpu.VMEM((tokens, 2 * inner), dt),
            pltpu.VMEM((tokens, 2 * STATE), dt),
            pltpu.VMEM((tokens, 128), jnp.float32),
            pltpu.VMEM((tokens, inner), dt),
            pltpu.VMEM((GROUP, 32, inner), jnp.float32),
            pltpu.VMEM((GROUP, 32, 2 * STATE), jnp.float32),
        ],
        compiler_params=pltpu.CompilerParams(vmem_limit_bytes=52 << 20),
        name="mixer",
    )(prev_slot, cont, acc, hid, fa, fb, *vectors, prev, pex, peb)


def per_device(
    hidden, w_zx, w_bc, w_dt, w_out, dt_bias, a_log, d_skip, conv_x_w, conv_x_b,
    conv_bc_w, conv_bc_b, norm_gain, prev_state, prev_edge_x, prev_edge_bc,
    holder, continued, owner, accepted,
):
    rows, cols = lax.axis_size("row"), lax.axis_size("col")
    col_index = lax.axis_index("col")
    requests = hidden.shape[0] // LEN
    heads = dt_bias.shape[0]
    inner = heads * HEAD_DIM
    held = prev_state.shape[0]
    cap = 4 * ((requests // 4 + cols - 1) // cols)
    home_key, send_from, pick, acc, cont, prev_slot, back_from = routing(
        owner, accepted, continued, col_index, requests, cap
    )
    prev_slot = jnp.minimum(prev_slot, held - 1)
    depth = w_zx.shape[0]
    wa = w_zx.reshape(depth, heads, 2, HEAD_DIM).transpose(0, 2, 1, 3).reshape(depth, 2 * inner)
    pad = jnp.zeros((depth, 128 - heads), w_dt.dtype)
    wb = jnp.concatenate([w_out, w_bc, w_dt, pad], axis=1)
    tokens, model = hidden.shape
    hid, fa, fb = gather_all(
        send_from, pick, hidden.reshape(requests, LEN, model), wa, wb, rows, cols, cap
    )
    hid = hid.reshape(tokens, model)

    def line(v):
        return jnp.pad(v, (0, 128 - v.shape[0]))[None, :]

    vectors = (
        line(dt_bias), line(-jnp.exp(a_log)), jnp.repeat(d_skip, HEAD_DIM)[None, :],
        conv_x_w, conv_x_b[None, :], conv_bc_w, conv_bc_b[None, :], norm_gain[None, :],
    )
    part, ss, new_state, new_edge_x, new_edge_bc = mixer(
        prev_slot, cont, acc, hid, fa, fb, vectors,
        prev_state.reshape(held, inner, STATE), prev_edge_x, prev_edge_bc,
    )
    mixed = send_home(back_from, home_key, part, ss, rows, cols, cap)
    return (
        mixed.reshape(tokens, model // rows), new_state.reshape(requests, heads, HEAD_DIM, STATE), new_edge_x, new_edge_bc,
    )


def solution(mesh):
    return jax.shard_map(
        per_device,
        mesh=mesh,
        in_specs=(
            P("col", None),
            P("col", "row"),
            P("col", None),
            P("col", "row"),
            P("col", "row"),
            P("row"),
            P("row"),
            P("row"),
            P(None, "row"),
            P("row"),
            P(),
            P(),
            P("row"),
            P("col", "row", None, None),
            P("col", None, "row"),
            P("col", None, None),
            P(),
            P(),
            P(),
            P(),
        ),
        out_specs=(
            P("col", "row"),
            P("col", "row", None, None),
            P("col", None, "row"),
            P("col", None, None),
        ),
        check_vma=False,
    )
```

time: 313 us -> 159 us (0.51)
  waiting for transfers between devices: 175 us -> 0 us
  Pallas kernels: 0 us -> 132 us
  matrix products: 48.1 us -> 0 us
  starting transfers between devices: 17.5 us -> 0 us
  local copies, waits for them, and re-layouts: 32.3 us -> 17.2 us
  between operations: 14.7 us -> 0.79 us
  blocking collectives: 8.43 us -> 0 us
  other arithmetic: 16 us -> 7.77 us
    pallas_call x0 -> x3, Pallas kernels: none -> 132 us  [the longest x1 55.8 us: gather_all(): pl.pallas_call(body, out_shape=(jax.ShapeDtypeStruct(hidden.shape, dt), j...]
    all_gather x3 -> x0, waiting for transfers between devices: 101 us -> none  [the longest x1 48.1 us: per_device(): full_rest = lax.all_gather(rest, 'col', axis=0, tiled=True)]
    reduce_scatter x1 -> x0, waiting for transfers between devices: 49.4 us -> none  [per_device(): lax.psum_scatter(partial_out, 'row', scatter_dimension=1, tiled=True)]
    dot_general x15 -> x0, matrix products: 48.1 us -> none  [the longest x1 15.3 us: per_device(): jnp.einsum('rsh,rshp,rsn->rhpn', weight_s, x_conv, b_in, precision=highest)]
    all_to_all x2 -> x0, waiting for transfers between devices: 23.5 us -> none  [the longest x1 18.2 us: per_device(): got = lax.all_to_all(packed, 'col', split_axis=0, concat_axis=0, tiled=True)]
    all_to_all x2 -> x0, starting transfers between devices: 17.4 us -> none  [the longest x1 9.57 us: per_device(): got = lax.all_to_all(packed, 'col', split_axis=0, concat_axis=0, tiled=True)]
    psum x1 -> x0, blocking collectives: 8.43 us -> none  [per_device(): totals = lax.psum(jnp.sum(gated * gated, axis=1), 'row')]
    reshape x9 -> x3, local copies, waits for them, and re-layouts: 7.43 us -> 1.3 us  [per_device(): w_zx.reshape(depth, heads, 2, HEAD_DIM).transpose(0, 2, 1, 3)]
  transfers between devices with their start and end apart: 6 -> 0, of which waited for: 6 -> 0; matrix products, arithmetic and copies ran while one was open for 14% -> 0% of each run, Pallas kernels for 0% -> 0%
where the time goes in v2:
time: 159 us; the launch traced here: 158 us
  Pallas kernels  132 us (83%)
  local copies, waits for them, and re-layouts  17.2 us (11%)
  other arithmetic  7.77 us (5%)
    pallas_call x1, Pallas kernels, gather_all(): pl.pallas_call(body, out_shape=(jax.ShapeDtypeStruct(hidden.shape, dt), j...  55.8 us
    pallas_call x1, Pallas kernels, send_home(): pl.pallas_call(body, out_shape=jax.ShapeDtypeStruct((requests, LEN, piece...  47.7 us
    pallas_call x1, Pallas kernels, mixer(): pl.pallas_call(mixer_kernel, out_shape=(jax.ShapeDtypeStruct((model // 12...  28.5 us
    unnamed x26, local copies, waits for them, and re-layouts  12.6 us

profile of v2, /device:TPU:1, one launch (start us, length us, event | category | flops | bytes accessed | tf_op | source)
XLA Modules:
  0.0 157.8 jit_solution(15292087465465304245)
XLA Ops:
  0.6 0.0 copy-start.8
  0.6 0.0 copy-start.9
  0.7 0.0 copy-start.6
  0.7 0.0 copy-start.7
  0.7 0.0 copy-start.5
  0.7 0.7 exponential_negate_fusion
  1.4 0.8 dynamic_slice.3
  2.1 0.2 convert_reduce_fusion
  2.3 0.8 multiply_add_fusion.refs_1_
  3.1 0.1 select_reduce_fusion.4.refs_0_
  3.2 0.7 pad_bitcast_fusion
  3.9 0.1 pad.12.clone
  3.9 0.7 broadcast_compare_fusion
  4.6 0.1 reshape.96
  4.7 0.1 convert_reduce_fusion.1
  4.9 0.1 select_reduce_fusion.7
  5.0 0.7 broadcast_in_dim.160
  5.7 0.1 broadcast_in_dim_reshape.2.skip
  5.8 0.7 compare_convert_fusion
  6.5 0.1 reshape.104
  6.6 0.8 copy.30
  7.4 0.6 select_reduce_fusion.3
  8.0 0.1 broadcast_add_fusion
  8.0 0.8 broadcast_in_dim.154
  8.8 2.7 %select_reduce_fusion = (s32[48]{0:T(128)S(1)}, s32[48]{0:T(128)S(1)}, s32[48]{0:T(128)S(1)}) fusion(s32[32,48]{1,0:T(8,128)S(1)} %broadcast_in_dim.154, s32[32,48]{1,0:T(8,128)S(1)} %get-tuple-element.32, s32[32,48]{1,0:T(8,128)S(1)} %reshape.104, s32[32,48]{1,0:T(8,128)S(1)} %get-tuple-element.31), kind=kLoop, calls=%fused_computation | loop fusion | flops 515952 | bytes 25152 | tf_op jit(solution)/shard_map/reduce_sum | solution.py:40
  11.5 0.1 select_reduce_fusion.5
  11.6 0.1 select_reduce_fusion.6.refs_0_
  11.7 0.8 copy.32.peb
  12.5 0.8 maximum_maximum_fusion.refs_4_
  13.3 0.9 copy.31.pex
  14.3 1.1 reshape.98
  15.4 0.2 reshape.99.refs_3_
  15.6 0.0 copy-start.2
  15.6 1.7 %copy-done.2 = bf16[768,1536]{1,0:T(8,128)(2,1)S(1)} copy-done((bf16[768,1536]{1,0:T(8,128)(2,1)S(1)}, bf16[768,1536]{1,0:T(8,128)(2,1)}, u32[]{:S(2)}) %copy-start.2) | copy-done | bytes 2359320
  17.3 55.8 %gather_all.1 = (bf16[48,16,1536]{2,1,0:T(8,128)(2,1)S(1)}, bf16[1536,1024]{1,0:T(8,128)(2,1)S(1)}, bf16[1536,896]{1,0:T(8,128)(2,1)S(1)}) custom-call(s32[128]{0:T(128)S(1)} %select_reduce_fusion.4.refs_0_, s32[48]{0:T(128)S(1)} %get-tuple-element.30.refs_1_, bf16[48,16,1536]{2,1,0:T(8,128)(2,1)S(1)} %bitcast.17, bf16[48,1024]{1,0:T(8,128)(2,1)S(1)} %reshape.99.refs_3_, ...), custom_call_target="tpu_custom_call" | custom-call | tf_op jit(solution)/shard_map/gather_all/pallas_call | solution.py:279
  73.1 0.0 copy-start
  73.1 1.7 %copy-done = bf16[1536,1024]{1,0:T(8,128)(2,1)} copy-done((bf16[1536,1024]{1,0:T(8,128)(2,1)}, bf16[1536,1024]{1,0:T(8,128)(2,1)S(1)}, u32[]{:S(2)}) %copy-start) | copy-done | bytes 3145752
  74.7 0.0 copy-start.1
  74.7 1.6 copy-done.1
  76.3 0.0 copy-start.4
  76.3 1.4 copy-done.4
  77.7 0.0 copy-done.8
  77.7 0.0 copy-done.9
  77.7 0.0 copy-done.6
  77.7 0.0 copy-done.7
  77.7 0.0 copy-done.5
  77.7 28.5 %mixer.1 = (bf16[12,768,128]{2,1,0:T(8,128)(2,1)}, f32[8,128]{1,0:T(8,128)S(1)}, bf16[48,512,128]{2,1,0:T(8,128)(2,1)}, bf16[48,3,512]{2,1,0:T(4,128)(2,1)S(1)}, bf16[48,3,256]{2,1,0:T(4,128)(2,1)S(1)}) custom-call(s32[48]{0:T(128)S(1)} %broadcast_minimum_fusion.prev_slot, s32[48]{0:T(128)S(1)} %get-tuple-element.29.cont, s32[48]{0:T(128)S(1)} %get-tuple-element.28.acc, ...), custom_call_target="tpu_custom_call" | custom-call | tf_op jit(solution)/shard_map/mixer/pallas_call | solution.py:599
  106.3 0.0 copy-start.3
  106.3 1.7 %copy-done.3 = bf16[12,768,128]{2,1,0:T(8,128)(2,1)S(1)} copy-done((bf16[12,768,128]{2,1,0:T(8,128)(2,1)S(1)}, bf16[12,768,128]{2,1,0:T(8,128)(2,1)}, u32[]{:S(2)}) %copy-start.3) | copy-done | bytes 2359320
  107.9 47.7 %send_home.1 = bf16[48,16,384]{2,1,0:T(8,128)(2,1)S(1)} custom-call(s32[128]{0:T(128)S(1)} %select_reduce_fusion.6.refs_0_, s32[48]{0:T(128)S(1)} %multiply_add_fusion.refs_1_, bf16[12,768,128]{2,1,0:T(8,128)(2,1)S(1)} %copy-done.3, f32[8,128]{1,0:T(8,128)S(1)} %get-tuple-element.16.refs_3_), custom_call_target="tpu_custom_call" | custom-call | tf_op jit(solution)/shard_map/send_home/pallas_call | solution.py:423
  155.7 0.6 copy.34
  156.3 0.7 copy.33
  157.0 0.8 copy.38
  (6 shorter events, 0.1 us)
Async XLA Ops:
  0.6 77.1 %copy-start.8 = (f32[512]{0:T(512)S(1)}, f32[512]{0:T(512)}, u32[]{:S(2)}) copy-start(f32[512]{0:T(512)} %param.32) | copy-start | bytes 6148
  0.6 77.1 %copy-start.9 = (f32[256]{0:T(256)S(1)}, f32[256]{0:T(256)}, u32[]{:S(2)}) copy-start(f32[256]{0:T(256)} %param.31) | copy-start | bytes 3076
  0.7 77.1 %copy-start.6 = (f32[4,256]{1,0:T(4,128)S(1)}, f32[4,256]{1,0:T(4,128)}, u32[]{:S(2)}) copy-start(f32[4,256]{1,0:T(4,128)} %cbw.1) | copy-start | bytes 12292
  0.7 77.1 %copy-start.7 = (f32[512]{0:T(512)S(1)}, f32[512]{0:T(512)}, u32[]{:S(2)}) copy-start(f32[512]{0:T(512)} %param.29) | copy-start | bytes 6148
  0.7 77.1 %copy-start.5 = (f32[4,512]{1,0:T(4,128)S(1)}, f32[4,512]{1,0:T(4,128)}, u32[]{:S(2)}) copy-start(f32[4,512]{1,0:T(4,128)} %cxw.1) | copy-start | bytes 24580
  15.6 1.7 %copy-start.2 = (bf16[768,1536]{1,0:T(8,128)(2,1)S(1)}, bf16[768,1536]{1,0:T(8,128)(2,1)}, u32[]{:S(2)}) copy-start(bf16[768,1536]{1,0:T(8,128)(2,1)} %param.20) | copy-start | bytes 7077892
  73.1 1.7 %copy-start = (bf16[1536,1024]{1,0:T(8,128)(2,1)}, bf16[1536,1024]{1,0:T(8,128)(2,1)S(1)}, u32[]{:S(2)}) copy-start(bf16[1536,1024]{1,0:T(8,128)(2,1)S(1)} %get-tuple-element.13.fa) | copy-start | bytes 9437188
  74.7 1.6 copy-start.1
  76.3 1.4 copy-start.4
  106.3 1.7 %copy-start.3 = (bf16[12,768,128]{2,1,0:T(8,128)(2,1)S(1)}, bf16[12,768,128]{2,1,0:T(8,128)(2,1)}, u32[]{:S(2)}) copy-start(bf16[12,768,128]{2,1,0:T(8,128)(2,1)} %get-tuple-element.15.refs_2_) | copy-start | bytes 7077892

commit v3 on v2

--- a/solution.py
+++ b/solution.py
@@ -17,34 +17,112 @@
 HIGHEST = lax.Precision.HIGHEST
 
 
-def routing(owner, accepted, continued, col_index, request_count, cap):
-    total = owner.shape[0]
-    groups = total // request_count
-    local = jnp.arange(request_count, dtype=jnp.int32)
-    slots = jnp.arange(groups * cap, dtype=jnp.int32)
-    mine = lax.dynamic_slice_in_dim(owner, col_index * request_count, request_count)
-    earlier = local[None, :] < local[:, None]
-    rank = jnp.sum(((mine[None, :] == mine[:, None]) & earlier).astype(jnp.int32), axis=1)
-    home_key = mine * cap + rank
-    send_from = jnp.sum(jnp.where(home_key[None, :] == slots[:, None], local[None, :], 0), axis=1)
-    owned = (owner == col_index).reshape(groups, request_count)
-    owned_int = owned.astype(jnp.int32)
-    in_group = jnp.sum(jnp.where(earlier[None], owned_int[:, None, :], 0), axis=2)
-    counts = jnp.sum(owned_int, axis=1)
-    group = jnp.arange(groups, dtype=jnp.int32)
-    before = jnp.sum(jnp.where(group[None, :] < group[:, None], counts[None, :], 0), axis=1)
-    slot = jnp.where(owned, in_group + before[:, None], -1)
-    match = slot[None] == local[:, None, None]
-
-    def picked(values):
-        return jnp.sum(jnp.where(match, values[None], 0), axis=(1, 2))
-
-    pick = picked(group[:, None] * cap + in_group)
-    own_accepted = picked(accepted.reshape(groups, request_count))
-    own_cont = picked((continued == 1).astype(jnp.int32).reshape(groups, request_count))
-    own_prev = jnp.sum(jnp.where(earlier, own_cont[None, :], 0), axis=1)
-    back_from = jnp.sum(jnp.where(pick[None, :] == slots[:, None], local[None, :], 0), axis=1)
-    return home_key, send_from, pick, own_accepted, own_cont, own_prev, back_from
+def route_kernel(held, code, out):
+    f32, bf16 = jnp.float32, jnp.bfloat16
+    me = lax.axis_index("col")
+    groups, requests = code.shape
+    value = code[...]
+    o, c, a = value & 63, (value >> 6) & 1, value >> 7
+
+    def dot(x, y):
+        return jnp.dot(x.astype(bf16), y.astype(bf16), preferred_element_type=f32)
+
+    def dot0(x, y):
+        return lax.dot_general(
+            x.astype(bf16), y.astype(bf16), (((0,), (0,)), ((), ())), preferred_element_type=f32
+        )
+
+    def ids(shape, dim):
+        return lax.broadcasted_iota(jnp.int32, shape, dim)
+
+    below = (ids((requests, requests), 0) < ids((requests, requests), 1)).astype(f32)
+    prior = (ids((groups, groups), 1) < ids((groups, groups), 0)).astype(f32)
+    lane = ids((groups, 128), 1).astype(f32)
+    group = ids((groups, 128), 0).astype(f32)
+    spots, inside, starts = [], [], []
+    for kind in (1, 0):
+        mask = ((o == me) & (c == kind)).astype(f32)
+        rank = dot(mask, below)
+        count = jnp.broadcast_to(jnp.sum(mask, axis=1, keepdims=True), (groups, 128))
+        start = dot(prior, count)
+        hot = ((start <= lane) & (lane < start + count)).astype(f32)
+        spots.append((jnp.where(mask > 0, rank, -1.0), hot))
+        inside.append(rank)
+        starts.append(start)
+    rank_all, start_all = inside[0] + inside[1], starts[0] + starts[1]
+    picks, places, taken = [], [], []
+    for k in (0, 1):
+        spot, hot = spots[k]
+        order = jnp.sum(hot * (lane - starts[k]), axis=0, keepdims=True)
+        any_hot = jnp.sum(hot, axis=0, keepdims=True)
+        order = jnp.where(any_hot > 0, order, -5.0)
+        match = (dot0(spot, hot) == order).astype(f32)
+        picks.append(jnp.sum(hot * (2 * group + lane - starts[k]), axis=0, keepdims=True))
+        places.append(
+            jnp.sum(hot * start_all, axis=0, keepdims=True)
+            + jnp.sum(match * dot0(rank_all, hot), axis=0, keepdims=True)
+        )
+        taken.append(jnp.sum(match * dot0(a, hot), axis=0, keepdims=True))
+    lane_i, group_i = ids((groups, 128), 1), ids((groups, 128), 0)
+    back = jnp.sum(
+        jnp.where(lane_i // 2 == group_i, starts[0] + (lane_i % 2).astype(f32), 0.0),
+        axis=0, keepdims=True,
+    )
+    back = jnp.minimum(back, held - 1.0)
+
+    def my_row(x, fill):
+        row = jnp.sum(
+            jnp.where(ids((groups, requests), 0) == me, x, 0).astype(f32), axis=0, keepdims=True
+        )
+        rest = jnp.full((1, 128 - requests), fill, f32)
+        return jnp.concatenate([row, rest], axis=1)
+
+    o_row, c_row, a_row = my_row(o, 99.0), my_row(c, 2.0), my_row(a, 0.0)
+
+    def column(row):
+        return jnp.broadcast_to(row, (128, 128)).T
+
+    o_col, c_col, a_col = column(o_row), column(c_row), column(a_row)
+    ii, jj = ids((128, 128), 0), ids((128, 128), 1)
+    alike = (o_col == o_row) & (c_col == c_row)
+    rank_row = jnp.sum((alike & (ii < jj)).astype(f32), axis=0, keepdims=True)
+    rank_col = jnp.sum((alike & (jj < ii)).astype(f32), axis=1, keepdims=True)
+    nth_row = jnp.sum(((c_col == 0) & (ii < jj)).astype(f32), axis=0, keepdims=True)
+    nth_col = jnp.sum(((c_row == 0) & (jj < ii)).astype(f32), axis=1, keepdims=True)
+    key_row = 2 * o_row + rank_row
+    key_col = 2 * o_col + rank_col
+    fi, fj = ii.astype(f32), jj.astype(f32)
+    goes = (c_col == 1) & (key_col == fj)
+    stays = (c_col == 0) & (nth_col == fj)
+
+    def total(mask, x):
+        return jnp.sum(jnp.where(mask, x, 0.0), axis=0, keepdims=True)
+
+    table = (
+        total(goes, fi), picks[0], back,
+        jnp.where(c_row == 1, key_row, 0.0), jnp.where(c_row == 0, held + nth_row, 0.0),
+        (c_row == 1).astype(f32),
+        total(stays, fi), total(stays, key_col), total(stays, a_col),
+        taken[0], places[0], picks[1], places[1],
+    )
+    for k, line in enumerate(table):
+        out[k : k + 1, :] = line.astype(jnp.int32)
+    out[len(table) :, :] = jnp.zeros((16 - len(table), 128), jnp.int32)
+
+
+SEND, PICK, BACK, FROM_MSG, FROM_MIX, MOVED, STAY, STAY_KEY, STAY_ACC, ACC, POS, PICK_O, POS_O = range(13)
+
+
+def route(code, held):
+    vmem = pl.BlockSpec(memory_space=pltpu.VMEM)
+
+    def body(*refs):
+        route_kernel(held, *refs)
+
+    return pl.pallas_call(
+        body, out_shape=jax.ShapeDtypeStruct((16, 128), jnp.int32),
+        in_specs=[vmem], out_specs=vmem, name="route",
+    )(code)
 
 
 def greet(row, me, rows, cols):
@@ -69,13 +147,13 @@
 
 
 def gather_kernel(
-    rows, cols, cap, send_from, pick, hidden, wa, wb, hid_full, fa, fb,
-    sl, packed, got, own, loc, a2a_s, a2a_r, was, wbs, war, wbr, y_s, y_r,
+    rows, cols, cap, tab, hidden, wa, w_out, w_bc, w_dt, hid_full, fa, fb,
+    wb, sl, packed, got, own, loc, a2a_s, a2a_r, was, wbs, war, wbr, y_s, y_r,
 ):
     row, me = lax.axis_index("row"), lax.axis_index("col")
     barrier = greet(row, me, rows, cols)
     width = sl.shape[2]
-    half = sl.shape[0] // 2
+    half = own.shape[0] // 2
     depth = wa.shape[0]
 
     def cols_of(r):
@@ -86,6 +164,14 @@
 
     load = pltpu.make_async_copy(hidden.at[:, :, cols_of(row)], sl, loc.at[0])
     load.start()
+    inner = w_out.shape[1]
+    states = w_bc.shape[1]
+    heads = w_dt.shape[0]
+    wb[:, :inner] = w_out[...]
+    wb[:, inner : inner + states] = w_bc[...]
+    square = jnp.concatenate([w_dt[...].astype(jnp.float32), jnp.zeros((heads, 128 - depth), jnp.float32)], axis=1)
+    square = jnp.concatenate([square, jnp.zeros((128 - heads, 128), jnp.float32)], axis=0).T
+    wb[:, inner + states :] = square[:depth, :].astype(wb.dtype)
     keep_a = pltpu.make_async_copy(wa, block(fa, me), loc.at[1])
     keep_b = pltpu.make_async_copy(wb, block(fb, me), loc.at[2])
     keep_a.start()
@@ -93,7 +179,7 @@
     load.wait()
 
     def pack(s, carry):
-        packed[s] = sl[send_from[s]]
+        packed[s] = sl[tab[SEND, s]]
         return carry
 
     lax.fori_loop(0, cols * cap, pack, 0)
@@ -171,7 +257,7 @@
     lax.fori_loop(1, cols, took, 0)
 
     def unpack(s, carry):
-        own[s] = got[pick[s]]
+        own[s] = got[tab[PICK, s]]
         return carry
 
     lax.fori_loop(0, own.shape[0], unpack, 0)
@@ -264,14 +350,16 @@
         pltpu.make_async_copy(part(hid_full, h, row), part(hid_full, h, row), y_s.at[k]).wait()
 
 
-def gather_all(send_from, pick, hidden, wa, wb, rows, cols, cap):
+def gather_all(tab, hidden, wa, w_out, w_bc, w_dt, rows, cols, cap, held):
     requests, _, model = hidden.shape
     width = model // rows
     dt = hidden.dtype
     smem = pl.BlockSpec(memory_space=pltpu.SMEM)
-    hbm = pl.BlockSpec(memory_space=pl.ANY)
+    hbm = pl.BlockSpec(memory_space=pltpu.HBM)
     vmem = pl.BlockSpec(memory_space=pltpu.VMEM)
     dma = pltpu.SemaphoreType.DMA
+    depth = wa.shape[0]
+    rest = w_out.shape[1] + w_bc.shape[1] + 128
 
     def body(*refs):
         gather_kernel(rows, cols, cap, *refs)
@@ -279,17 +367,18 @@
     return pl.pallas_call(
         body,
         out_shape=(
-            jax.ShapeDtypeStruct(hidden.shape, dt),
-            jax.ShapeDtypeStruct((wa.shape[0] * cols, wa.shape[1]), dt),
-            jax.ShapeDtypeStruct((wb.shape[0] * cols, wb.shape[1]), dt),
+            jax.ShapeDtypeStruct((held, LEN, model), dt),
+            jax.ShapeDtypeStruct((depth * cols, wa.shape[1]), dt),
+            jax.ShapeDtypeStruct((depth * cols, rest), dt),
         ),
-        in_specs=[smem, smem, hbm, vmem, vmem],
+        in_specs=[smem, hbm, vmem, vmem, vmem, vmem],
         out_specs=(hbm, hbm, hbm),
         scratch_shapes=[
+            pltpu.VMEM((depth, rest), dt),
             pltpu.VMEM((requests, LEN, width), dt),
             pltpu.VMEM((cols * cap, LEN, width), dt),
             pltpu.VMEM((cols * cap, LEN, width), dt),
-            pltpu.VMEM((requests, LEN, width), dt),
+            pltpu.VMEM((held, LEN, width), dt),
             dma((5,)), dma((cols,)), dma((cols,)),
             dma((48,)), dma((48,)), dma((cols,)), dma((cols,)),
             dma((6,)), dma((rows, 2)),
@@ -298,13 +387,13 @@
             collective_id=0, has_side_effects=True, vmem_limit_bytes=32 << 20
         ),
         name="gather_all",
-    )(send_from, pick, hidden, wa, wb)
+    )(tab, hidden, wa, w_out, w_bc, w_dt)
 
 
 def return_kernel(
-    rows, cols, cap, back_from, home_key, part, ss, mixed,
-    mine, came, ss_in, scale, mix, packed, got0, got1, got2,
-    loc, ss_s, ss_r, y_s, y_r, a2a_s, a2a_r,
+    rows, cols, cap, tab, part, ss, xmsg, emsg, mixed, xgot, egot,
+    mine, came, ss_in, scale, mix0, mix1, mix2, packed, got0, got1, got2,
+    loc, ss_s, ss_r, y_s, y_r, a2a_s, a2a_r, x_s, x_r, e_s, e_r,
 ):
     row, me = lax.axis_index("row"), lax.axis_index("col")
     barrier = greet(row, me, rows, cols)
@@ -327,6 +416,23 @@
                 part.at[peer * pieces + j], came.at[row, j], y_s.at[j, k], y_r.at[row, j],
                 device_id=(peer, me), device_id_type=MESH,
             ).start()
+    def piece(ref, c):
+        return ref.at[pl.ds(c * cap, cap)]
+
+    def push_factors(d, carry):
+        peer = (me + d) % cols
+        for src, dst, ss_, rs_ in ((xmsg, xgot, x_s, x_r), (emsg, egot, e_s, e_r)):
+            pltpu.make_async_remote_copy(
+                piece(src, peer), piece(dst, me), ss_.at[peer], rs_.at[me],
+                device_id=(row, peer), device_id_type=MESH,
+            ).start()
+        return carry
+
+    lax.fori_loop(1, cols, push_factors, 0)
+    keep_x = pltpu.make_async_copy(piece(xmsg, me), piece(xgot, me), loc.at[4])
+    keep_e = pltpu.make_async_copy(piece(emsg, me), piece(egot, me), loc.at[5])
+    keep_x.start()
+    keep_e.start()
     total = ss[...]
     for d in order:
         peer = (row + d) % rows
@@ -339,10 +445,9 @@
     keep.wait()
     gots = (got0, got1, got2)
 
-    def piece(ref, c):
-        return ref.at[pl.ds(c * cap, cap)]
-
+    mixes = (mix0, mix1, mix2)
     for j in range(pieces):
+        mix = mixes[j]
         for d in order:
             peer = (row + d) % rows
             pltpu.make_async_copy(came.at[peer, j], came.at[peer, j], y_r.at[peer, j]).wait()
@@ -359,7 +464,7 @@
         lax.fori_loop(0, tokens // TOK, add, 0)
 
         def pack(s, carry):
-            packed[j, s] = mix[back_from[s]]
+            packed[j, s] = mix[tab[BACK, s]]
             return carry
 
         lax.fori_loop(0, cols * cap, pack, 0)
@@ -375,7 +480,7 @@
         lax.fori_loop(1, cols, push, 0)
         pltpu.make_async_copy(piece(packed.at[j], me), piece(gots[j], me), loc.at[1 + j]).start()
     for j in range(pieces):
-        got = gots[j]
+        got, mix = gots[j], mixes[j]
         pltpu.make_async_copy(piece(packed.at[j], me), piece(got, me), loc.at[1 + j]).wait()
 
         def took(d, carry):
@@ -386,7 +491,11 @@
         lax.fori_loop(1, cols, took, 0)
 
         def unpack(s, carry):
-            mixed[s, :, j * 128 : (j + 1) * 128] = got[home_key[s]]
+            moved = tab[MOVED, s].astype(jnp.float32)
+            away = got[tab[FROM_MSG, s]].astype(jnp.float32)
+            here = mix[tab[FROM_MIX, s]].astype(jnp.float32)
+            value = jnp.where(moved > 0.5, away, here)
+            mixed[s, :, j * 128 : (j + 1) * 128] = value.astype(mixed.dtype)
             return carry
 
         lax.fori_loop(0, mixed.shape[0], unpack, 0)
@@ -406,11 +515,24 @@
         lax.fori_loop(1, cols, gone, 0)
 
 
-def send_home(back_from, home_key, part, ss, rows, cols, cap):
+    keep_x.wait()
+    keep_e.wait()
+
+    def factors(d, carry):
+        peer = (me + d) % cols
+        for ref, ss_, rs_ in ((xgot, x_s, x_r), (egot, e_s, e_r)):
+            pltpu.make_async_copy(piece(ref, peer), piece(ref, peer), rs_.at[peer]).wait()
+            pltpu.make_async_copy(piece(ref, peer), piece(ref, peer), ss_.at[peer]).wait()
+        return carry
+
+    lax.fori_loop(1, cols, factors, 0)
+
+
+def send_home(tab, part, ss, xmsg, emsg, rows, cols, cap):
     pieces = part.shape[0] // rows
     tokens = part.shape[1]
     smem = pl.BlockSpec(memory_space=pltpu.SMEM)
-    hbm = pl.BlockSpec(memory_space=pl.ANY)
+    hbm = pl.BlockSpec(memory_space=pltpu.HBM)
     vmem = pl.BlockSpec(memory_space=pltpu.VMEM)
     dma = pltpu.SemaphoreType.DMA
     slots = cols * cap
@@ -420,56 +542,90 @@
     def body(*refs):
         return_kernel(rows, cols, cap, *refs)
 
+    mix = pltpu.VMEM((requests, LEN, 128), dt)
+    got = pltpu.VMEM((slots, LEN, 128), dt)
     return pl.pallas_call(
         body,
-        out_shape=jax.ShapeDtypeStruct((requests, LEN, pieces * 128), dt),
-        in_specs=[smem, smem, hbm, vmem],
-        out_specs=vmem,
+        out_shape=(
+            jax.ShapeDtypeStruct((requests, LEN, pieces * 128), dt),
+            jax.ShapeDtypeStruct(xmsg.shape, dt),
+            jax.ShapeDtypeStruct(emsg.shape, dt),
+        ),
+        in_specs=[smem, hbm, vmem, hbm, hbm],
+        out_specs=(vmem, hbm, hbm),
         scratch_shapes=[
             pltpu.VMEM((pieces, tokens, 128), dt),
             pltpu.VMEM((rows, pieces, tokens, 128), dt),
             pltpu.VMEM((rows,) + ss.shape, jnp.float32),
             pltpu.VMEM((tokens, 128), jnp.float32),
-            pltpu.VMEM((requests, LEN, 128), dt),
+            mix, mix, mix,
             pltpu.VMEM((pieces, slots, LEN, 128), dt),
-            pltpu.VMEM((slots, LEN, 128), dt),
-            pltpu.VMEM((slots, LEN, 128), dt),
-            pltpu.VMEM((slots, LEN, 128), dt),
-            dma((1 + pieces,)), dma((3,)), dma((rows,)),
+            got, got, got,
+            dma((3 + pieces,)), dma((3,)), dma((rows,)),
             dma((pieces, 3)), dma((rows, pieces)), dma((pieces, cols)), dma((pieces, cols)),
+            dma((cols,)), dma((cols,)), dma((cols,)), dma((cols,)),
         ],
         compiler_params=pltpu.CompilerParams(
             collective_id=1, has_side_effects=True, vmem_limit_bytes=32 << 20
         ),
         name="send_home",
-    )(back_from, home_key, part, ss)
+    )(tab, part, ss, xmsg, emsg)
 
 
 def silu(v):
     return v / (1.0 + jnp.exp(-v))
 
 
+def token_masks():
+    t_ids = lax.broadcasted_iota(jnp.int32, (TOK, TOK), 0)
+    s_ids = lax.broadcasted_iota(jnp.int32, (TOK, TOK), 1)
+    return t_ids, s_ids
+
+
 def mixer_kernel(
-    prev_slot, cont, acc, hid, fa, fb, dtb, rate, skip, cxw, cxb, cbw, cbb, gain,
-    prev, pex, peb, part, ss, nst, nex, neb, zx, bc, dts, gg, cx, cb,
+    held, tab, hid_c, hidden, fa, fb, dtb, alog, skip, cxw, cxb, cbw, cbb, gain, prev, pex, peb,
+    part, ss, xmsg, emsg, nst, nex, neb,
+    hid, wa, wb, old, gate, xin, bc, dts, gg, cx, cb, pexf, pebf, new, outs,
+    h_sem, o_sem, w_sem, n_sem, p_sem,
 ):
     f32, bf16 = jnp.float32, jnp.bfloat16
     inner = gain.shape[1]
-    tokens = hid.shape[0]
+    requests = hid.shape[0]
+    tokens = requests * LEN
+    model = hid.shape[2]
     heads = inner // HEAD_DIM
-
-    @pl.loop(0, 2 * inner // 256)
+    blocks = wa.shape[1] // 256
+
+    load_h = pltpu.make_async_copy(hid_c, hid.at[pl.ds(0, held)], h_sem)
+    load_h.start()
+
+    def wa_load(n):
+        at = pl.ds(n * 256, 256)
+        return pltpu.make_async_copy(fa.at[:, at], wa.at[:, at], w_sem.at[n])
+
+    wa_load(0).start()
+
+    def home(n):
+        return pltpu.make_async_copy(hidden.at[tab[STAY, n]], hid.at[held + n], o_sem.at[n])
+
+    @pl.loop(0, requests - held)
     def _(n):
-        at = pl.ds(pl.multiple_of(n * 256, 256), 256)
-        zx[:, at] = jnp.dot(hid[...], fa[:, at], preferred_element_type=f32).astype(bf16)
-
-    bc[...] = jnp.dot(
-        hid[...], fb[:, inner : inner + 2 * STATE], preferred_element_type=f32
-    ).astype(bf16)
-    dts[...] = jnp.dot(hid[...], fb[:, inner + 2 * STATE :], preferred_element_type=f32)
-
-    t_ids = lax.broadcasted_iota(jnp.int32, (TOK, TOK), 0)
-    s_ids = lax.broadcasted_iota(jnp.int32, (TOK, TOK), 1)
+        home(n).start()
+
+    for n in range(1, blocks):
+        wa_load(n).start()
+    late = pl.ds(inner, wb.shape[1] - inner)
+    early = pl.ds(0, inner)
+    load_bc = pltpu.make_async_copy(fb.at[:, late], wb.at[:, late], w_sem.at[blocks])
+    load_out = pltpu.make_async_copy(fb.at[:, early], wb.at[:, early], w_sem.at[blocks + 1])
+    load_old = pltpu.make_async_copy(prev, old, w_sem.at[blocks + 2])
+    load_bc.start()
+    load_old.start()
+    load_out.start()
+    pexf[...] = pex[...].astype(f32)
+    pebf[...] = peb[...].astype(f32)
+
+    t_ids, s_ids = token_masks()
     same = (t_ids // LEN) == (s_ids // LEN)
     causal = same & (t_ids >= s_ids)
     tri = causal.astype(f32)
@@ -478,18 +634,58 @@
         == lax.broadcasted_iota(jnp.int32, (TOK, inner), 0)
     ).astype(f32)
 
-    @pl.loop(0, tokens // TOK)
-    def _(i):
+    def wide(ref):
+        return jnp.concatenate([ref[...], jnp.zeros((1, TOK - heads), f32)], axis=1)
+
+    bias, rate = wide(dtb), -jnp.exp(wide(alog))
+    skip_x = jnp.dot(
+        jnp.broadcast_to(wide(skip), (8, TOK)), spread_h,
+        precision=HIGHEST, preferred_element_type=f32,
+    )[0:1, :]
+
+    load_h.wait()
+
+    @pl.loop(0, requests - held)
+    def _(n):
+        home(n).wait()
+
+    left = lax.broadcasted_iota(jnp.int32, (tokens, 128), 1) < HEAD_DIM
+    for n in range(blocks):
+        wa_load(n).wait()
+        z = jnp.dot(
+            hid[...].reshape(tokens, model), wa[:, n * 256 : (n + 1) * 256],
+            preferred_element_type=f32,
+        )
+        z0, z1 = z[:, :128], z[:, 128:]
+        at = slice(n * 128, (n + 1) * 128)
+        gate[:, at] = jnp.where(left, z0, pltpu.roll(z1, HEAD_DIM, 1)).astype(bf16)
+        xin[:, at] = jnp.where(left, pltpu.roll(z0, HEAD_DIM, 1), z1).astype(bf16)
+    load_bc.wait()
+    z = jnp.dot(hid[...].reshape(tokens, model), wb[:, inner:], preferred_element_type=f32)
+    bc[...] = z[:, : 2 * STATE].astype(bf16)
+    dts[...] = z[:, 2 * STATE :]
+    load_old.wait()
+
+    def store(s):
+        return pltpu.make_async_copy(new.at[s], nst.at[tab[POS, s]], n_sem.at[s])
+
+    def group(i, live):
         at = pl.ds(pl.multiple_of(i * TOK, TOK), TOK)
-        live, last = [], jnp.zeros((TOK, TOK), jnp.int32)
+        first = i * GROUP
+        last = jnp.zeros((TOK, TOK), jnp.int32)
+        accs = []
         for r in range(GROUP):
-            s = i * GROUP + r
-            flag = cont[s].astype(f32)
-            live.append(flag)
-            last = jnp.where(t_ids // LEN == r, acc[s], last)
-            cx[r, 13:16, :] = pex[prev_slot[s]].astype(f32) * flag
-            cb[r, 13:16, :] = peb[prev_slot[s]].astype(f32) * flag
-        cx[:, 16:32, :] = zx[at, inner:].astype(f32).reshape(GROUP, LEN, inner)
+            acc = tab[ACC, first + r] if live else tab[STAY_ACC, first - held + r]
+            accs.append(acc)
+            last = jnp.where(t_ids // LEN == r, acc, last)
+            if live:
+                for k in range(KCONV - 1):
+                    cx[r, 13 + k : 14 + k, :] = pexf[k, pl.ds(first + r, 1), :]
+                    cb[r, 13 + k : 14 + k, :] = pebf[k, pl.ds(first + r, 1), :]
+        if not live:
+            cx[:, 8:16, :] = jnp.zeros((GROUP, 8, inner), f32)
+            cb[:, 8:16, :] = jnp.zeros((GROUP, 8, 2 * STATE), f32)
+        cx[:, 16:32, :] = xin[at, :].astype(f32).reshape(GROUP, LEN, inner)
         cb[:, 16:32, :] = bc[at, :].astype(f32).reshape(GROUP, LEN, 2 * STATE)
         tot_x = cxb[...].reshape(1, 1, inner) + cxw[0:1, :].reshape(1, 1, inner) * cx[:, 13:29, :]
         tot_b = cbb[...].reshape(1, 1, 2 * STATE) + cbw[0:1, :].reshape(
@@ -501,14 +697,25 @@
         xc = silu(tot_x).reshape(TOK, inner).astype(bf16)
         bcc = silu(tot_b).reshape(TOK, 2 * STATE).astype(bf16)
         for r in range(GROUP):
-            s = i * GROUP + r
-            nex[s] = pltpu.roll(cx[r], 19 - acc[s], 0)[0:3, :].astype(bf16)
-            neb[s] = pltpu.roll(cb[r], 19 - acc[s], 0)[0:3, :].astype(bf16)
+            ex = pltpu.roll(cx[r], 19 - accs[r], 0)
+            eb = pltpu.roll(cb[r], 19 - accs[r], 0)
+            if live:
+                place = tab[POS, first + r]
+                for k in range(KCONV - 1):
+                    nex[k, pl.ds(place, 1), :] = ex[k : k + 1, :]
+                    neb[k, pl.ds(place, 1), :] = eb[k : k + 1, :]
+            else:
+                lines = []
+                for k in range(KCONV - 1):
+                    lines.append(ex[k : k + 1, :384])
+                    lines.append(jnp.concatenate([ex[k : k + 1, 384:], eb[k : k + 1, :]], axis=1))
+                lines.append(jnp.zeros((2, 384), f32))
+                emsg[tab[STAY_KEY, first - held + r]] = jnp.concatenate(lines, axis=0).astype(bf16)
         b_in, c_in = bcc[:, :STATE], bcc[:, STATE:]
         xf = xc.astype(f32)
-        raw = dts[at, :] + dtb[...]
+        raw = dts[at, :] + bias
         step = jnp.maximum(raw, 0.0) + jnp.log(1.0 + jnp.exp(-jnp.abs(raw)))
-        decay = jnp.dot(tri, step * rate[...], precision=HIGHEST, preferred_element_type=f32)
+        decay = jnp.dot(tri, step * rate, precision=HIGHEST, preferred_element_type=f32)
         decay_t = decay.T
         step_t = step.T
         choose = (same & (s_ids % LEN == last - 1)).astype(f32)
@@ -516,7 +723,6 @@
         taken = t_ids % LEN < last
         weight = jnp.where(taken, jnp.exp(jnp.minimum(reach - decay, 0.0)), 0.0) * step
         weight_x = jnp.dot(weight, spread_h, precision=HIGHEST, preferred_element_type=f32)
-        grow_x = jnp.dot(jnp.exp(decay), spread_h, precision=HIGHEST, preferred_element_type=f32)
         scores = lax.dot_general(
             c_in, b_in, (((1,), (1,)), ((), ())), preferred_element_type=f32
         )
@@ -537,20 +743,30 @@
                 jnp.dot(jnp.concatenate(mats, axis=1), both, preferred_element_type=f32)
             )
         y = jnp.concatenate(y, axis=1)
-        carried = []
-        for r in range(GROUP):
-            s = i * GROUP + r
-            from_state = lax.dot_general(
-                c_in[r * LEN : (r + 1) * LEN, :], prev[prev_slot[s]], (((1,), (1,)), ((), ())),
-                preferred_element_type=f32,
-            )
-            carried.append(from_state * live[r])
-        y = y + grow_x * jnp.concatenate(carried, axis=0) + skip[...] * xf
-        gated = y * silu(zx[at, :inner].astype(f32))
+        if live:
+            grow_x = jnp.dot(jnp.exp(decay), spread_h, precision=HIGHEST, preferred_element_type=f32)
+            carried = [
+                lax.dot_general(
+                    c_in[r * LEN : (r + 1) * LEN, :], old[first + r], (((1,), (1,)), ((), ())),
+                    preferred_element_type=f32,
+                )
+                for r in range(GROUP)
+            ]
+            y = y + grow_x * jnp.concatenate(carried, axis=0)
+        y = y + skip_x * xf
+        gated = y * silu(gate[at, :].astype(f32))
         gg[at, :] = (gated * gain[...]).astype(bf16)
         squares = jnp.sum(gated * gated, axis=1, keepdims=True)
         ss[pl.ds(i, 1), :] = jnp.broadcast_to(squares, (TOK, TOK)).T[0:1, :]
 
+        if not live:
+            sent = (xf * weight_x).astype(bf16)
+            for r in range(GROUP):
+                key = tab[STAY_KEY, first - held + r]
+                lines = slice(r * LEN, (r + 1) * LEN)
+                xmsg[key, :, :inner] = sent[lines, :]
+                xmsg[key, :, inner:] = b_in[lines, :]
+            return
         xw = (xf * weight_x).T
         high = xw.astype(bf16)
         low = (xw - high.astype(f32)).astype(bf16)
@@ -570,54 +786,181 @@
             )
             for k in (0, 1):
                 r = 2 * pair + k
-                s = i * GROUP + r
+                s = first + r
                 factor = jnp.broadcast_to(keep_t[0:heads, r * LEN : r * LEN + 1], (heads, STATE))
-                factor = factor * live[r]
-                old = prev[prev_slot[s]].astype(f32).reshape(heads, HEAD_DIM, STATE)
-                new = factor[:, None, :] * old + added[:, k * STATE : (k + 1) * STATE].reshape(
+                was = old[s].astype(f32).reshape(heads, HEAD_DIM, STATE)
+                now = factor[:, None, :] * was + added[:, k * STATE : (k + 1) * STATE].reshape(
                     heads, HEAD_DIM, STATE
                 )
-                nst[s] = new.reshape(inner, STATE).astype(bf16)
+                new[s] = now.reshape(inner, STATE).astype(bf16)
+                store(s).start()
+
+    @pl.loop(0, held // GROUP)
+    def _(i):
+        group(i, True)
+
+    @pl.loop(held // GROUP, requests // GROUP)
+    def _(i):
+        group(i, False)
+
+    load_out.wait()
+
+    def put(q):
+        at = pl.ds(2 * q, 2)
+        return pltpu.make_async_copy(outs.at[at], part.at[at], p_sem.at[q])
 
     @pl.loop(0, part.shape[0] // 2)
     def _(q):
         at = pl.ds(pl.multiple_of(q * 256, 256), 256)
         out = lax.dot_general(
-            gg[...], fb[at, :inner], (((1,), (1,)), ((), ())), preferred_element_type=f32
+            gg[...], wb[at, :inner], (((1,), (1,)), ((), ())), preferred_element_type=f32
         ).astype(bf16)
-        part[2 * q] = out[:, :128]
-        part[2 * q + 1] = out[:, 128:]
-
-
-def mixer(prev_slot, cont, acc, hid, fa, fb, vectors, prev, pex, peb):
-    tokens, model = hid.shape
+        outs[2 * q] = out[:, :128]
+        outs[2 * q + 1] = out[:, 128:]
+        put(q).start()
+
+    @pl.loop(0, part.shape[0] // 2)
+    def _(q):
+        put(q).wait()
+
+    @pl.loop(0, held)
+    def _(s):
+        store(s).wait()
+
+
+def mixer(tab, hid_c, hidden, fa, fb, vectors, prev, pex, peb, slots):
+    requests, _, model = hidden.shape
+    held = hid_c.shape[0]
+    tokens = requests * LEN
     inner = fa.shape[1] // 2
-    requests = tokens // LEN
-    dt = hid.dtype
+    heads = inner // HEAD_DIM
+    dt = hidden.dtype
+    f32 = jnp.float32
     smem = pl.BlockSpec(memory_space=pltpu.SMEM)
     vmem = pl.BlockSpec(memory_space=pltpu.VMEM)
+    hbm = pl.BlockSpec(memory_space=pltpu.HBM)
+    dma = pltpu.SemaphoreType.DMA
+
+    def body(*refs):
+        mixer_kernel(held, *refs)
+
     return pl.pallas_call(
-        mixer_kernel,
+        body,
         out_shape=(
             jax.ShapeDtypeStruct((model // 128, tokens, 128), dt),
-            jax.ShapeDtypeStruct((8, 128), jnp.float32),
+            jax.ShapeDtypeStruct((8, 128), f32),
+            jax.ShapeDtypeStruct((slots, LEN, inner + STATE), dt),
+            jax.ShapeDtypeStruct((slots, 8, 384), dt),
             jax.ShapeDtypeStruct((requests, inner, STATE), dt),
-            jax.ShapeDtypeStruct((requests, 3, inner), dt),
-            jax.ShapeDtypeStruct((requests, 3, 2 * STATE), dt),
+            jax.ShapeDtypeStruct((3, requests, inner), f32),
+            jax.ShapeDtypeStruct((3, requests, 2 * STATE), f32),
         ),
-        in_specs=[smem] * 3 + [vmem] * (6 + len(vectors)),
-        out_specs=(vmem,) * 5,
+        in_specs=[smem] + [hbm] * 4 + [vmem] * len(vectors) + [hbm, vmem, vmem],
+        out_specs=(hbm, vmem, vmem, vmem, hbm, vmem, vmem),
         scratch_shapes=[
-            pltpu.VMEM((tokens, 2 * inner), dt),
+            pltpu.VMEM((requests, LEN, model), dt),
+            pltpu.VMEM(fa.shape, dt),
+            pltpu.VMEM(fb.shape, dt),
+            pltpu.VMEM((held, inner, STATE), dt),
+            pltpu.VMEM((tokens, inner), dt),
+            pltpu.VMEM((tokens, inner), dt),
             pltpu.VMEM((tokens, 2 * STATE), dt),
-            pltpu.VMEM((tokens, 128), jnp.float32),
+            pltpu.VMEM((tokens, 128), f32),
             pltpu.VMEM((tokens, inner), dt),
-            pltpu.VMEM((GROUP, 32, inner), jnp.float32),
-            pltpu.VMEM((GROUP, 32, 2 * STATE), jnp.float32),
+            pltpu.VMEM((GROUP, 32, inner), f32),
+            pltpu.VMEM((GROUP, 32, 2 * STATE), f32),
+            pltpu.VMEM((3, held, inner), f32),
+            pltpu.VMEM((3, held, 2 * STATE), f32),
+            pltpu.VMEM((held, inner, STATE), dt),
+            pltpu.VMEM((model // 128, tokens, 128), dt),
+            dma(()), dma((requests - held,)), dma((fa.shape[1] // 256 + 3,)), dma((held,)),
+            dma((model // 256,)),
         ],
         compiler_params=pltpu.CompilerParams(vmem_limit_bytes=52 << 20),
         name="mixer",
-    )(prev_slot, cont, acc, hid, fa, fb, *vectors, prev, pex, peb)
+    )(tab, hid_c, hidden, fa, fb, *vectors, prev, pex, peb)
+
+
+def arrive_kernel(tab, xgot, egot, exf, ebf, nst_in, nst, nex, neb, xs, bs, ex, eb, new, n_sem):
+    f32, bf16 = jnp.float32, jnp.bfloat16
+    count, inner = new.shape[0], new.shape[1]
+    t_ids, _ = token_masks()
+    none = jnp.zeros((TOK, STATE), bf16)
+
+    def store(u):
+        return pltpu.make_async_copy(new.at[u], nst.at[tab[POS_O, u]], n_sem.at[u])
+
+    @pl.loop(0, count // GROUP)
+    def _(i):
+        for r in range(GROUP):
+            slot = tab[PICK_O, i * GROUP + r]
+            xs[r] = xgot[slot, :, :inner]
+            bs[r] = xgot[slot, :, inner:]
+        lhs = xs[...].reshape(TOK, inner).astype(f32).T.astype(bf16)
+        b_in = bs[...].reshape(TOK, STATE)
+        for pair in range(GROUP // 2):
+            cut = jnp.concatenate(
+                [
+                    jnp.where(t_ids // LEN == r, b_in, none)
+                    for r in (2 * pair, 2 * pair + 1)
+                ],
+                axis=1,
+            )
+            out = jnp.dot(lhs, cut, preferred_element_type=f32).astype(bf16)
+            for k in (0, 1):
+                u = i * GROUP + 2 * pair + k
+                new[u] = out[:, k * STATE : (k + 1) * STATE]
+                store(u).start()
+
+    ex[...] = exf[...]
+    eb[...] = ebf[...]
+
+    @pl.loop(0, count)
+    def _(u):
+        lines = egot[tab[PICK_O, u]].astype(f32)
+        at = pl.ds(tab[POS_O, u], 1)
+        for k in range(KCONV - 1):
+            ex[k, at, :] = jnp.concatenate(
+                [lines[2 * k : 2 * k + 1, :], lines[2 * k + 1 : 2 * k + 2, :128]], axis=1
+            )
+            eb[k, at, :] = lines[2 * k + 1 : 2 * k + 2, 128:]
+
+    nex[...] = ex[...].astype(bf16)
+    neb[...] = eb[...].astype(bf16)
+
+    @pl.loop(0, count)
+    def _(u):
+        store(u).wait()
+
+
+def arrive(tab, xgot, egot, exf, ebf, nst):
+    requests, inner, _ = nst.shape
+    count = requests // 2
+    dt, f32 = nst.dtype, jnp.float32
+    smem = pl.BlockSpec(memory_space=pltpu.SMEM)
+    vmem = pl.BlockSpec(memory_space=pltpu.VMEM)
+    hbm = pl.BlockSpec(memory_space=pltpu.HBM)
+    return pl.pallas_call(
+        arrive_kernel,
+        out_shape=(
+            jax.ShapeDtypeStruct(nst.shape, dt),
+            jax.ShapeDtypeStruct(exf.shape, dt),
+            jax.ShapeDtypeStruct(ebf.shape, dt),
+        ),
+        in_specs=[smem, vmem, vmem, vmem, vmem, hbm],
+        out_specs=(hbm, vmem, vmem),
+        scratch_shapes=[
+            pltpu.VMEM((GROUP, LEN, inner), dt),
+            pltpu.VMEM((GROUP, LEN, STATE), dt),
+            pltpu.VMEM(exf.shape, f32),
+            pltpu.VMEM(ebf.shape, f32),
+            pltpu.VMEM((count, inner, STATE), dt),
+            pltpu.SemaphoreType.DMA((count,)),
+        ],
+        input_output_aliases={5: 0},
+        compiler_params=pltpu.CompilerParams(vmem_limit_bytes=40 << 20),
+        name="arrive",
+    )(tab, xgot, egot, exf, ebf, nst)
 
 
 def per_device(
@@ -626,40 +969,31 @@
     holder, continued, owner, accepted,
 ):
     rows, cols = lax.axis_size("row"), lax.axis_size("col")
-    col_index = lax.axis_index("col")
-    requests = hidden.shape[0] // LEN
+    tokens, model = hidden.shape
+    requests = tokens // LEN
     heads = dt_bias.shape[0]
     inner = heads * HEAD_DIM
     held = prev_state.shape[0]
-    cap = 4 * ((requests // 4 + cols - 1) // cols)
-    home_key, send_from, pick, acc, cont, prev_slot, back_from = routing(
-        owner, accepted, continued, col_index, requests, cap
-    )
-    prev_slot = jnp.minimum(prev_slot, held - 1)
-    depth = w_zx.shape[0]
-    wa = w_zx.reshape(depth, heads, 2, HEAD_DIM).transpose(0, 2, 1, 3).reshape(depth, 2 * inner)
-    pad = jnp.zeros((depth, 128 - heads), w_dt.dtype)
-    wb = jnp.concatenate([w_out, w_bc, w_dt, pad], axis=1)
-    tokens, model = hidden.shape
-    hid, fa, fb = gather_all(
-        send_from, pick, hidden.reshape(requests, LEN, model), wa, wb, rows, cols, cap
-    )
-    hid = hid.reshape(tokens, model)
-
-    def line(v):
-        return jnp.pad(v, (0, 128 - v.shape[0]))[None, :]
-
+    cap = 2 * ((requests // 4 + cols - 1) // cols)
+    code = owner + 64 * (continued == 1).astype(jnp.int32) + 128 * accepted
+    tab = route(code.reshape(cols, requests), held)
+    hidden = hidden.reshape(requests, LEN, model)
+    hid_c, fa, fb = gather_all(tab, hidden, w_zx, w_out, w_bc, w_dt.T, rows, cols, cap, held)
     vectors = (
-        line(dt_bias), line(-jnp.exp(a_log)), jnp.repeat(d_skip, HEAD_DIM)[None, :],
+        dt_bias[None, :], a_log[None, :], d_skip[None, :],
         conv_x_w, conv_x_b[None, :], conv_bc_w, conv_bc_b[None, :], norm_gain[None, :],
     )
-    part, ss, new_state, new_edge_x, new_edge_bc = mixer(
-        prev_slot, cont, acc, hid, fa, fb, vectors,
-        prev_state.reshape(held, inner, STATE), prev_edge_x, prev_edge_bc,
+    part, ss, xmsg, emsg, states, exf, ebf = mixer(
+        tab, hid_c, hidden, fa, fb, vectors, prev_state.reshape(held, inner, STATE),
+        prev_edge_x.transpose(1, 0, 2), prev_edge_bc.transpose(1, 0, 2), cols * cap,
     )
-    mixed = send_home(back_from, home_key, part, ss, rows, cols, cap)
+    mixed, xgot, egot = send_home(tab, part, ss, xmsg, emsg, rows, cols, cap)
+    states, new_x, new_bc = arrive(tab, xgot, egot, exf, ebf, states)
     return (
-        mixed.reshape(tokens, model // rows), new_state.reshape(requests, heads, HEAD_DIM, STATE), new_edge_x, new_edge_bc,
+        mixed.reshape(tokens, model // rows),
+        states.reshape(requests, heads, HEAD_DIM, STATE),
+        new_x.transpose(1, 0, 2),
+        new_bc.transpose(1, 0, 2),
     )
 
 

time: 159 us -> 142 us (0.89)
  Pallas kernels: 132 us -> 117 us
  other arithmetic: 7.77 us -> 0.74 us
  local copies, waits for them, and re-layouts: 17.2 us -> 21.9 us
    pallas_call x3 -> x5, Pallas kernels: 132 us -> 117 us  [the longest x1 45.2 us: send_home(): pl.pallas_call(body, out_shape=(jax.ShapeDtypeStruct((requests, LEN, piec...]
    unnamed x26 -> x45, local copies, waits for them, and re-layouts: 12.6 us -> 21.2 us
    reduce_sum x8 -> x0, other arithmetic: 3.97 us -> none  [the longest x1 2.66 us: picked(): return jnp.sum(jnp.where(match, values[None], 0), axis=(1, 2))]
    broadcast_in_dim x5 -> x0, local copies, waits for them, and re-layouts: 2.25 us -> none  [the longest x2 0.85 us: picked(): return jnp.sum(jnp.where(match, values[None], 0), axis=(1, 2))]
where the time goes in v3:
time: 142 us; the launch traced here: 141 us
  Pallas kernels  117 us (82%)
  local copies, waits for them, and re-layouts  21.9 us (15%)
    pallas_call x1, Pallas kernels, send_home(): pl.pallas_call(body, out_shape=(jax.ShapeDtypeStruct((requests, LEN, piec...  45.2 us
    pallas_call x1, Pallas kernels, gather_all(): pl.pallas_call(body, out_shape=(jax.ShapeDtypeStruct((held, LEN, model),...  41.2 us
    pallas_call x1, Pallas kernels, mixer(): pl.pallas_call(body, out_shape=(jax.ShapeDtypeStruct((model // 128, token...  25.3 us
    unnamed x45, local copies, waits for them, and re-layouts  21.2 us
    pallas_call x1, Pallas kernels, arrive(): pl.pallas_call(arrive_kernel, out_shape=(jax.ShapeDtypeStruct(nst.shape,...  3.99 us

profile of v3, /device:TPU:1, one launch (start us, length us, event | category | flops | bytes accessed | tf_op | source)
XLA Modules:
  0.0 140.7 jit_solution(16854125164094210683)
XLA Ops:
  0.6 0.7 multiply_add_fusion
  1.4 0.7 reshape.23.refs_0_
  2.1 1.8 %route.1.refs_0_.tab = s32[16,128]{1,0:T(8,128)} custom-call(s32[32,48]{1,0:T(8,128)} %reshape.23.refs_0_), custom_call_target="tpu_custom_call" | custom-call | tf_op jit(solution)/shard_map/route/pallas_call | solution.py:122
  3.8 0.0 copy-start
  3.8 1.7 %copy-done = bf16[768,1536]{1,0:T(8,128)(2,1)S(1)} copy-done((bf16[768,1536]{1,0:T(8,128)(2,1)S(1)}, bf16[768,1536]{1,0:T(8,128)(2,1)}, u32[]{:S(2)}) %copy-start) | copy-done | bytes 2359320
  5.5 0.0 copy-start.6
  5.5 0.7 copy-done.6
  6.2 0.0 copy-start.8
  6.2 0.9 copy-done.8
  7.1 0.0 copy-start.10
  7.1 0.8 copy-done.10
  7.9 0.0 copy-start.12
  7.9 0.7 copy-done.12
  8.6 0.0 copy-start.17
  8.6 0.7 copy-done.17
  9.3 41.2 %gather_all.1 = (bf16[24,16,1536]{2,1,0:T(8,128)(2,1)S(1)}, bf16[1536,1024]{1,0:T(8,128)(2,1)S(1)}, bf16[1536,896]{1,0:T(8,128)(2,1)S(1)}) custom-call(s32[16,128]{1,0:T(8,128)S(1)} %copy-done.6, bf16[48,16,1536]{2,1,0:T(8,128)(2,1)S(1)} %bitcast.16, bf16[48,1024]{1,0:T(8,128)(2,1)S(1)} %copy-done.8, bf16[48,512]{1,0:T(8,128)(2,1)S(1)} %copy-done.10, ...), custom_call_target="tpu_custom_call" | custom-call | tf_op jit(solution)/shard_map/gather_all/pallas_call | solution.py:367
  50.5 0.0 copy-start.1
  50.5 1.6 %copy-done.1 = bf16[1536,1024]{1,0:T(8,128)(2,1)} copy-done((bf16[1536,1024]{1,0:T(8,128)(2,1)}, bf16[1536,1024]{1,0:T(8,128)(2,1)S(1)}, u32[]{:S(2)}) %copy-start.1) | copy-done | bytes 3145752
  52.1 0.0 copy-start.2
  52.1 1.5 %copy-done.2 = bf16[1536,896]{1,0:T(8,128)(2,1)} copy-done((bf16[1536,896]{1,0:T(8,128)(2,1)}, bf16[1536,896]{1,0:T(8,128)(2,1)S(1)}, u32[]{:S(2)}) %copy-start.2) | copy-done | bytes 2752536
  53.7 0.0 copy-start.5
  53.7 1.0 copy-done.5
  54.7 0.0 copy-start.7
  54.7 0.7 copy-done.7
  55.4 0.0 copy-start.9
  55.4 0.9 copy-done.9
  56.3 0.0 copy-start.11
  56.3 0.8 copy-done.11
  57.0 0.0 copy-start.13
  57.0 0.7 copy-done.13
  57.7 0.0 copy-start.14
  57.7 0.7 copy-done.14
  58.4 0.0 copy-start.15
  58.4 0.7 copy-done.15
  59.1 0.0 copy-start.16
  59.1 0.7 copy-done.16
  59.8 0.0 copy-start.18
  59.8 0.7 copy-done.18
  60.5 0.0 copy-start.19
  60.5 0.7 copy-done.19
  61.1 0.0 copy-start.20
  61.1 0.7 copy-done.20
  61.8 0.0 copy-start.21
  61.8 0.7 copy-done.21
  62.4 25.3 %mixer.1 = (bf16[12,768,128]{2,1,0:T(8,128)(2,1)}, f32[8,128]{1,0:T(8,128)S(1)}, bf16[64,16,640]{2,1,0:T(8,128)(2,1)}, bf16[64,8,384]{2,1,0:T(8,128)(2,1)S(1)}, ...) custom-call(s32[16,128]{1,0:T(8,128)S(1)} %copy-done.7, ...), custom_call_target="tpu_custom_call" | custom-call | tf_op jit(solution)/shard_map/mixer/pallas_call | solution.py:847
  87.7 0.0 copy-start.3
  87.7 1.7 %copy-done.3 = bf16[12,768,128]{2,1,0:T(8,128)(2,1)S(1)} copy-done((bf16[12,768,128]{2,1,0:T(8,128)(2,1)S(1)}, bf16[12,768,128]{2,1,0:T(8,128)(2,1)}, u32[]{:S(2)}) %copy-start.3) | copy-done | bytes 2359320
  89.4 0.0 copy-start.4
  89.4 1.3 copy-done.4
  90.7 45.2 %send_home.1 = (bf16[48,16,384]{2,1,0:T(8,128)(2,1)S(1)}, bf16[64,16,640]{2,1,0:T(8,128)(2,1)S(1)}, bf16[64,8,384]{2,1,0:T(8,128)(2,1)S(1)}) custom-call(s32[16,128]{1,0:T(8,128)S(1)} %copy-done.7, bf16[12,768,128]{2,1,0:T(8,128)(2,1)S(1)} %copy-done.3, f32[8,128]{1,0:T(8,128)S(1)} %get-tuple-element.24.refs_2_, bf16[64,16,640]{2,1,0:T(8,128)(2,1)S(1)} %copy-done.4, ...), custom_call_target="tpu_custom_call" | custom-call | tf_op jit(solution)/shard_map/send_home/pallas_call | solution.py:547
  135.9 4.0 %arrive.1 = (bf16[48,512,128]{2,1,0:T(8,128)(2,1)}, bf16[3,48,512]{2,1,0:T(8,128)(2,1)}, bf16[3,48,256]{2,1,0:T(8,128)(2,1)}) custom-call(s32[16,128]{1,0:T(8,128)S(1)} %copy-done.7, bf16[64,16,640]{2,1,0:T(8,128)(2,1)S(1)} %get-tuple-element.28.xgot, bf16[64,8,384]{2,1,0:T(8,128)(2,1)S(1)} %get-tuple-element.29.egot, ...), custom_call_target="tpu_custom_call", output_to_operand_aliasing={{0}: (5, {})} | custom-call | tf_op jit(solution)/shard_map/arrive/pallas_call | solution.py:943
  139.9 0.8 copy.26
Async XLA Ops:
  3.8 1.7 %copy-start = (bf16[768,1536]{1,0:T(8,128)(2,1)S(1)}, bf16[768,1536]{1,0:T(8,128)(2,1)}, u32[]{:S(2)}) copy-start(bf16[768,1536]{1,0:T(8,128)(2,1)} %param.20) | copy-start | bytes 7077892
  5.5 0.7 copy-start.6
  6.2 0.9 copy-start.8
  7.1 0.8 copy-start.10
  7.9 0.7 copy-start.12
  8.6 0.7 copy-start.17
  50.5 1.6 %copy-start.1 = (bf16[1536,1024]{1,0:T(8,128)(2,1)}, bf16[1536,1024]{1,0:T(8,128)(2,1)S(1)}, u32[]{:S(2)}) copy-start(bf16[1536,1024]{1,0:T(8,128)(2,1)S(1)} %get-tuple-element.21.refs_3_) | copy-start | bytes 9437188
  52.1 1.5 %copy-start.2 = (bf16[1536,896]{1,0:T(8,128)(2,1)}, bf16[1536,896]{1,0:T(8,128)(2,1)S(1)}, u32[]{:S(2)}) copy-start(bf16[1536,896]{1,0:T(8,128)(2,1)S(1)} %get-tuple-element.22.refs_4_) | copy-start | bytes 8257540
  53.7 1.0 copy-start.5
  54.7 0.7 copy-start.7
  55.4 0.9 copy-start.9
  56.3 0.8 copy-start.11
  57.0 0.7 copy-start.13
  57.7 0.7 copy-start.14
  58.4 0.7 copy-start.15
  59.1 0.7 copy-start.16
  59.8 0.7 copy-start.18
  60.5 0.7 copy-start.19
  61.1 0.7 copy-start.20
  61.8 0.7 copy-start.21
  87.7 1.7 %copy-start.3 = (bf16[12,768,128]{2,1,0:T(8,128)(2,1)S(1)}, bf16[12,768,128]{2,1,0:T(8,128)(2,1)}, u32[]{:S(2)}) copy-start(bf16[12,768,128]{2,1,0:T(8,128)(2,1)} %get-tuple-element.23.refs_1_) | copy-start | bytes 7077892
  89.4 1.3 copy-start.4

commit v4 on v3

--- a/solution.py
+++ b/solution.py
@@ -122,6 +122,7 @@
     return pl.pallas_call(
         body, out_shape=jax.ShapeDtypeStruct((16, 128), jnp.int32),
         in_specs=[vmem], out_specs=vmem, name="route",
+        compiler_params=pltpu.CompilerParams(vmem_limit_bytes=60 << 20),
     )(code)
 
 
@@ -147,8 +148,8 @@
 
 
 def gather_kernel(
-    rows, cols, cap, tab, hidden, wa, w_out, w_bc, w_dt, hid_full, fa, fb,
-    wb, sl, packed, got, own, loc, a2a_s, a2a_r, was, wbs, war, wbr, y_s, y_r,
+    rows, cols, cap, tab_in, hidden, wa, w_out, w_bc, w_dt_in, hid_full, fa, fb,
+    tab, w_dt, wb, sl, packed, got, own, loc, a2a_s, a2a_r, was, wbs, war, wbr, y_s, y_r,
 ):
     row, me = lax.axis_index("row"), lax.axis_index("col")
     barrier = greet(row, me, rows, cols)
@@ -166,9 +167,17 @@
     load.start()
     inner = w_out.shape[1]
     states = w_bc.shape[1]
-    heads = w_dt.shape[0]
-    wb[:, :inner] = w_out[...]
-    wb[:, inner : inner + states] = w_bc[...]
+    heads = w_dt_in.shape[0]
+    loads = (
+        pltpu.make_async_copy(tab_in, tab, loc.at[5]),
+        pltpu.make_async_copy(w_dt_in, w_dt, loc.at[6]),
+        pltpu.make_async_copy(w_out, wb.at[:, pl.ds(0, inner)], loc.at[7]),
+        pltpu.make_async_copy(w_bc, wb.at[:, pl.ds(inner, states)], loc.at[8]),
+    )
+    for copy in loads:
+        copy.start()
+    for copy in loads:
+        copy.wait()
     square = jnp.concatenate([w_dt[...].astype(jnp.float32), jnp.zeros((heads, 128 - depth), jnp.float32)], axis=1)
     square = jnp.concatenate([square, jnp.zeros((128 - heads, 128), jnp.float32)], axis=0).T
     wb[:, inner + states :] = square[:depth, :].astype(wb.dtype)
@@ -354,9 +363,7 @@
     requests, _, model = hidden.shape
     width = model // rows
     dt = hidden.dtype
-    smem = pl.BlockSpec(memory_space=pltpu.SMEM)
     hbm = pl.BlockSpec(memory_space=pltpu.HBM)
-    vmem = pl.BlockSpec(memory_space=pltpu.VMEM)
     dma = pltpu.SemaphoreType.DMA
     depth = wa.shape[0]
     rest = w_out.shape[1] + w_bc.shape[1] + 128
@@ -371,54 +378,87 @@
             jax.ShapeDtypeStruct((depth * cols, wa.shape[1]), dt),
             jax.ShapeDtypeStruct((depth * cols, rest), dt),
         ),
-        in_specs=[smem, hbm, vmem, vmem, vmem, vmem],
+        in_specs=[hbm] * 6,
         out_specs=(hbm, hbm, hbm),
         scratch_shapes=[
+            pltpu.SMEM(tab.shape, jnp.int32),
+            pltpu.VMEM(w_dt.shape, dt),
             pltpu.VMEM((depth, rest), dt),
             pltpu.VMEM((requests, LEN, width), dt),
             pltpu.VMEM((cols * cap, LEN, width), dt),
             pltpu.VMEM((cols * cap, LEN, width), dt),
             pltpu.VMEM((held, LEN, width), dt),
-            dma((5,)), dma((cols,)), dma((cols,)),
+            dma((9,)), dma((cols,)), dma((cols,)),
             dma((48,)), dma((48,)), dma((cols,)), dma((cols,)),
             dma((6,)), dma((rows, 2)),
         ],
         compiler_params=pltpu.CompilerParams(
-            collective_id=0, has_side_effects=True, vmem_limit_bytes=32 << 20
+            collective_id=0, has_side_effects=True, vmem_limit_bytes=60 << 20
         ),
         name="gather_all",
     )(tab, hidden, wa, w_out, w_bc, w_dt)
 
 
 def return_kernel(
-    rows, cols, cap, tab, part, ss, xmsg, emsg, mixed, xgot, egot,
-    mine, came, ss_in, scale, mix0, mix1, mix2, packed, got0, got1, got2,
-    loc, ss_s, ss_r, y_s, y_r, a2a_s, a2a_r, x_s, x_r, e_s, e_r,
+    rows, cols, cap, tab_in, gg_in, ss_from, fb, xmsg, emsg, mixed, xgot, egot,
+    tab, gg, wo, ss, part, came, ss_in, scale, mix0, mix1, mix2, packed, got0, got1, got2,
+    ld, loc, ss_s, ss_r, y_s, y_r, a2a_s, a2a_r, x_s, x_r, e_s, e_r,
 ):
     row, me = lax.axis_index("row"), lax.axis_index("col")
     barrier = greet(row, me, rows, cols)
     pieces = part.shape[0] // rows
     tokens = part.shape[1]
-    keep = pltpu.make_async_copy(part.at[pl.ds(row * pieces, pieces)], mine, loc.at[0])
-    keep.start()
+    inner = gg.shape[1]
+    width = pieces * 128
+    loads = (
+        pltpu.make_async_copy(gg_in, gg, ld.at[0]),
+        pltpu.make_async_copy(fb.at[:, pl.ds(0, inner)], wo, ld.at[1]),
+        pltpu.make_async_copy(ss_from, ss, ld.at[2]),
+        pltpu.make_async_copy(tab_in, tab, ld.at[3]),
+    )
+    for copy in loads:
+        copy.start()
+    for copy in loads:
+        copy.wait()
+    order = (1, 3, 2)
+
+    def block(peer, j, count):
+        at = pl.ds(pl.multiple_of(peer * width + j * 128, 128), count * 128)
+        out = lax.dot_general(
+            gg[...], wo[at, :], (((1,), (1,)), ((), ())), preferred_element_type=jnp.float32
+        ).astype(part.dtype)
+        for k in range(count):
+            part[peer * pieces + j + k] = out[:, k * 128 : (k + 1) * 128]
+
+    def send_block(peer, j, d):
+        pltpu.make_async_remote_copy(
+            part.at[peer * pieces + j], came.at[row, j], y_s.at[j, d], y_r.at[row, j],
+            device_id=(peer, me), device_id_type=MESH,
+        ).start()
+
+    def first(d, carry):
+        peer = (row + d) % rows
+        block(peer, 0, 1)
+        send_block(peer, 0, d)
+        return carry
+
+    def later(d, carry):
+        peer = (row + d) % rows
+        block(peer, 1, pieces - 1)
+        for j in range(1, pieces):
+            send_block(peer, j, d)
+        return carry
+
+    def piece(ref, c):
+        return ref.at[pl.ds(c * cap, cap)]
+
     pl.semaphore_wait(barrier, cols - 1 + rows - 1)
-    order = (1, 3, 2)
     for k, d in enumerate(order):
-        peer = (row + d) % rows
         pltpu.make_async_remote_copy(
             ss, ss_in.at[row], ss_s.at[k], ss_r.at[row],
-            device_id=(peer, me), device_id_type=MESH,
+            device_id=((row + d) % rows, me), device_id_type=MESH,
         ).start()
-    for j in range(pieces):
-        for k, d in enumerate(order):
-            peer = (row + d) % rows
-            pltpu.make_async_remote_copy(
-                part.at[peer * pieces + j], came.at[row, j], y_s.at[j, k], y_r.at[row, j],
-                device_id=(peer, me), device_id_type=MESH,
-            ).start()
-    def piece(ref, c):
-        return ref.at[pl.ds(c * cap, cap)]
-
+    lax.fori_loop(1, rows, first, 0)
     def push_factors(d, carry):
         peer = (me + d) % cols
         for src, dst, ss_, rs_ in ((xmsg, xgot, x_s, x_r), (emsg, egot, e_s, e_r)):
@@ -433,6 +473,9 @@
     keep_e = pltpu.make_async_copy(piece(emsg, me), piece(egot, me), loc.at[5])
     keep_x.start()
     keep_e.start()
+    lax.fori_loop(1, rows, later, 0)
+    block(row, 0, 1)
+    block(row, 1, pieces - 1)
     total = ss[...]
     for d in order:
         peer = (row + d) % rows
@@ -442,7 +485,6 @@
     for i in range(tokens // TOK):
         line = jnp.broadcast_to(factor[i : i + 1, :], (TOK, TOK))
         scale[pl.ds(i * TOK, TOK), :] = line.T
-    keep.wait()
     gots = (got0, got1, got2)
 
     mixes = (mix0, mix1, mix2)
@@ -454,7 +496,7 @@
 
         def add(i, carry):
             at = pl.ds(pl.multiple_of(i * TOK, TOK), TOK)
-            value = mine[j, at, :].astype(jnp.float32)
+            value = part[row * pieces + j, at, :].astype(jnp.float32)
             for d in order:
                 value = value + came[(row + d) % rows, j, at, :].astype(jnp.float32)
             value = (value * scale[at, :]).astype(mix.dtype)
@@ -502,7 +544,7 @@
     for k in range(3):
         pltpu.make_async_copy(ss, ss, ss_s.at[k]).wait()
         for j in range(pieces):
-            pltpu.make_async_copy(mine.at[j], mine.at[j], y_s.at[j, k]).wait()
+            pltpu.make_async_copy(part.at[j], part.at[j], y_s.at[j, k + 1]).wait()
     for j in range(pieces):
 
         def gone(d, carry):
@@ -528,16 +570,16 @@
     lax.fori_loop(1, cols, factors, 0)
 
 
-def send_home(tab, part, ss, xmsg, emsg, rows, cols, cap):
-    pieces = part.shape[0] // rows
-    tokens = part.shape[1]
-    smem = pl.BlockSpec(memory_space=pltpu.SMEM)
+def send_home(tab, gg, ss, fb, xmsg, emsg, rows, cols, cap):
+    blocks = fb.shape[0] // 128
+    pieces = blocks // rows
+    tokens, inner = gg.shape
     hbm = pl.BlockSpec(memory_space=pltpu.HBM)
     vmem = pl.BlockSpec(memory_space=pltpu.VMEM)
     dma = pltpu.SemaphoreType.DMA
     slots = cols * cap
     requests = tokens // LEN
-    dt = part.dtype
+    dt = gg.dtype
 
     def body(*refs):
         return_kernel(rows, cols, cap, *refs)
@@ -551,25 +593,29 @@
             jax.ShapeDtypeStruct(xmsg.shape, dt),
             jax.ShapeDtypeStruct(emsg.shape, dt),
         ),
-        in_specs=[smem, hbm, vmem, hbm, hbm],
+        in_specs=[hbm] * 6,
         out_specs=(vmem, hbm, hbm),
         scratch_shapes=[
-            pltpu.VMEM((pieces, tokens, 128), dt),
+            pltpu.SMEM(tab.shape, jnp.int32),
+            pltpu.VMEM((tokens, inner), dt),
+            pltpu.VMEM((fb.shape[0], inner), dt),
+            pltpu.VMEM(ss.shape, jnp.float32),
+            pltpu.VMEM((blocks, tokens, 128), dt),
             pltpu.VMEM((rows, pieces, tokens, 128), dt),
             pltpu.VMEM((rows,) + ss.shape, jnp.float32),
             pltpu.VMEM((tokens, 128), jnp.float32),
             mix, mix, mix,
             pltpu.VMEM((pieces, slots, LEN, 128), dt),
             got, got, got,
-            dma((3 + pieces,)), dma((3,)), dma((rows,)),
-            dma((pieces, 3)), dma((rows, pieces)), dma((pieces, cols)), dma((pieces, cols)),
+            dma((4,)), dma((3 + pieces,)), dma((3,)), dma((rows,)),
+            dma((pieces, rows)), dma((rows, pieces)), dma((pieces, cols)), dma((pieces, cols)),
             dma((cols,)), dma((cols,)), dma((cols,)), dma((cols,)),
         ],
         compiler_params=pltpu.CompilerParams(
-            collective_id=1, has_side_effects=True, vmem_limit_bytes=32 << 20
+            collective_id=1, has_side_effects=True, vmem_limit_bytes=60 << 20
         ),
         name="send_home",
-    )(tab, part, ss, xmsg, emsg)
+    )(tab, gg, ss, fb, xmsg, emsg)
 
 
 def silu(v):
@@ -583,11 +629,16 @@
 
 
 def mixer_kernel(
-    held, tab, hid_c, hidden, fa, fb, dtb, alog, skip, cxw, cxb, cbw, cbb, gain, prev, pex, peb,
-    part, ss, xmsg, emsg, nst, nex, neb,
-    hid, wa, wb, old, gate, xin, bc, dts, gg, cx, cb, pexf, pebf, new, outs,
-    h_sem, o_sem, w_sem, n_sem, p_sem,
+    held, tab_in, hid_c, hidden, fa, fb, *refs,
 ):
+    sources, refs = refs[:8], refs[8:]
+    prev, pex_in, peb_in, gg, ss, xmsg, emsg, nst, nex, neb, tab, *refs = refs
+    params, refs = refs[:8], refs[8:]
+    dtb, alog, skip, cxw, cxb, cbw, cbb, gain = params
+    (
+        pex, peb, hid, wa, wb, old, gate, xin, bc, dts, cx, cb, pexf, pebf, new,
+        h_sem, o_sem, w_sem, n_sem, v_sem,
+    ) = refs
     f32, bf16 = jnp.float32, jnp.bfloat16
     inner = gain.shape[1]
     requests = hid.shape[0]
@@ -598,6 +649,12 @@
 
     load_h = pltpu.make_async_copy(hid_c, hid.at[pl.ds(0, held)], h_sem)
     load_h.start()
+    small = list(zip(sources + (pex_in, peb_in, tab_in), list(params) + [pex, peb, tab]))
+    small = [pltpu.make_async_copy(a, b, v_sem.at[k]) for k, (a, b) in enumerate(small)]
+    small[-1].start()
+    for copy in small[:-1]:
+        copy.start()
+    small[-1].wait()
 
     def wa_load(n):
         at = pl.ds(n * 256, 256)
@@ -614,14 +671,13 @@
 
     for n in range(1, blocks):
         wa_load(n).start()
-    late = pl.ds(inner, wb.shape[1] - inner)
-    early = pl.ds(0, inner)
-    load_bc = pltpu.make_async_copy(fb.at[:, late], wb.at[:, late], w_sem.at[blocks])
-    load_out = pltpu.make_async_copy(fb.at[:, early], wb.at[:, early], w_sem.at[blocks + 1])
-    load_old = pltpu.make_async_copy(prev, old, w_sem.at[blocks + 2])
+    late = pl.ds(inner, wb.shape[1])
+    load_bc = pltpu.make_async_copy(fb.at[:, late], wb, w_sem.at[blocks])
+    load_old = pltpu.make_async_copy(prev, old, w_sem.at[blocks + 1])
     load_bc.start()
     load_old.start()
-    load_out.start()
+    for copy in small[:-1]:
+        copy.wait()
     pexf[...] = pex[...].astype(f32)
     pebf[...] = peb[...].astype(f32)
 
@@ -661,7 +717,7 @@
         gate[:, at] = jnp.where(left, z0, pltpu.roll(z1, HEAD_DIM, 1)).astype(bf16)
         xin[:, at] = jnp.where(left, pltpu.roll(z0, HEAD_DIM, 1), z1).astype(bf16)
     load_bc.wait()
-    z = jnp.dot(hid[...].reshape(tokens, model), wb[:, inner:], preferred_element_type=f32)
+    z = jnp.dot(hid[...].reshape(tokens, model), wb[...], preferred_element_type=f32)
     bc[...] = z[:, : 2 * STATE].astype(bf16)
     dts[...] = z[:, 2 * STATE :]
     load_old.wait()
@@ -803,26 +859,6 @@
     def _(i):
         group(i, False)
 
-    load_out.wait()
-
-    def put(q):
-        at = pl.ds(2 * q, 2)
-        return pltpu.make_async_copy(outs.at[at], part.at[at], p_sem.at[q])
-
-    @pl.loop(0, part.shape[0] // 2)
-    def _(q):
-        at = pl.ds(pl.multiple_of(q * 256, 256), 256)
-        out = lax.dot_general(
-            gg[...], wb[at, :inner], (((1,), (1,)), ((), ())), preferred_element_type=f32
-        ).astype(bf16)
-        outs[2 * q] = out[:, :128]
-        outs[2 * q + 1] = out[:, 128:]
-        put(q).start()
-
-    @pl.loop(0, part.shape[0] // 2)
-    def _(q):
-        put(q).wait()
-
     @pl.loop(0, held)
     def _(s):
         store(s).wait()
@@ -836,7 +872,6 @@
     heads = inner // HEAD_DIM
     dt = hidden.dtype
     f32 = jnp.float32
-    smem = pl.BlockSpec(memory_space=pltpu.SMEM)
     vmem = pl.BlockSpec(memory_space=pltpu.VMEM)
     hbm = pl.BlockSpec(memory_space=pltpu.HBM)
     dma = pltpu.SemaphoreType.DMA
@@ -847,7 +882,7 @@
     return pl.pallas_call(
         body,
         out_shape=(
-            jax.ShapeDtypeStruct((model // 128, tokens, 128), dt),
+            jax.ShapeDtypeStruct((tokens, inner), dt),
             jax.ShapeDtypeStruct((8, 128), f32),
             jax.ShapeDtypeStruct((slots, LEN, inner + STATE), dt),
             jax.ShapeDtypeStruct((slots, 8, 384), dt),
@@ -855,35 +890,50 @@
             jax.ShapeDtypeStruct((3, requests, inner), f32),
             jax.ShapeDtypeStruct((3, requests, 2 * STATE), f32),
         ),
-        in_specs=[smem] + [hbm] * 4 + [vmem] * len(vectors) + [hbm, vmem, vmem],
-        out_specs=(hbm, vmem, vmem, vmem, hbm, vmem, vmem),
+        in_specs=[hbm] * (8 + len(vectors)),
+        out_specs=(vmem, vmem, vmem, vmem, hbm, vmem, vmem),
         scratch_shapes=[
+            pltpu.SMEM(tab.shape, jnp.int32),
+            *[pltpu.VMEM(v.shape, v.dtype) for v in vectors],
+            pltpu.VMEM(pex.shape, dt),
+            pltpu.VMEM(peb.shape, dt),
             pltpu.VMEM((requests, LEN, model), dt),
             pltpu.VMEM(fa.shape, dt),
-            pltpu.VMEM(fb.shape, dt),
+            pltpu.VMEM((fb.shape[0], fb.shape[1] - inner), dt),
             pltpu.VMEM((held, inner, STATE), dt),
             pltpu.VMEM((tokens, inner), dt),
             pltpu.VMEM((tokens, inner), dt),
             pltpu.VMEM((tokens, 2 * STATE), dt),
             pltpu.VMEM((tokens, 128), f32),
-            pltpu.VMEM((tokens, inner), dt),
             pltpu.VMEM((GROUP, 32, inner), f32),
             pltpu.VMEM((GROUP, 32, 2 * STATE), f32),
             pltpu.VMEM((3, held, inner), f32),
             pltpu.VMEM((3, held, 2 * STATE), f32),
             pltpu.VMEM((held, inner, STATE), dt),
-            pltpu.VMEM((model // 128, tokens, 128), dt),
-            dma(()), dma((requests - held,)), dma((fa.shape[1] // 256 + 3,)), dma((held,)),
-            dma((model // 256,)),
+            dma(()), dma((requests - held,)), dma((fa.shape[1] // 256 + 2,)), dma((held,)),
+            dma((len(vectors) + 3,)),
         ],
-        compiler_params=pltpu.CompilerParams(vmem_limit_bytes=52 << 20),
+        compiler_params=pltpu.CompilerParams(vmem_limit_bytes=60 << 20),
         name="mixer",
     )(tab, hid_c, hidden, fa, fb, *vectors, prev, pex, peb)
 
 
-def arrive_kernel(tab, xgot, egot, exf, ebf, nst_in, nst, nex, neb, xs, bs, ex, eb, new, n_sem):
+def arrive_kernel(
+    tab_in, xgot_in, egot_in, exf, ebf, nst_in, nst, nex, neb,
+    tab, xgot, egot, xs, bs, ex, eb, new, n_sem, l_sem,
+):
     f32, bf16 = jnp.float32, jnp.bfloat16
     count, inner = new.shape[0], new.shape[1]
+    loads = [
+        pltpu.make_async_copy(a, b, l_sem.at[k])
+        for k, (a, b) in enumerate(
+            ((tab_in, tab), (xgot_in, xgot), (egot_in, egot), (exf, ex), (ebf, eb))
+        )
+    ]
+    for copy in loads:
+        copy.start()
+    loads[0].wait()
+    loads[1].wait()
     t_ids, _ = token_masks()
     none = jnp.zeros((TOK, STATE), bf16)
 
@@ -912,8 +962,8 @@
                 new[u] = out[:, k * STATE : (k + 1) * STATE]
                 store(u).start()
 
-    ex[...] = exf[...]
-    eb[...] = ebf[...]
+    for copy in loads[2:]:
+        copy.wait()
 
     @pl.loop(0, count)
     def _(u):
@@ -937,7 +987,6 @@
     requests, inner, _ = nst.shape
     count = requests // 2
     dt, f32 = nst.dtype, jnp.float32
-    smem = pl.BlockSpec(memory_space=pltpu.SMEM)
     vmem = pl.BlockSpec(memory_space=pltpu.VMEM)
     hbm = pl.BlockSpec(memory_space=pltpu.HBM)
     return pl.pallas_call(
@@ -947,18 +996,22 @@
             jax.ShapeDtypeStruct(exf.shape, dt),
             jax.ShapeDtypeStruct(ebf.shape, dt),
         ),
-        in_specs=[smem, vmem, vmem, vmem, vmem, hbm],
+        in_specs=[hbm] * 6,
         out_specs=(hbm, vmem, vmem),
         scratch_shapes=[
+            pltpu.SMEM(tab.shape, jnp.int32),
+            pltpu.VMEM(xgot.shape, dt),
+            pltpu.VMEM(egot.shape, dt),
             pltpu.VMEM((GROUP, LEN, inner), dt),
             pltpu.VMEM((GROUP, LEN, STATE), dt),
             pltpu.VMEM(exf.shape, f32),
             pltpu.VMEM(ebf.shape, f32),
             pltpu.VMEM((count, inner, STATE), dt),
             pltpu.SemaphoreType.DMA((count,)),
+            pltpu.SemaphoreType.DMA((5,)),
         ],
         input_output_aliases={5: 0},
-        compiler_params=pltpu.CompilerParams(vmem_limit_bytes=40 << 20),
+        compiler_params=pltpu.CompilerParams(vmem_limit_bytes=60 << 20),
         name="arrive",
     )(tab, xgot, egot, exf, ebf, nst)
 
@@ -983,11 +1036,11 @@
         dt_bias[None, :], a_log[None, :], d_skip[None, :],
         conv_x_w, conv_x_b[None, :], conv_bc_w, conv_bc_b[None, :], norm_gain[None, :],
     )
-    part, ss, xmsg, emsg, states, exf, ebf = mixer(
+    gg, ss, xmsg, emsg, states, exf, ebf = mixer(
         tab, hid_c, hidden, fa, fb, vectors, prev_state.reshape(held, inner, STATE),
         prev_edge_x.transpose(1, 0, 2), prev_edge_bc.transpose(1, 0, 2), cols * cap,
     )
-    mixed, xgot, egot = send_home(tab, part, ss, xmsg, emsg, rows, cols, cap)
+    mixed, xgot, egot = send_home(tab, gg, ss, fb, xmsg, emsg, rows, cols, cap)
     states, new_x, new_bc = arrive(tab, xgot, egot, exf, ebf, states)
     return (
         mixed.reshape(tokens, model // rows),

time: 142 us -> 120 us (0.85)
  local copies, waits for them, and re-layouts: 21.9 us -> 1.5 us
    unnamed x45 -> x3, local copies, waits for them, and re-layouts: 21.2 us -> 0.82 us
    pallas_call x1, Pallas kernels: 25.3 us -> 22.5 us  [mixer(): pl.pallas_call(body, out_shape=(jax.ShapeDtypeStruct((tokens, inner), dt)...]
    pallas_call x1, Pallas kernels: 45.2 us -> 46.9 us  [send_home(): pl.pallas_call(body, out_shape=(jax.ShapeDtypeStruct((requests, LEN, piec...]
where the time goes in v4:
time: 120 us
  Pallas kernels  117 us (98%)
  local copies, waits for them, and re-layouts  1.5 us (1%)
    pallas_call x1, Pallas kernels, send_home(): pl.pallas_call(body, out_shape=(jax.ShapeDtypeStruct((requests, LEN, piec...  46.9 us
    pallas_call x1, Pallas kernels, gather_all(): pl.pallas_call(body, out_shape=(jax.ShapeDtypeStruct((held, LEN, model),...  41 us
    pallas_call x1, Pallas kernels, mixer(): pl.pallas_call(body, out_shape=(jax.ShapeDtypeStruct((tokens, inner), dt)...  22.5 us
    pallas_call x1, Pallas kernels, arrive(): pl.pallas_call(arrive_kernel, out_shape=(jax.ShapeDtypeStruct(nst.shape,...  4.78 us

profile of v4, /device:TPU:1, one launch (start us, length us, event | category | flops | bytes accessed | tf_op | source)
XLA Modules:
  0.0 119.9 jit_solution(5875685797907535564)
XLA Ops:
  0.6 0.7 multiply_add_fusion
  1.4 0.7 reshape.23.refs_0_
  2.1 1.8 %route.1.refs_0_.tab_in = s32[16,128]{1,0:T(8,128)} custom-call(s32[32,48]{1,0:T(8,128)} %reshape.23.refs_0_), custom_call_target="tpu_custom_call" | custom-call | tf_op jit(solution)/shard_map/route/pallas_call | solution.py:122
  3.8 41.0 %gather_all.1 = (bf16[24,16,1536]{2,1,0:T(8,128)(2,1)}, bf16[1536,1024]{1,0:T(8,128)(2,1)}, bf16[1536,896]{1,0:T(8,128)(2,1)}) custom-call(s32[16,128]{1,0:T(8,128)} %route.1.refs_0_.tab_in, bf16[48,16,1536]{2,1,0:T(8,128)(2,1)} %bitcast.15, bf16[48,1024]{1,0:T(8,128)(2,1)} %refs_2_.1, bf16[48,512]{1,0:T(8,128)(2,1)} %refs_3_.1, bf16[48,256]{1,0:T(8,128)(2,1)} %refs_4_.1, ...), custom_call_target="tpu_custom_call" | custom-call | tf_op jit(solution)/shard_map/gather_all/pallas_call | solution.py:374
  44.9 22.5 %mixer.1 = (bf16[768,512]{1,0:T(8,128)(2,1)}, f32[8,128]{1,0:T(8,128)}, bf16[64,16,640]{2,1,0:T(8,128)(2,1)}, bf16[64,8,384]{2,1,0:T(8,128)(2,1)}, bf16[48,512,1...) custom-call(s32[16,128]{1,0:T(8,128)} %route.1.refs_0_.tab_in, ...), custom_call_target="tpu_custom_call" | custom-call | tf_op jit(solution)/shard_map/mixer/pallas_call | solution.py:882
  67.4 46.9 %send_home.1 = (bf16[48,16,384]{2,1,0:T(8,128)(2,1)}, bf16[64,16,640]{2,1,0:T(8,128)(2,1)}, bf16[64,8,384]{2,1,0:T(8,128)(2,1)}) custom-call(s32[16,128]{1,0:T(8,128)} %route.1.refs_0_.tab_in, bf16[768,512]{1,0:T(8,128)(2,1)} %get-tuple-element.23.refs_1_, f32[8,128]{1,0:T(8,128)} %get-tuple-element.24.refs_2_, ...), custom_call_target="tpu_custom_call" | custom-call | tf_op jit(solution)/shard_map/send_home/pallas_call | solution.py:589
  114.3 0.0 copy-start
  114.3 4.8 %arrive.1 = (bf16[48,512,128]{2,1,0:T(8,128)(2,1)}, bf16[3,48,512]{2,1,0:T(8,128)(2,1)}, bf16[3,48,256]{2,1,0:T(8,128)(2,1)}) custom-call(s32[16,128]{1,0:T(8,128)} %route.1.refs_0_.tab_in, bf16[64,16,640]{2,1,0:T(8,128)(2,1)} %get-tuple-element.28.xgot_in, bf16[64,8,384]{2,1,0:T(8,128)(2,1)} %get-tuple-element.29.egot_in, ...), custom_call_target="tpu_custom_call", output_to_operand_aliasing={{0}: (5, {})} | custom-call | tf_op jit(solution)/shard_map/arrive/pallas_call | solution.py:992
  119.1 0.0 copy-done
  119.1 0.8 copy.26
Async XLA Ops:
  114.3 4.8 %copy-start = (bf16[48,16,384]{2,1,0:T(8,128)(2,1)S(1)}, bf16[48,16,384]{2,1,0:T(8,128)(2,1)}, u32[]{:S(2)}) copy-start(bf16[48,16,384]{2,1,0:T(8,128)(2,1)} %get-tuple-element.27) | copy-start | bytes 1769476

commit v5 on v4

--- a/solution.py
+++ b/solution.py
@@ -93,6 +93,7 @@
     key_col = 2 * o_col + rank_col
     fi, fj = ii.astype(f32), jj.astype(f32)
     goes = (c_col == 1) & (key_col == fj)
+    leaves = (c_col == 0) & (key_col == fj)
     stays = (c_col == 0) & (nth_col == fj)
 
     def total(mask, x):
@@ -100,17 +101,17 @@
 
     table = (
         total(goes, fi), picks[0], back,
-        jnp.where(c_row == 1, key_row, 0.0), jnp.where(c_row == 0, held + nth_row, 0.0),
+        jnp.where(c_row == 1, key_row, 0.0), jnp.where(c_row == 0, nth_row, 0.0),
         (c_row == 1).astype(f32),
         total(stays, fi), total(stays, key_col), total(stays, a_col),
-        taken[0], places[0], picks[1], places[1],
+        taken[0], places[0], picks[1], places[1], total(leaves, nth_col),
     )
     for k, line in enumerate(table):
         out[k : k + 1, :] = line.astype(jnp.int32)
     out[len(table) :, :] = jnp.zeros((16 - len(table), 128), jnp.int32)
 
 
-SEND, PICK, BACK, FROM_MSG, FROM_MIX, MOVED, STAY, STAY_KEY, STAY_ACC, ACC, POS, PICK_O, POS_O = range(13)
+SEND, PICK, BACK, FROM_MSG, FROM_MIX, MOVED, STAY, STAY_KEY, STAY_ACC, ACC, POS, PICK_O, POS_O, LEAVE = range(14)
 
 
 def route(code, held):
@@ -399,225 +400,6 @@
     )(tab, hidden, wa, w_out, w_bc, w_dt)
 
 
-def return_kernel(
-    rows, cols, cap, tab_in, gg_in, ss_from, fb, xmsg, emsg, mixed, xgot, egot,
-    tab, gg, wo, ss, part, came, ss_in, scale, mix0, mix1, mix2, packed, got0, got1, got2,
-    ld, loc, ss_s, ss_r, y_s, y_r, a2a_s, a2a_r, x_s, x_r, e_s, e_r,
-):
-    row, me = lax.axis_index("row"), lax.axis_index("col")
-    barrier = greet(row, me, rows, cols)
-    pieces = part.shape[0] // rows
-    tokens = part.shape[1]
-    inner = gg.shape[1]
-    width = pieces * 128
-    loads = (
-        pltpu.make_async_copy(gg_in, gg, ld.at[0]),
-        pltpu.make_async_copy(fb.at[:, pl.ds(0, inner)], wo, ld.at[1]),
-        pltpu.make_async_copy(ss_from, ss, ld.at[2]),
-        pltpu.make_async_copy(tab_in, tab, ld.at[3]),
-    )
-    for copy in loads:
-        copy.start()
-    for copy in loads:
-        copy.wait()
-    order = (1, 3, 2)
-
-    def block(peer, j, count):
-        at = pl.ds(pl.multiple_of(peer * width + j * 128, 128), count * 128)
-        out = lax.dot_general(
-            gg[...], wo[at, :], (((1,), (1,)), ((), ())), preferred_element_type=jnp.float32
-        ).astype(part.dtype)
-        for k in range(count):
-            part[peer * pieces + j + k] = out[:, k * 128 : (k + 1) * 128]
-
-    def send_block(peer, j, d):
-        pltpu.make_async_remote_copy(
-            part.at[peer * pieces + j], came.at[row, j], y_s.at[j, d], y_r.at[row, j],
-            device_id=(peer, me), device_id_type=MESH,
-        ).start()
-
-    def first(d, carry):
-        peer = (row + d) % rows
-        block(peer, 0, 1)
-        send_block(peer, 0, d)
-        return carry
-
-    def later(d, carry):
-        peer = (row + d) % rows
-        block(peer, 1, pieces - 1)
-        for j in range(1, pieces):
-            send_block(peer, j, d)
-        return carry
-
-    def piece(ref, c):
-        return ref.at[pl.ds(c * cap, cap)]
-
-    pl.semaphore_wait(barrier, cols - 1 + rows - 1)
-    for k, d in enumerate(order):
-        pltpu.make_async_remote_copy(
-            ss, ss_in.at[row], ss_s.at[k], ss_r.at[row],
-            device_id=((row + d) % rows, me), device_id_type=MESH,
-        ).start()
-    lax.fori_loop(1, rows, first, 0)
-    def push_factors(d, carry):
-        peer = (me + d) % cols
-        for src, dst, ss_, rs_ in ((xmsg, xgot, x_s, x_r), (emsg, egot, e_s, e_r)):
-            pltpu.make_async_remote_copy(
-                piece(src, peer), piece(dst, me), ss_.at[peer], rs_.at[me],
-                device_id=(row, peer), device_id_type=MESH,
-            ).start()
-        return carry
-
-    lax.fori_loop(1, cols, push_factors, 0)
-    keep_x = pltpu.make_async_copy(piece(xmsg, me), piece(xgot, me), loc.at[4])
-    keep_e = pltpu.make_async_copy(piece(emsg, me), piece(egot, me), loc.at[5])
-    keep_x.start()
-    keep_e.start()
-    lax.fori_loop(1, rows, later, 0)
-    block(row, 0, 1)
-    block(row, 1, pieces - 1)
-    total = ss[...]
-    for d in order:
-        peer = (row + d) % rows
-        pltpu.make_async_copy(ss_in.at[peer], ss_in.at[peer], ss_r.at[peer]).wait()
-        total = total + ss_in[peer]
-    factor = lax.rsqrt(total / INNER + 1e-05)
-    for i in range(tokens // TOK):
-        line = jnp.broadcast_to(factor[i : i + 1, :], (TOK, TOK))
-        scale[pl.ds(i * TOK, TOK), :] = line.T
-    gots = (got0, got1, got2)
-
-    mixes = (mix0, mix1, mix2)
-    for j in range(pieces):
-        mix = mixes[j]
-        for d in order:
-            peer = (row + d) % rows
-            pltpu.make_async_copy(came.at[peer, j], came.at[peer, j], y_r.at[peer, j]).wait()
-
-        def add(i, carry):
-            at = pl.ds(pl.multiple_of(i * TOK, TOK), TOK)
-            value = part[row * pieces + j, at, :].astype(jnp.float32)
-            for d in order:
-                value = value + came[(row + d) % rows, j, at, :].astype(jnp.float32)
-            value = (value * scale[at, :]).astype(mix.dtype)
-            mix[pl.ds(i * GROUP, GROUP)] = value.reshape(GROUP, LEN, 128)
-            return carry
-
-        lax.fori_loop(0, tokens // TOK, add, 0)
-
-        def pack(s, carry):
-            packed[j, s] = mix[tab[BACK, s]]
-            return carry
-
-        lax.fori_loop(0, cols * cap, pack, 0)
-
-        def push(d, carry):
-            peer = (me + d) % cols
-            pltpu.make_async_remote_copy(
-                piece(packed.at[j], peer), piece(gots[j], me), a2a_s.at[j, peer], a2a_r.at[j, me],
-                device_id=(row, peer), device_id_type=MESH,
-            ).start()
-            return carry
-
-        lax.fori_loop(1, cols, push, 0)
-        pltpu.make_async_copy(piece(packed.at[j], me), piece(gots[j], me), loc.at[1 + j]).start()
-    for j in range(pieces):
-        got, mix = gots[j], mixes[j]
-        pltpu.make_async_copy(piece(packed.at[j], me), piece(got, me), loc.at[1 + j]).wait()
-
-        def took(d, carry):
-            peer = (me + d) % cols
-            pltpu.make_async_copy(piece(got, peer), piece(got, peer), a2a_r.at[j, peer]).wait()
-            return carry
-
-        lax.fori_loop(1, cols, took, 0)
-
-        def unpack(s, carry):
-            moved = tab[MOVED, s].astype(jnp.float32)
-            away = got[tab[FROM_MSG, s]].astype(jnp.float32)
-            here = mix[tab[FROM_MIX, s]].astype(jnp.float32)
-            value = jnp.where(moved > 0.5, away, here)
-            mixed[s, :, j * 128 : (j + 1) * 128] = value.astype(mixed.dtype)
-            return carry
-
-        lax.fori_loop(0, mixed.shape[0], unpack, 0)
-    for k in range(3):
-        pltpu.make_async_copy(ss, ss, ss_s.at[k]).wait()
-        for j in range(pieces):
-            pltpu.make_async_copy(part.at[j], part.at[j], y_s.at[j, k + 1]).wait()
-    for j in range(pieces):
-
-        def gone(d, carry):
-            peer = (me + d) % cols
-            pltpu.make_async_copy(
-                piece(packed.at[j], peer), piece(packed.at[j], peer), a2a_s.at[j, peer]
-            ).wait()
-            return carry
-
-        lax.fori_loop(1, cols, gone, 0)
-
-
-    keep_x.wait()
-    keep_e.wait()
-
-    def factors(d, carry):
-        peer = (me + d) % cols
-        for ref, ss_, rs_ in ((xgot, x_s, x_r), (egot, e_s, e_r)):
-            pltpu.make_async_copy(piece(ref, peer), piece(ref, peer), rs_.at[peer]).wait()
-            pltpu.make_async_copy(piece(ref, peer), piece(ref, peer), ss_.at[peer]).wait()
-        return carry
-
-    lax.fori_loop(1, cols, factors, 0)
-
-
-def send_home(tab, gg, ss, fb, xmsg, emsg, rows, cols, cap):
-    blocks = fb.shape[0] // 128
-    pieces = blocks // rows
-    tokens, inner = gg.shape
-    hbm = pl.BlockSpec(memory_space=pltpu.HBM)
-    vmem = pl.BlockSpec(memory_space=pltpu.VMEM)
-    dma = pltpu.SemaphoreType.DMA
-    slots = cols * cap
-    requests = tokens // LEN
-    dt = gg.dtype
-
-    def body(*refs):
-        return_kernel(rows, cols, cap, *refs)
-
-    mix = pltpu.VMEM((requests, LEN, 128), dt)
-    got = pltpu.VMEM((slots, LEN, 128), dt)
-    return pl.pallas_call(
-        body,
-        out_shape=(
-            jax.ShapeDtypeStruct((requests, LEN, pieces * 128), dt),
-            jax.ShapeDtypeStruct(xmsg.shape, dt),
-            jax.ShapeDtypeStruct(emsg.shape, dt),
-        ),
-        in_specs=[hbm] * 6,
-        out_specs=(vmem, hbm, hbm),
-        scratch_shapes=[
-            pltpu.SMEM(tab.shape, jnp.int32),
-            pltpu.VMEM((tokens, inner), dt),
-            pltpu.VMEM((fb.shape[0], inner), dt),
-            pltpu.VMEM(ss.shape, jnp.float32),
-            pltpu.VMEM((blocks, tokens, 128), dt),
-            pltpu.VMEM((rows, pieces, tokens, 128), dt),
-            pltpu.VMEM((rows,) + ss.shape, jnp.float32),
-            pltpu.VMEM((tokens, 128), jnp.float32),
-            mix, mix, mix,
-            pltpu.VMEM((pieces, slots, LEN, 128), dt),
-            got, got, got,
-            dma((4,)), dma((3 + pieces,)), dma((3,)), dma((rows,)),
-            dma((pieces, rows)), dma((rows, pieces)), dma((pieces, cols)), dma((pieces, cols)),
-            dma((cols,)), dma((cols,)), dma((cols,)), dma((cols,)),
-        ],
-        compiler_params=pltpu.CompilerParams(
-            collective_id=1, has_side_effects=True, vmem_limit_bytes=60 << 20
-        ),
-        name="send_home",
-    )(tab, gg, ss, fb, xmsg, emsg)
-
-
 def silu(v):
     return v / (1.0 + jnp.exp(-v))
 
@@ -629,16 +411,21 @@
 
 
 def mixer_kernel(
-    held, tab_in, hid_c, hidden, fa, fb, *refs,
+    rows, cols, cap, held, tab_in, hid_c, hidden, fa, fb, *refs,
 ):
     sources, refs = refs[:8], refs[8:]
-    prev, pex_in, peb_in, gg, ss, xmsg, emsg, nst, nex, neb, tab, *refs = refs
+    prev, pex_in, peb_in, mixed, nst, edge_c, xgot, egot, tab, *refs = refs
     params, refs = refs[:8], refs[8:]
     dtb, alog, skip, cxw, cxb, cbw, cbb, gain = params
     (
-        pex, peb, hid, wa, wb, old, gate, xin, bc, dts, cx, cb, pexf, pebf, new,
-        h_sem, o_sem, w_sem, n_sem, v_sem,
+        pex, peb, hid, home, wa, wb, wo, old, gate, xin, bc, dts, gg, ss, cx, cb, pexf, pebf, es,
+        new, sent, edge_o, xmsg, emsg, part_o, part_c, came_o, came_c, ss_in, scale, mix_o,
+        mix0, mix1, mix2, packed, got0, got1, got2,
+        h_sem, o_sem, w_sem, n_sem, v_sem, loc, ss_s, ss_r, yo_s, yo_r, yc_s, yc_r,
+        a2a_s, a2a_r, x_s, x_r, e_s, e_r,
     ) = refs
+    row, me = lax.axis_index("row"), lax.axis_index("col")
+    barrier = greet(row, me, rows, cols)
     f32, bf16 = jnp.float32, jnp.bfloat16
     inner = gain.shape[1]
     requests = hid.shape[0]
@@ -662,19 +449,16 @@
 
     wa_load(0).start()
 
-    def home(n):
-        return pltpu.make_async_copy(hidden.at[tab[STAY, n]], hid.at[held + n], o_sem.at[n])
-
-    @pl.loop(0, requests - held)
-    def _(n):
-        home(n).start()
-
+    load_home = pltpu.make_async_copy(hidden, home, o_sem)
+    load_home.start()
     for n in range(1, blocks):
         wa_load(n).start()
     late = pl.ds(inner, wb.shape[1])
     load_bc = pltpu.make_async_copy(fb.at[:, late], wb, w_sem.at[blocks])
+    load_out = pltpu.make_async_copy(fb.at[:, pl.ds(0, inner)], wo, w_sem.at[blocks + 2])
     load_old = pltpu.make_async_copy(prev, old, w_sem.at[blocks + 1])
     load_bc.start()
+    load_out.start()
     load_old.start()
     for copy in small[:-1]:
         copy.wait()
@@ -682,6 +466,10 @@
     pebf[...] = peb[...].astype(f32)
 
     t_ids, s_ids = token_masks()
+    row_ids = lax.broadcasted_iota(jnp.int32, (4 * GROUP, TOK), 0)
+    k_ids = lax.broadcasted_iota(jnp.int32, (4 * GROUP, TOK), 1)
+    r_ids, q_ids = row_ids // 4, row_ids % 4
+    es[...] = jnp.zeros(es.shape, f32)
     same = (t_ids // LEN) == (s_ids // LEN)
     causal = same & (t_ids >= s_ids)
     tri = causal.astype(f32)
@@ -700,11 +488,13 @@
     )[0:1, :]
 
     load_h.wait()
-
-    @pl.loop(0, requests - held)
-    def _(n):
-        home(n).wait()
-
+    load_home.wait()
+
+    def stay(n, carry):
+        hid[held + n] = home[tab[STAY, n]]
+        return carry
+
+    lax.fori_loop(0, requests - held, stay, 0)
     left = lax.broadcasted_iota(jnp.int32, (tokens, 128), 1) < HEAD_DIM
     for n in range(blocks):
         wa_load(n).wait()
@@ -723,16 +513,16 @@
     load_old.wait()
 
     def store(s):
-        return pltpu.make_async_copy(new.at[s], nst.at[tab[POS, s]], n_sem.at[s])
+        return pltpu.make_async_copy(new.at[s], nst.at[s], n_sem.at[s])
 
     def group(i, live):
         at = pl.ds(pl.multiple_of(i * TOK, TOK), TOK)
         first = i * GROUP
         last = jnp.zeros((TOK, TOK), jnp.int32)
-        accs = []
+        row_acc = jnp.zeros((4 * GROUP, TOK), jnp.int32)
         for r in range(GROUP):
             acc = tab[ACC, first + r] if live else tab[STAY_ACC, first - held + r]
-            accs.append(acc)
+            row_acc = jnp.where(r_ids == r, acc, row_acc)
             last = jnp.where(t_ids // LEN == r, acc, last)
             if live:
                 for k in range(KCONV - 1):
@@ -752,21 +542,25 @@
             tot_b = tot_b + cbw[k : k + 1, :].reshape(1, 1, 2 * STATE) * cb[:, 13 + k : 29 + k, :]
         xc = silu(tot_x).reshape(TOK, inner).astype(bf16)
         bcc = silu(tot_b).reshape(TOK, 2 * STATE).astype(bf16)
+        near = jnp.concatenate([xin[at, :], bc[at, :]], axis=1)
+        want = q_ids + row_acc
+        pick = (k_ids == LEN * r_ids + want - 3) & (want >= 3) & (q_ids < 3)
+        edge = jnp.dot(pick.astype(bf16), near, preferred_element_type=f32)
+        if live:
+            for k in range(KCONV - 1):
+                rows8 = pl.ds(pl.multiple_of(first, GROUP), GROUP)
+                es[k * GROUP : (k + 1) * GROUP, :inner] = pexf[k, rows8, :]
+                es[k * GROUP : (k + 1) * GROUP, inner:] = pebf[k, rows8, :]
+            pick = (k_ids == GROUP * want + r_ids) & (want < 3) & (q_ids < 3)
+            edge = edge + jnp.dot(
+                pick.astype(bf16), es[...].astype(bf16), preferred_element_type=f32
+            )
         for r in range(GROUP):
-            ex = pltpu.roll(cx[r], 19 - accs[r], 0)
-            eb = pltpu.roll(cb[r], 19 - accs[r], 0)
+            lines = edge[4 * r : 4 * r + 4, :].astype(bf16)
             if live:
-                place = tab[POS, first + r]
-                for k in range(KCONV - 1):
-                    nex[k, pl.ds(place, 1), :] = ex[k : k + 1, :]
-                    neb[k, pl.ds(place, 1), :] = eb[k : k + 1, :]
+                edge_c[first + r] = lines
             else:
-                lines = []
-                for k in range(KCONV - 1):
-                    lines.append(ex[k : k + 1, :384])
-                    lines.append(jnp.concatenate([ex[k : k + 1, 384:], eb[k : k + 1, :]], axis=1))
-                lines.append(jnp.zeros((2, 384), f32))
-                emsg[tab[STAY_KEY, first - held + r]] = jnp.concatenate(lines, axis=0).astype(bf16)
+                edge_o[first - held + r] = lines
         b_in, c_in = bcc[:, :STATE], bcc[:, STATE:]
         xf = xc.astype(f32)
         raw = dts[at, :] + bias
@@ -816,12 +610,11 @@
         ss[pl.ds(i, 1), :] = jnp.broadcast_to(squares, (TOK, TOK)).T[0:1, :]
 
         if not live:
-            sent = (xf * weight_x).astype(bf16)
+            out = (xf * weight_x).astype(bf16)
             for r in range(GROUP):
-                key = tab[STAY_KEY, first - held + r]
                 lines = slice(r * LEN, (r + 1) * LEN)
-                xmsg[key, :, :inner] = sent[lines, :]
-                xmsg[key, :, inner:] = b_in[lines, :]
+                sent[first - held + r, :, :inner] = out[lines, :]
+                sent[first - held + r, :, inner:] = b_in[lines, :]
             return
         xw = (xf * weight_x).T
         high = xw.astype(bf16)
@@ -851,25 +644,223 @@
                 new[s] = now.reshape(inner, STATE).astype(bf16)
                 store(s).start()
 
+    @pl.loop(held // GROUP, requests // GROUP)
+    def _(i):
+        group(i, False)
+
+    load_out.wait()
+    moving = held * LEN
+    resting = tokens - moving
+    pieces = part_c.shape[1]
+    width = pieces * 128
+    order = (1, 3, 2)
+
+    def project(lines, peer, j, count):
+        at = pl.ds(pl.multiple_of(peer * width + j * 128, 128), count * 128)
+        return lax.dot_general(
+            gg[lines, :], wo[at, :], (((1,), (1,)), ((), ())), preferred_element_type=f32
+        ).astype(bf16)
+
+    def rest_block(peer):
+        part_o[peer] = project(slice(moving, tokens), peer, 0, pieces)
+
+    def move_block(peer, j, count):
+        out = project(slice(0, moving), peer, j, count)
+        for k in range(count):
+            part_c[peer, j + k] = out[:, k * 128 : (k + 1) * 128]
+
+    def piece(ref, c):
+        return ref.at[pl.ds(c * cap, cap)]
+
+    def to_slots(q, carry):
+        n = tab[LEAVE, q]
+        xmsg[q] = sent[n]
+        emsg[q] = edge_o[n]
+        return carry
+
+    lax.fori_loop(0, cols * cap, to_slots, 0)
+    pl.semaphore_wait(barrier, cols - 1 + rows - 1)
+
+    def push_factors(d, carry):
+        peer = (me + d) % cols
+        for a, b, s_, r_ in ((xmsg, xgot, x_s, x_r), (emsg, egot, e_s, e_r)):
+            pltpu.make_async_remote_copy(
+                piece(a, peer), piece(b, me), s_.at[peer], r_.at[me],
+                device_id=(row, peer), device_id_type=MESH,
+            ).start()
+        return carry
+
+    lax.fori_loop(1, cols, push_factors, 0)
+    keep_x = pltpu.make_async_copy(piece(xmsg, me), piece(xgot, me), loc.at[0])
+    keep_e = pltpu.make_async_copy(piece(emsg, me), piece(egot, me), loc.at[1])
+    keep_x.start()
+    keep_e.start()
+
+    def send_rest(d, carry):
+        peer = (row + d) % rows
+        rest_block(peer)
+        pltpu.make_async_remote_copy(
+            part_o.at[peer], came_o.at[row], yo_s.at[d], yo_r.at[row],
+            device_id=(peer, me), device_id_type=MESH,
+        ).start()
+        return carry
+
+    lax.fori_loop(1, rows, send_rest, 0)
+
     @pl.loop(0, held // GROUP)
     def _(i):
         group(i, True)
 
-    @pl.loop(held // GROUP, requests // GROUP)
-    def _(i):
-        group(i, False)
+    for k, d in enumerate(order):
+        pltpu.make_async_remote_copy(
+            ss, ss_in.at[row], ss_s.at[k], ss_r.at[row],
+            device_id=((row + d) % rows, me), device_id_type=MESH,
+        ).start()
+
+    def send_block(peer, j, d):
+        pltpu.make_async_remote_copy(
+            part_c.at[peer, j], came_c.at[row, j], yc_s.at[j, d], yc_r.at[row, j],
+            device_id=(peer, me), device_id_type=MESH,
+        ).start()
+
+    def first_block(d, carry):
+        peer = (row + d) % rows
+        move_block(peer, 0, 1)
+        send_block(peer, 0, d)
+        return carry
+
+    def later_blocks(d, carry):
+        peer = (row + d) % rows
+        move_block(peer, 1, pieces - 1)
+        for j in range(1, pieces):
+            send_block(peer, j, d)
+        return carry
+
+    lax.fori_loop(1, rows, first_block, 0)
+    lax.fori_loop(1, rows, later_blocks, 0)
+    move_block(row, 0, 1)
+    move_block(row, 1, pieces - 1)
+    rest_block(row)
+    total = ss[...]
+    for d in order:
+        peer = (row + d) % rows
+        pltpu.make_async_copy(ss_in.at[peer], ss_in.at[peer], ss_r.at[peer]).wait()
+        total = total + ss_in[peer]
+    factor = lax.rsqrt(total / INNER + 1e-05)
+    for i in range(tokens // TOK):
+        line = jnp.broadcast_to(factor[i : i + 1, :], (TOK, TOK))
+        scale[pl.ds(i * TOK, TOK), :] = line.T
+    for d in order:
+        peer = (row + d) % rows
+        pltpu.make_async_copy(came_o.at[peer], came_o.at[peer], yo_r.at[peer]).wait()
+
+    def add_rest(i, carry):
+        at = pl.ds(pl.multiple_of(i * TOK, TOK), TOK)
+        by = scale[pl.ds(pl.multiple_of(moving + i * TOK, TOK), TOK), :]
+        for j in range(pieces):
+            lanes = slice(j * 128, (j + 1) * 128)
+            value = part_o[row, at, lanes].astype(f32)
+            for d in order:
+                value = value + came_o[(row + d) % rows, at, lanes].astype(f32)
+            mix_o[j, pl.ds(i * GROUP, GROUP)] = (value * by).astype(bf16).reshape(GROUP, LEN, 128)
+        return carry
+
+    lax.fori_loop(0, resting // TOK, add_rest, 0)
+    gots, mixes = (got0, got1, got2), (mix0, mix1, mix2)
+    for j in range(pieces):
+        mix = mixes[j]
+        for d in order:
+            peer = (row + d) % rows
+            pltpu.make_async_copy(came_c.at[peer, j], came_c.at[peer, j], yc_r.at[peer, j]).wait()
+
+        def add(i, carry):
+            at = pl.ds(pl.multiple_of(i * TOK, TOK), TOK)
+            value = part_c[row, j, at, :].astype(f32)
+            for d in order:
+                value = value + came_c[(row + d) % rows, j, at, :].astype(f32)
+            value = (value * scale[at, :]).astype(bf16)
+            mix[pl.ds(i * GROUP, GROUP)] = value.reshape(GROUP, LEN, 128)
+            return carry
+
+        lax.fori_loop(0, moving // TOK, add, 0)
+
+        def pack(q, carry):
+            packed[j, q] = mix[tab[BACK, q]]
+            return carry
+
+        lax.fori_loop(0, cols * cap, pack, 0)
+
+        def push(d, carry):
+            peer = (me + d) % cols
+            pltpu.make_async_remote_copy(
+                piece(packed.at[j], peer), piece(gots[j], me), a2a_s.at[j, peer], a2a_r.at[j, me],
+                device_id=(row, peer), device_id_type=MESH,
+            ).start()
+            return carry
+
+        lax.fori_loop(1, cols, push, 0)
+        pltpu.make_async_copy(piece(packed.at[j], me), piece(gots[j], me), loc.at[2 + j]).start()
+    for j in range(pieces):
+        got = gots[j]
+        pltpu.make_async_copy(piece(packed.at[j], me), piece(got, me), loc.at[2 + j]).wait()
+
+        def took(d, carry):
+            peer = (me + d) % cols
+            pltpu.make_async_copy(piece(got, peer), piece(got, peer), a2a_r.at[j, peer]).wait()
+            return carry
+
+        lax.fori_loop(1, cols, took, 0)
+
+        def unpack(s, carry):
+            moved = tab[MOVED, s].astype(f32)
+            away = got[tab[FROM_MSG, s]].astype(f32)
+            here = mix_o[j, tab[FROM_MIX, s]].astype(f32)
+            value = jnp.where(moved > 0.5, away, here)
+            mixed[s, :, j * 128 : (j + 1) * 128] = value.astype(bf16)
+            return carry
+
+        lax.fori_loop(0, requests, unpack, 0)
+    for k in range(rows - 1):
+        pltpu.make_async_copy(ss, ss, ss_s.at[k]).wait()
+        pltpu.make_async_copy(part_o.at[0], part_o.at[0], yo_s.at[k + 1]).wait()
+        for j in range(pieces):
+            pltpu.make_async_copy(part_c.at[0, j], part_c.at[0, j], yc_s.at[j, k + 1]).wait()
+    for j in range(pieces):
+
+        def gone(d, carry):
+            peer = (me + d) % cols
+            pltpu.make_async_copy(
+                piece(packed.at[j], peer), piece(packed.at[j], peer), a2a_s.at[j, peer]
+            ).wait()
+            return carry
+
+        lax.fori_loop(1, cols, gone, 0)
+    keep_x.wait()
+    keep_e.wait()
+
+    def factors(d, carry):
+        peer = (me + d) % cols
+        for ref, s_, r_ in ((xgot, x_s, x_r), (egot, e_s, e_r)):
+            pltpu.make_async_copy(piece(ref, peer), piece(ref, peer), r_.at[peer]).wait()
+            pltpu.make_async_copy(piece(ref, peer), piece(ref, peer), s_.at[peer]).wait()
+        return carry
+
+    lax.fori_loop(1, cols, factors, 0)
 
     @pl.loop(0, held)
     def _(s):
         store(s).wait()
 
 
-def mixer(tab, hid_c, hidden, fa, fb, vectors, prev, pex, peb, slots):
+def mixer(tab, hid_c, hidden, fa, fb, vectors, prev, pex, peb, rows, cols, cap):
     requests, _, model = hidden.shape
     held = hid_c.shape[0]
     tokens = requests * LEN
     inner = fa.shape[1] // 2
-    heads = inner // HEAD_DIM
+    width = model // rows
+    pieces = width // 128
+    slots = cols * cap
+    rest = requests - held
     dt = hidden.dtype
     f32 = jnp.float32
     vmem = pl.BlockSpec(memory_space=pltpu.VMEM)
@@ -877,62 +868,95 @@
     dma = pltpu.SemaphoreType.DMA
 
     def body(*refs):
-        mixer_kernel(held, *refs)
-
+        mixer_kernel(rows, cols, cap, held, *refs)
+
+    wide = inner + 2 * STATE
+    mix = pltpu.VMEM((held, LEN, 128), dt)
+    got = pltpu.VMEM((slots, LEN, 128), dt)
     return pl.pallas_call(
         body,
         out_shape=(
-            jax.ShapeDtypeStruct((tokens, inner), dt),
-            jax.ShapeDtypeStruct((8, 128), f32),
+            jax.ShapeDtypeStruct((requests, LEN, width), dt),
+            jax.ShapeDtypeStruct((held, inner, STATE), dt),
+            jax.ShapeDtypeStruct((held, 4, wide), dt),
             jax.ShapeDtypeStruct((slots, LEN, inner + STATE), dt),
-            jax.ShapeDtypeStruct((slots, 8, 384), dt),
-            jax.ShapeDtypeStruct((requests, inner, STATE), dt),
-            jax.ShapeDtypeStruct((3, requests, inner), f32),
-            jax.ShapeDtypeStruct((3, requests, 2 * STATE), f32),
+            jax.ShapeDtypeStruct((slots, 4, wide), dt),
         ),
         in_specs=[hbm] * (8 + len(vectors)),
-        out_specs=(vmem, vmem, vmem, vmem, hbm, vmem, vmem),
+        out_specs=(vmem, hbm, vmem, hbm, hbm),
         scratch_shapes=[
             pltpu.SMEM(tab.shape, jnp.int32),
             *[pltpu.VMEM(v.shape, v.dtype) for v in vectors],
             pltpu.VMEM(pex.shape, dt),
             pltpu.VMEM(peb.shape, dt),
             pltpu.VMEM((requests, LEN, model), dt),
+            pltpu.VMEM((requests, LEN, model), dt),
             pltpu.VMEM(fa.shape, dt),
             pltpu.VMEM((fb.shape[0], fb.shape[1] - inner), dt),
+            pltpu.VMEM((fb.shape[0], inner), dt),
             pltpu.VMEM((held, inner, STATE), dt),
             pltpu.VMEM((tokens, inner), dt),
             pltpu.VMEM((tokens, inner), dt),
             pltpu.VMEM((tokens, 2 * STATE), dt),
             pltpu.VMEM((tokens, 128), f32),
+            pltpu.VMEM((tokens, inner), dt),
+            pltpu.VMEM((8, 128), f32),
             pltpu.VMEM((GROUP, 32, inner), f32),
             pltpu.VMEM((GROUP, 32, 2 * STATE), f32),
             pltpu.VMEM((3, held, inner), f32),
             pltpu.VMEM((3, held, 2 * STATE), f32),
+            pltpu.VMEM((TOK, wide), f32),
             pltpu.VMEM((held, inner, STATE), dt),
-            dma(()), dma((requests - held,)), dma((fa.shape[1] // 256 + 2,)), dma((held,)),
-            dma((len(vectors) + 3,)),
+            pltpu.VMEM((rest, LEN, inner + STATE), dt),
+            pltpu.VMEM((rest, 4, wide), dt),
+            pltpu.VMEM((slots, LEN, inner + STATE), dt),
+            pltpu.VMEM((slots, 4, wide), dt),
+            pltpu.VMEM((rows, rest * LEN, width), dt),
+            pltpu.VMEM((rows, pieces, held * LEN, 128), dt),
+            pltpu.VMEM((rows, rest * LEN, width), dt),
+            pltpu.VMEM((rows, pieces, held * LEN, 128), dt),
+            pltpu.VMEM((rows, 8, 128), f32),
+            pltpu.VMEM((tokens, 128), f32),
+            pltpu.VMEM((pieces, rest, LEN, 128), dt),
+            mix, mix, mix,
+            pltpu.VMEM((pieces, slots, LEN, 128), dt),
+            got, got, got,
+            dma(()), dma(()), dma((fa.shape[1] // 256 + 3,)), dma((held,)),
+            dma((len(vectors) + 3,)), dma((2 + pieces,)), dma((3,)), dma((rows,)),
+            dma((rows,)), dma((rows,)), dma((pieces, rows)), dma((rows, pieces)),
+            dma((pieces, cols)), dma((pieces, cols)),
+            dma((cols,)), dma((cols,)), dma((cols,)), dma((cols,)),
         ],
-        compiler_params=pltpu.CompilerParams(vmem_limit_bytes=60 << 20),
+        compiler_params=pltpu.CompilerParams(
+            collective_id=1, has_side_effects=True, vmem_limit_bytes=60 << 20
+        ),
         name="mixer",
     )(tab, hid_c, hidden, fa, fb, *vectors, prev, pex, peb)
 
 
 def arrive_kernel(
-    tab_in, xgot_in, egot_in, exf, ebf, nst_in, nst, nex, neb,
-    tab, xgot, egot, xs, bs, ex, eb, new, n_sem, l_sem,
+    tab_in, xgot_in, egot_in, edge_in, nst_in, nst, nex, neb,
+    tab, xgot, egot, edge, xs, bs, ex, eb, new, n_sem, m_sem, l_sem,
 ):
     f32, bf16 = jnp.float32, jnp.bfloat16
     count, inner = new.shape[0], new.shape[1]
     loads = [
         pltpu.make_async_copy(a, b, l_sem.at[k])
         for k, (a, b) in enumerate(
-            ((tab_in, tab), (xgot_in, xgot), (egot_in, egot), (exf, ex), (ebf, eb))
+            ((tab_in, tab), (xgot_in, xgot), (egot_in, egot), (edge_in, edge))
         )
     ]
     for copy in loads:
         copy.start()
     loads[0].wait()
+
+    def place(s):
+        return pltpu.make_async_copy(nst_in.at[s], nst.at[tab[POS, s]], m_sem.at[s])
+
+    @pl.loop(0, count)
+    def _(s):
+        place(s).start()
+
     loads[1].wait()
     t_ids, _ = token_masks()
     none = jnp.zeros((TOK, STATE), bf16)
@@ -967,13 +991,14 @@
 
     @pl.loop(0, count)
     def _(u):
-        lines = egot[tab[PICK_O, u]].astype(f32)
-        at = pl.ds(tab[POS_O, u], 1)
-        for k in range(KCONV - 1):
-            ex[k, at, :] = jnp.concatenate(
-                [lines[2 * k : 2 * k + 1, :], lines[2 * k + 1 : 2 * k + 2, :128]], axis=1
-            )
-            eb[k, at, :] = lines[2 * k + 1 : 2 * k + 2, 128:]
+        for source, k, spot in (
+            (egot, tab[PICK_O, u], tab[POS_O, u]), (edge, u, tab[POS, u])
+        ):
+            lines = source[k].astype(f32)
+            at = pl.ds(spot, 1)
+            for q in range(KCONV - 1):
+                ex[q, at, :] = lines[q : q + 1, :inner]
+                eb[q, at, :] = lines[q : q + 1, inner:]
 
     nex[...] = ex[...].astype(bf16)
     neb[...] = eb[...].astype(bf16)
@@ -981,39 +1006,41 @@
     @pl.loop(0, count)
     def _(u):
         store(u).wait()
-
-
-def arrive(tab, xgot, egot, exf, ebf, nst):
-    requests, inner, _ = nst.shape
-    count = requests // 2
+        place(u).wait()
+
+
+def arrive(tab, xgot, egot, edge, nst):
+    count, inner, _ = nst.shape
+    requests = 2 * count
     dt, f32 = nst.dtype, jnp.float32
     vmem = pl.BlockSpec(memory_space=pltpu.VMEM)
     hbm = pl.BlockSpec(memory_space=pltpu.HBM)
     return pl.pallas_call(
         arrive_kernel,
         out_shape=(
-            jax.ShapeDtypeStruct(nst.shape, dt),
-            jax.ShapeDtypeStruct(exf.shape, dt),
-            jax.ShapeDtypeStruct(ebf.shape, dt),
+            jax.ShapeDtypeStruct((requests, inner, STATE), dt),
+            jax.ShapeDtypeStruct((3, requests, inner), dt),
+            jax.ShapeDtypeStruct((3, requests, 2 * STATE), dt),
         ),
-        in_specs=[hbm] * 6,
+        in_specs=[hbm] * 5,
         out_specs=(hbm, vmem, vmem),
         scratch_shapes=[
             pltpu.SMEM(tab.shape, jnp.int32),
             pltpu.VMEM(xgot.shape, dt),
             pltpu.VMEM(egot.shape, dt),
+            pltpu.VMEM(edge.shape, dt),
             pltpu.VMEM((GROUP, LEN, inner), dt),
             pltpu.VMEM((GROUP, LEN, STATE), dt),
-            pltpu.VMEM(exf.shape, f32),
-            pltpu.VMEM(ebf.shape, f32),
+            pltpu.VMEM((3, requests, inner), f32),
+            pltpu.VMEM((3, requests, 2 * STATE), f32),
             pltpu.VMEM((count, inner, STATE), dt),
             pltpu.SemaphoreType.DMA((count,)),
-            pltpu.SemaphoreType.DMA((5,)),
+            pltpu.SemaphoreType.DMA((count,)),
+            pltpu.SemaphoreType.DMA((4,)),
         ],
-        input_output_aliases={5: 0},
         compiler_params=pltpu.CompilerParams(vmem_limit_bytes=60 << 20),
         name="arrive",
-    )(tab, xgot, egot, exf, ebf, nst)
+    )(tab, xgot, egot, edge, nst)
 
 
 def per_device(
@@ -1036,12 +1063,12 @@
         dt_bias[None, :], a_log[None, :], d_skip[None, :],
         conv_x_w, conv_x_b[None, :], conv_bc_w, conv_bc_b[None, :], norm_gain[None, :],
     )
-    gg, ss, xmsg, emsg, states, exf, ebf = mixer(
+    mixed, moved, edge, xgot, egot = mixer(
         tab, hid_c, hidden, fa, fb, vectors, prev_state.reshape(held, inner, STATE),
-        prev_edge_x.transpose(1, 0, 2), prev_edge_bc.transpose(1, 0, 2), cols * cap,
+        prev_edge_x.transpose(1, 0, 2), prev_edge_bc.transpose(1, 0, 2),
+        rows, cols, cap,
     )
-    mixed, xgot, egot = send_home(tab, gg, ss, fb, xmsg, emsg, rows, cols, cap)
-    states, new_x, new_bc = arrive(tab, xgot, egot, exf, ebf, states)
+    states, new_x, new_bc = arrive(tab, xgot, egot, edge, moved)
     return (
         mixed.reshape(tokens, model // rows),
         states.reshape(requests, heads, HEAD_DIM, STATE),

time: 120 us -> 208 us (1.73)
  Pallas kernels: 117 us -> 205 us
    pallas_call x3 -> x2, Pallas kernels: 74.2 us -> 162 us  [the longest x1 98.5 us: arrive(): pl.pallas_call(arrive_kernel, out_shape=(jax.ShapeDtypeStruct((requests,...]
where the time goes in v5:
time: 208 us
  Pallas kernels  205 us (99%)
    pallas_call x1, Pallas kernels, arrive(): pl.pallas_call(arrive_kernel, out_shape=(jax.ShapeDtypeStruct((requests,...  98.5 us
    pallas_call x1, Pallas kernels, mixer(): pl.pallas_call(body, out_shape=(jax.ShapeDtypeStruct((requests, LEN, widt...  63.4 us
    pallas_call x1, Pallas kernels, gather_all(): pl.pallas_call(body, out_shape=(jax.ShapeDtypeStruct((held, LEN, model),...  41 us

profile of v5, /device:TPU:1, one launch (start us, length us, event | category | flops | bytes accessed | tf_op | source)
XLA Modules:
  0.0 207.7 jit_solution(7587520975354735682)
XLA Ops:
  0.6 0.7 multiply_add_fusion
  1.4 0.7 reshape.23.refs_0_
  2.1 1.8 route.1.refs_0_.tab_in
  3.8 41.0 %gather_all.1 = (bf16[24,16,1536]{2,1,0:T(8,128)(2,1)}, bf16[1536,1024]{1,0:T(8,128)(2,1)}, bf16[1536,896]{1,0:T(8,128)(2,1)}) custom-call(s32[16,128]{1,0:T(8,128)} %route.1.refs_0_.tab_in, bf16[48,16,1536]{2,1,0:T(8,128)(2,1)} %bitcast.15, bf16[48,1024]{1,0:T(8,128)(2,1)} %refs_2_.1, bf16[48,512]{1,0:T(8,128)(2,1)} %refs_3_.1, bf16[48,256]{1,0:T(8,128)(2,1)} %refs_4_.1, ...), custom_call_target="tpu_custom_call" | custom-call | tf_op jit(solution)/shard_map/gather_all/pallas_call | solution.py:375
  44.9 63.4 %mixer.1 = (bf16[48,16,384]{2,1,0:T(8,128)(2,1)}, bf16[24,512,128]{2,1,0:T(8,128)(2,1)}, bf16[24,4,768]{2,1,0:T(4,128)(2,1)}, bf16[64,16,640]{2,1,0:T(8,128)(2,1)}, bf16[64,4,768]{2,1,0:T(4,128)(2,1)}) custom-call(s32[16,128]{1,0:T(8,128)} %route.1.refs_0_.tab_in, bf16[24,16,1536]{2,1,0:T(8,128)(2,1)} %get-tuple-element.15.refs_1_, ...), custom_call_target="tpu_custom_call" | custom-call | tf_op jit(solution)/shard_map/mixer/pallas_call | solution.py:876
  108.3 0.0 copy-start
  108.4 98.5 %arrive.1 = (bf16[48,512,128]{2,1,0:T(8,128)(2,1)}, bf16[3,48,512]{2,1,0:T(8,128)(2,1)}, bf16[3,48,256]{2,1,0:T(8,128)(2,1)}) custom-call(s32[16,128]{1,0:T(8,128)} %route.1.refs_0_.tab_in, bf16[64,16,640]{2,1,0:T(8,128)(2,1)} %get-tuple-element.19.xgot_in, bf16[64,4,768]{2,1,0:T(4,128)(2,1)} %get-tuple-element.20.egot_in, ...), custom_call_target="tpu_custom_call" | custom-call | tf_op jit(solution)/shard_map/arrive/pallas_call | solution.py:1018
  206.8 0.0 copy-done
  206.8 0.8 copy.24
Async XLA Ops:
  108.3 98.5 %copy-start = (bf16[48,16,384]{2,1,0:T(8,128)(2,1)S(1)}, bf16[48,16,384]{2,1,0:T(8,128)(2,1)}, u32[]{:S(2)}) copy-start(bf16[48,16,384]{2,1,0:T(8,128)(2,1)} %get-tuple-element.18) | copy-start | bytes 1769476

commit v6 on v5

--- a/solution.py
+++ b/solution.py
@@ -127,6 +127,15 @@
     )(code)
 
 
+def unrolled(count, step, body):
+    def some(i, carry):
+        for k in range(step):
+            body(i * step + k)
+        return carry
+
+    lax.fori_loop(0, count // step, some, 0)
+
+
 def greet(row, me, rows, cols):
     barrier = pltpu.get_barrier_semaphore()
 
@@ -150,7 +159,7 @@
 
 def gather_kernel(
     rows, cols, cap, tab_in, hidden, wa, w_out, w_bc, w_dt_in, hid_full, fa, fb,
-    tab, w_dt, wb, sl, packed, got, own, loc, a2a_s, a2a_r, was, wbs, war, wbr, y_s, y_r,
+    tab, w_dt, wb, sl, packed, got, own, loc, a2a_s, a2a_r, gone, twin, war, wbr, y_s, y_r,
 ):
     row, me = lax.axis_index("row"), lax.axis_index("col")
     barrier = greet(row, me, rows, cols)
@@ -188,11 +197,10 @@
     keep_b.start()
     load.wait()
 
-    def pack(s, carry):
+    def pack(s):
         packed[s] = sl[tab[SEND, s]]
-        return carry
-
-    lax.fori_loop(0, cols * cap, pack, 0)
+
+    unrolled(cols * cap, 8, pack)
     pl.semaphore_wait(barrier, cols - 1 + rows - 1)
 
     def piece(ref, c):
@@ -201,7 +209,7 @@
     def push(d, carry):
         peer = (me + d) % cols
         pltpu.make_async_remote_copy(
-            piece(packed, peer), piece(got, me), a2a_s.at[peer], a2a_r.at[me],
+            piece(packed, peer), piece(got, me), a2a_s, a2a_r,
             device_id=(row, peer), device_id_type=MESH,
         ).start()
         return carry
@@ -226,11 +234,11 @@
     sent = [0, 0]
 
     def send(which, src, c, dest):
-        full, ss, rs = ((fa, was, war), (fb, wbs, wbr))[which]
-        k = sent[which]
+        full, rs = ((fa, war), (fb, wbr))[which]
         sent[which] += 1
+        rs = twin.at[which] if dest is sibling else rs.at[c]
         pltpu.make_async_remote_copy(
-            src, block(full, c), ss.at[k], rs.at[c],
+            src, block(full, c), gone.at[which], rs,
             device_id=(row, dest), device_id_type=MESH,
         ).start()
 
@@ -259,18 +267,13 @@
                 forward(which, c, dest)
     keep_m.wait()
 
-    def took(d, carry):
-        peer = (me + d) % cols
-        pltpu.make_async_copy(piece(got, peer), piece(got, peer), a2a_r.at[peer]).wait()
-        return carry
-
-    lax.fori_loop(1, cols, took, 0)
-
-    def unpack(s, carry):
+    others = pl.ds(0, (cols - 1) * cap)
+    pltpu.make_async_copy(got.at[others], got.at[others], a2a_r).wait()
+
+    def unpack(s):
         own[s] = got[tab[PICK, s]]
-        return carry
-
-    lax.fori_loop(0, own.shape[0], unpack, 0)
+
+    unrolled(own.shape[0], 8, unpack)
 
     def part(ref, h, r):
         return ref.at[pl.ds(h * half, half), :, cols_of(r)]
@@ -326,35 +329,18 @@
     y_here(0, far_row)
     y_here(1, far_row)
 
-    def from_sibling(k, carry):
-        c = 2 * k + 1 - core
-        pltpu.make_async_copy(block(fa, c), block(fa, c), war.at[c]).wait()
-        pltpu.make_async_copy(block(fb, c), block(fb, c), wbr.at[c]).wait()
-        return carry
-
-    lax.fori_loop(0, cols // 2, from_sibling, 0)
+    for which, ref in ((0, fa), (1, fb)):
+        lines = pl.ds(0, (cols // 2) * depth)
+        pltpu.make_async_copy(ref.at[lines, :], ref.at[lines, :], twin.at[which]).wait()
     keep_a.wait()
     keep_b.wait()
     keep_y.wait()
 
-    def a2a_done(d, carry):
-        peer = (me + d) % cols
-        pltpu.make_async_copy(piece(packed, peer), piece(packed, peer), a2a_s.at[peer]).wait()
-        return carry
-
-    lax.fori_loop(1, cols, a2a_done, 0)
-
-    def a_done(k, carry):
-        pltpu.make_async_copy(block(fa, me), block(fa, me), was.at[k]).wait()
-        return carry
-
-    lax.fori_loop(0, sent[0], a_done, 0)
-
-    def b_done(k, carry):
-        pltpu.make_async_copy(block(fb, me), block(fb, me), wbs.at[k]).wait()
-        return carry
-
-    lax.fori_loop(0, sent[1], b_done, 0)
+    pltpu.make_async_copy(packed.at[others], packed.at[others], a2a_s).wait()
+
+    for which, ref in ((0, fa), (1, fb)):
+        lines = pl.ds(0, sent[which] * depth)
+        pltpu.make_async_copy(ref.at[lines, :], ref.at[lines, :], gone.at[which]).wait()
     for k in range(6):
         h = (0, 1, 0, 1, 0, 1)[k]
         pltpu.make_async_copy(part(hid_full, h, row), part(hid_full, h, row), y_s.at[k]).wait()
@@ -389,8 +375,8 @@
             pltpu.VMEM((cols * cap, LEN, width), dt),
             pltpu.VMEM((cols * cap, LEN, width), dt),
             pltpu.VMEM((held, LEN, width), dt),
-            dma((9,)), dma((cols,)), dma((cols,)),
-            dma((48,)), dma((48,)), dma((cols,)), dma((cols,)),
+            dma((9,)), dma(()), dma(()),
+            dma((2,)), dma((2,)), dma((cols,)), dma((cols,)),
             dma((6,)), dma((rows, 2)),
         ],
         compiler_params=pltpu.CompilerParams(
@@ -490,11 +476,10 @@
     load_h.wait()
     load_home.wait()
 
-    def stay(n, carry):
+    def stay(n):
         hid[held + n] = home[tab[STAY, n]]
-        return carry
-
-    lax.fori_loop(0, requests - held, stay, 0)
+
+    unrolled(requests - held, 4, stay)
     left = lax.broadcasted_iota(jnp.int32, (tokens, 128), 1) < HEAD_DIM
     for n in range(blocks):
         wa_load(n).wait()
@@ -672,20 +657,20 @@
     def piece(ref, c):
         return ref.at[pl.ds(c * cap, cap)]
 
-    def to_slots(q, carry):
+    def to_slots(q):
         n = tab[LEAVE, q]
         xmsg[q] = sent[n]
         emsg[q] = edge_o[n]
-        return carry
-
-    lax.fori_loop(0, cols * cap, to_slots, 0)
+
+    unrolled(cols * cap, 8, to_slots)
+    others = pl.ds(0, (cols - 1) * cap)
     pl.semaphore_wait(barrier, cols - 1 + rows - 1)
 
     def push_factors(d, carry):
         peer = (me + d) % cols
         for a, b, s_, r_ in ((xmsg, xgot, x_s, x_r), (emsg, egot, e_s, e_r)):
             pltpu.make_async_remote_copy(
-                piece(a, peer), piece(b, me), s_.at[peer], r_.at[me],
+                piece(a, peer), piece(b, me), s_, r_,
                 device_id=(row, peer), device_id_type=MESH,
             ).start()
         return carry
@@ -784,16 +769,15 @@
 
         lax.fori_loop(0, moving // TOK, add, 0)
 
-        def pack(q, carry):
+        def pack(q):
             packed[j, q] = mix[tab[BACK, q]]
-            return carry
-
-        lax.fori_loop(0, cols * cap, pack, 0)
+
+        unrolled(cols * cap, 16, pack)
 
         def push(d, carry):
             peer = (me + d) % cols
             pltpu.make_async_remote_copy(
-                piece(packed.at[j], peer), piece(gots[j], me), a2a_s.at[j, peer], a2a_r.at[j, me],
+                piece(packed.at[j], peer), piece(gots[j], me), a2a_s.at[j], a2a_r.at[j],
                 device_id=(row, peer), device_id_type=MESH,
             ).start()
             return carry
@@ -804,48 +788,29 @@
         got = gots[j]
         pltpu.make_async_copy(piece(packed.at[j], me), piece(got, me), loc.at[2 + j]).wait()
 
-        def took(d, carry):
-            peer = (me + d) % cols
-            pltpu.make_async_copy(piece(got, peer), piece(got, peer), a2a_r.at[j, peer]).wait()
-            return carry
-
-        lax.fori_loop(1, cols, took, 0)
-
-        def unpack(s, carry):
+        pltpu.make_async_copy(got.at[others], got.at[others], a2a_r.at[j]).wait()
+
+        def unpack(s):
             moved = tab[MOVED, s].astype(f32)
             away = got[tab[FROM_MSG, s]].astype(f32)
             here = mix_o[j, tab[FROM_MIX, s]].astype(f32)
             value = jnp.where(moved > 0.5, away, here)
             mixed[s, :, j * 128 : (j + 1) * 128] = value.astype(bf16)
-            return carry
-
-        lax.fori_loop(0, requests, unpack, 0)
+
+        unrolled(requests, 8, unpack)
     for k in range(rows - 1):
         pltpu.make_async_copy(ss, ss, ss_s.at[k]).wait()
         pltpu.make_async_copy(part_o.at[0], part_o.at[0], yo_s.at[k + 1]).wait()
         for j in range(pieces):
             pltpu.make_async_copy(part_c.at[0, j], part_c.at[0, j], yc_s.at[j, k + 1]).wait()
     for j in range(pieces):
-
-        def gone(d, carry):
-            peer = (me + d) % cols
-            pltpu.make_async_copy(
-                piece(packed.at[j], peer), piece(packed.at[j], peer), a2a_s.at[j, peer]
-            ).wait()
-            return carry
-
-        lax.fori_loop(1, cols, gone, 0)
+        pltpu.make_async_copy(gots[j].at[others], gots[j].at[others], a2a_s.at[j]).wait()
     keep_x.wait()
     keep_e.wait()
 
-    def factors(d, carry):
-        peer = (me + d) % cols
-        for ref, s_, r_ in ((xgot, x_s, x_r), (egot, e_s, e_r)):
-            pltpu.make_async_copy(piece(ref, peer), piece(ref, peer), r_.at[peer]).wait()
-            pltpu.make_async_copy(piece(ref, peer), piece(ref, peer), s_.at[peer]).wait()
-        return carry
-
-    lax.fori_loop(1, cols, factors, 0)
+    for ref, s_, r_ in ((xgot, x_s, x_r), (egot, e_s, e_r)):
+        pltpu.make_async_copy(ref.at[others], ref.at[others], r_).wait()
+        pltpu.make_async_copy(ref.at[others], ref.at[others], s_).wait()
 
     @pl.loop(0, held)
     def _(s):
@@ -924,8 +889,8 @@
             dma(()), dma(()), dma((fa.shape[1] // 256 + 3,)), dma((held,)),
             dma((len(vectors) + 3,)), dma((2 + pieces,)), dma((3,)), dma((rows,)),
             dma((rows,)), dma((rows,)), dma((pieces, rows)), dma((rows, pieces)),
-            dma((pieces, cols)), dma((pieces, cols)),
-            dma((cols,)), dma((cols,)), dma((cols,)), dma((cols,)),
+            dma((pieces,)), dma((pieces,)),
+            dma(()), dma(()), dma(()), dma(()),
         ],
         compiler_params=pltpu.CompilerParams(
             collective_id=1, has_side_effects=True, vmem_limit_bytes=60 << 20
@@ -936,14 +901,14 @@
 
 def arrive_kernel(
     tab_in, xgot_in, egot_in, edge_in, nst_in, nst, nex, neb,
-    tab, xgot, egot, edge, xs, bs, ex, eb, new, n_sem, m_sem, l_sem,
+    tab, xgot, egot, edge, was, xs, bs, ex, eb, new, n_sem, m_sem, l_sem,
 ):
     f32, bf16 = jnp.float32, jnp.bfloat16
     count, inner = new.shape[0], new.shape[1]
     loads = [
         pltpu.make_async_copy(a, b, l_sem.at[k])
         for k, (a, b) in enumerate(
-            ((tab_in, tab), (xgot_in, xgot), (egot_in, egot), (edge_in, edge))
+            ((tab_in, tab), (xgot_in, xgot), (nst_in, was), (egot_in, egot), (edge_in, edge))
         )
     ]
     for copy in loads:
@@ -951,13 +916,15 @@
     loads[0].wait()
 
     def place(s):
-        return pltpu.make_async_copy(nst_in.at[s], nst.at[tab[POS, s]], m_sem.at[s])
+        return pltpu.make_async_copy(was.at[s], nst.at[tab[POS, s]], m_sem.at[s])
+
+    loads[1].wait()
+    loads[2].wait()
 
     @pl.loop(0, count)
     def _(s):
         place(s).start()
 
-    loads[1].wait()
     t_ids, _ = token_masks()
     none = jnp.zeros((TOK, STATE), bf16)
 
@@ -986,7 +953,7 @@
                 new[u] = out[:, k * STATE : (k + 1) * STATE]
                 store(u).start()
 
-    for copy in loads[2:]:
+    for copy in loads[3:]:
         copy.wait()
 
     @pl.loop(0, count)
@@ -1029,6 +996,7 @@
             pltpu.VMEM(xgot.shape, dt),
             pltpu.VMEM(egot.shape, dt),
             pltpu.VMEM(edge.shape, dt),
+            pltpu.VMEM(nst.shape, dt),
             pltpu.VMEM((GROUP, LEN, inner), dt),
             pltpu.VMEM((GROUP, LEN, STATE), dt),
             pltpu.VMEM((3, requests, inner), f32),
@@ -1036,7 +1004,7 @@
             pltpu.VMEM((count, inner, STATE), dt),
             pltpu.SemaphoreType.DMA((count,)),
             pltpu.SemaphoreType.DMA((count,)),
-            pltpu.SemaphoreType.DMA((4,)),
+            pltpu.SemaphoreType.DMA((5,)),
         ],
         compiler_params=pltpu.CompilerParams(vmem_limit_bytes=60 << 20),
         name="arrive",

time: 208 us -> 108 us (0.52)
  Pallas kernels: 205 us -> 105 us
    pallas_call x1, Pallas kernels: 98.5 us -> 6.11 us  [arrive(): pl.pallas_call(arrive_kernel, out_shape=(jax.ShapeDtypeStruct((requests,...]
    pallas_call x1, Pallas kernels: 63.4 us -> 57.9 us  [mixer(): pl.pallas_call(body, out_shape=(jax.ShapeDtypeStruct((requests, LEN, widt...]
    pallas_call x1, Pallas kernels: 41 us -> 38.8 us  [gather_all(): pl.pallas_call(body, out_shape=(jax.ShapeDtypeStruct((held, LEN, model),...]
where the time goes in v6:
time: 108 us
  Pallas kernels  105 us (97%)
  local copies, waits for them, and re-layouts  1.5 us (1%)
    pallas_call x1, Pallas kernels, mixer(): pl.pallas_call(body, out_shape=(jax.ShapeDtypeStruct((requests, LEN, widt...  57.9 us
    pallas_call x1, Pallas kernels, gather_all(): pl.pallas_call(body, out_shape=(jax.ShapeDtypeStruct((held, LEN, model),...  38.8 us
    pallas_call x1, Pallas kernels, arrive(): pl.pallas_call(arrive_kernel, out_shape=(jax.ShapeDtypeStruct((requests,...  6.11 us

profile of v6, /device:TPU:1, one launch (start us, length us, event | category | flops | bytes accessed | tf_op | source)
XLA Modules:
  0.0 107.5 jit_solution(8923441451354039836)
XLA Ops:
  0.6 0.7 multiply_add_fusion
  1.4 0.7 reshape.23.refs_0_
  2.1 1.8 %route.1.refs_0_.tab_in = s32[16,128]{1,0:T(8,128)} custom-call(s32[32,48]{1,0:T(8,128)} %reshape.23.refs_0_), custom_call_target="tpu_custom_call" | custom-call | tf_op jit(solution)/shard_map/route/pallas_call | solution.py:123
  3.8 38.8 %gather_all.1 = (bf16[24,16,1536]{2,1,0:T(8,128)(2,1)}, bf16[1536,1024]{1,0:T(8,128)(2,1)}, bf16[1536,896]{1,0:T(8,128)(2,1)}) custom-call(s32[16,128]{1,0:T(8,128)} %route.1.refs_0_.tab_in, bf16[48,16,1536]{2,1,0:T(8,128)(2,1)} %bitcast.15, bf16[48,1024]{1,0:T(8,128)(2,1)} %refs_2_.1, bf16[48,512]{1,0:T(8,128)(2,1)} %refs_3_.1, bf16[48,256]{1,0:T(8,128)(2,1)} %refs_4_.1, ...), custom_call_target="tpu_custom_call" | custom-call | tf_op jit(solution)/shard_map/gather_all/pallas_call | solution.py:361
  42.7 57.9 %mixer.1 = (bf16[48,16,384]{2,1,0:T(8,128)(2,1)}, bf16[24,512,128]{2,1,0:T(8,128)(2,1)}, bf16[24,4,768]{2,1,0:T(4,128)(2,1)}, bf16[64,16,640]{2,1,0:T(8,128)(2,1)}, bf16[64,4,768]{2,1,0:T(4,128)(2,1)}) custom-call(s32[16,128]{1,0:T(8,128)} %route.1.refs_0_.tab_in, bf16[24,16,1536]{2,1,0:T(8,128)(2,1)} %get-tuple-element.15.refs_1_, ...), custom_call_target="tpu_custom_call" | custom-call | tf_op jit(solution)/shard_map/mixer/pallas_call | solution.py:841
  100.6 0.0 copy-start
  100.6 6.1 %arrive.1 = (bf16[48,512,128]{2,1,0:T(8,128)(2,1)}, bf16[3,48,512]{2,1,0:T(8,128)(2,1)}, bf16[3,48,256]{2,1,0:T(8,128)(2,1)}) custom-call(s32[16,128]{1,0:T(8,128)} %route.1.refs_0_.tab_in, bf16[64,16,640]{2,1,0:T(8,128)(2,1)} %get-tuple-element.19.xgot_in, bf16[64,4,768]{2,1,0:T(4,128)(2,1)} %get-tuple-element.20.egot_in, ...), custom_call_target="tpu_custom_call" | custom-call | tf_op jit(solution)/shard_map/arrive/pallas_call | solution.py:985
  106.7 0.0 copy-done
  106.7 0.8 copy.24
Async XLA Ops:
  100.6 6.1 %copy-start = (bf16[48,16,384]{2,1,0:T(8,128)(2,1)S(1)}, bf16[48,16,384]{2,1,0:T(8,128)(2,1)}, u32[]{:S(2)}) copy-start(bf16[48,16,384]{2,1,0:T(8,128)(2,1)} %get-tuple-element.18) | copy-start | bytes 1769476

commit v7 on v6

--- a/solution.py
+++ b/solution.py
@@ -406,7 +406,7 @@
     (
         pex, peb, hid, home, wa, wb, wo, old, gate, xin, bc, dts, gg, ss, cx, cb, pexf, pebf, es,
         new, sent, edge_o, xmsg, emsg, part_o, part_c, came_o, came_c, ss_in, scale, mix_o,
-        mix0, mix1, mix2, packed, got0, got1, got2,
+        mix, packed, got,
         h_sem, o_sem, w_sem, n_sem, v_sem, loc, ss_s, ss_r, yo_s, yo_r, yc_s, yc_r,
         a2a_s, a2a_r, x_s, x_r, e_s, e_r,
     ) = refs
@@ -636,8 +636,8 @@
     load_out.wait()
     moving = held * LEN
     resting = tokens - moving
-    pieces = part_c.shape[1]
-    width = pieces * 128
+    width = part_c.shape[2]
+    pieces = width // 128
     order = (1, 3, 2)
 
     def project(lines, peer, j, count):
@@ -649,10 +649,9 @@
     def rest_block(peer):
         part_o[peer] = project(slice(moving, tokens), peer, 0, pieces)
 
-    def move_block(peer, j, count):
-        out = project(slice(0, moving), peer, j, count)
-        for k in range(count):
-            part_c[peer, j + k] = out[:, k * 128 : (k + 1) * 128]
+    def move_block(i, peer):
+        lines = pl.ds(pl.multiple_of(i * TOK, TOK), TOK)
+        part_c[peer, lines, :] = project(lines, peer, 0, pieces)
 
     def piece(ref, c):
         return ref.at[pl.ds(c * cap, cap)]
@@ -681,6 +680,28 @@
     keep_x.start()
     keep_e.start()
 
+    @pl.loop(0, held // GROUP)
+    def _(i):
+        group(i, True)
+
+        def send_moved(d, carry):
+            peer = (row + d) % rows
+            move_block(i, peer)
+            at = pl.ds(pl.multiple_of(i * TOK, TOK), TOK)
+            pltpu.make_async_remote_copy(
+                part_c.at[peer, at], came_c.at[row, at], yc_s.at[d, i], yc_r.at[row, i],
+                device_id=(peer, me), device_id_type=MESH,
+            ).start()
+            return carry
+
+        lax.fori_loop(1, rows, send_moved, 0)
+
+    for k, d in enumerate(order):
+        pltpu.make_async_remote_copy(
+            ss, ss_in.at[row], ss_s.at[k], ss_r.at[row],
+            device_id=((row + d) % rows, me), device_id_type=MESH,
+        ).start()
+
     def send_rest(d, carry):
         peer = (row + d) % rows
         rest_block(peer)
@@ -692,39 +713,8 @@
 
     lax.fori_loop(1, rows, send_rest, 0)
 
-    @pl.loop(0, held // GROUP)
-    def _(i):
-        group(i, True)
-
-    for k, d in enumerate(order):
-        pltpu.make_async_remote_copy(
-            ss, ss_in.at[row], ss_s.at[k], ss_r.at[row],
-            device_id=((row + d) % rows, me), device_id_type=MESH,
-        ).start()
-
-    def send_block(peer, j, d):
-        pltpu.make_async_remote_copy(
-            part_c.at[peer, j], came_c.at[row, j], yc_s.at[j, d], yc_r.at[row, j],
-            device_id=(peer, me), device_id_type=MESH,
-        ).start()
-
-    def first_block(d, carry):
-        peer = (row + d) % rows
-        move_block(peer, 0, 1)
-        send_block(peer, 0, d)
-        return carry
-
-    def later_blocks(d, carry):
-        peer = (row + d) % rows
-        move_block(peer, 1, pieces - 1)
-        for j in range(1, pieces):
-            send_block(peer, j, d)
-        return carry
-
-    lax.fori_loop(1, rows, first_block, 0)
-    lax.fori_loop(1, rows, later_blocks, 0)
-    move_block(row, 0, 1)
-    move_block(row, 1, pieces - 1)
+    for i in range(held // GROUP):
+        move_block(i, row)
     rest_block(row)
     total = ss[...]
     for d in order:
@@ -735,76 +725,66 @@
     for i in range(tokens // TOK):
         line = jnp.broadcast_to(factor[i : i + 1, :], (TOK, TOK))
         scale[pl.ds(i * TOK, TOK), :] = line.T
+
+    def add(part, came, into, start, count):
+        def some(i, carry):
+            at = pl.ds(pl.multiple_of(i * TOK, TOK), TOK)
+            by = scale[pl.ds(pl.multiple_of(start + i * TOK, TOK), TOK), :]
+            for j in range(pieces):
+                lanes = slice(j * 128, (j + 1) * 128)
+                value = part[row, at, lanes].astype(f32)
+                for d in order:
+                    value = value + came[(row + d) % rows, at, lanes].astype(f32)
+                value = (value * by).astype(bf16)
+                into[pl.ds(i * GROUP, GROUP), :, lanes] = value.reshape(GROUP, LEN, 128)
+            return carry
+
+        lax.fori_loop(0, count // TOK, some, 0)
+
+    for i in range(held // GROUP):
+        at = pl.ds(i * TOK, TOK)
+        for d in order:
+            spot = came_c.at[(row + d) % rows, at]
+            pltpu.make_async_copy(spot, spot, yc_r.at[(row + d) % rows, i]).wait()
+    add(part_c, came_c, mix, 0, moving)
+
+    def pack(q):
+        packed[q] = mix[tab[BACK, q]]
+
+    unrolled(cols * cap, 8, pack)
+
+    def push(d, carry):
+        peer = (me + d) % cols
+        pltpu.make_async_remote_copy(
+            piece(packed, peer), piece(got, me), a2a_s, a2a_r,
+            device_id=(row, peer), device_id_type=MESH,
+        ).start()
+        return carry
+
+    lax.fori_loop(1, cols, push, 0)
+    keep_m = pltpu.make_async_copy(piece(packed, me), piece(got, me), loc.at[2])
+    keep_m.start()
     for d in order:
-        peer = (row + d) % rows
-        pltpu.make_async_copy(came_o.at[peer], came_o.at[peer], yo_r.at[peer]).wait()
-
-    def add_rest(i, carry):
-        at = pl.ds(pl.multiple_of(i * TOK, TOK), TOK)
-        by = scale[pl.ds(pl.multiple_of(moving + i * TOK, TOK), TOK), :]
-        for j in range(pieces):
-            lanes = slice(j * 128, (j + 1) * 128)
-            value = part_o[row, at, lanes].astype(f32)
-            for d in order:
-                value = value + came_o[(row + d) % rows, at, lanes].astype(f32)
-            mix_o[j, pl.ds(i * GROUP, GROUP)] = (value * by).astype(bf16).reshape(GROUP, LEN, 128)
-        return carry
-
-    lax.fori_loop(0, resting // TOK, add_rest, 0)
-    gots, mixes = (got0, got1, got2), (mix0, mix1, mix2)
-    for j in range(pieces):
-        mix = mixes[j]
-        for d in order:
-            peer = (row + d) % rows
-            pltpu.make_async_copy(came_c.at[peer, j], came_c.at[peer, j], yc_r.at[peer, j]).wait()
-
-        def add(i, carry):
-            at = pl.ds(pl.multiple_of(i * TOK, TOK), TOK)
-            value = part_c[row, j, at, :].astype(f32)
-            for d in order:
-                value = value + came_c[(row + d) % rows, j, at, :].astype(f32)
-            value = (value * scale[at, :]).astype(bf16)
-            mix[pl.ds(i * GROUP, GROUP)] = value.reshape(GROUP, LEN, 128)
-            return carry
-
-        lax.fori_loop(0, moving // TOK, add, 0)
-
-        def pack(q):
-            packed[j, q] = mix[tab[BACK, q]]
-
-        unrolled(cols * cap, 16, pack)
-
-        def push(d, carry):
-            peer = (me + d) % cols
-            pltpu.make_async_remote_copy(
-                piece(packed.at[j], peer), piece(gots[j], me), a2a_s.at[j], a2a_r.at[j],
-                device_id=(row, peer), device_id_type=MESH,
-            ).start()
-            return carry
-
-        lax.fori_loop(1, cols, push, 0)
-        pltpu.make_async_copy(piece(packed.at[j], me), piece(gots[j], me), loc.at[2 + j]).start()
-    for j in range(pieces):
-        got = gots[j]
-        pltpu.make_async_copy(piece(packed.at[j], me), piece(got, me), loc.at[2 + j]).wait()
-
-        pltpu.make_async_copy(got.at[others], got.at[others], a2a_r.at[j]).wait()
-
-        def unpack(s):
-            moved = tab[MOVED, s].astype(f32)
-            away = got[tab[FROM_MSG, s]].astype(f32)
-            here = mix_o[j, tab[FROM_MIX, s]].astype(f32)
-            value = jnp.where(moved > 0.5, away, here)
-            mixed[s, :, j * 128 : (j + 1) * 128] = value.astype(bf16)
-
-        unrolled(requests, 8, unpack)
+        spot = came_o.at[(row + d) % rows]
+        pltpu.make_async_copy(spot, spot, yo_r.at[(row + d) % rows]).wait()
+    add(part_o, came_o, mix_o, moving, resting)
+    keep_m.wait()
+    pltpu.make_async_copy(got.at[others], got.at[others], a2a_r).wait()
+
+    def unpack(s):
+        moved = tab[MOVED, s].astype(f32)
+        away = got[tab[FROM_MSG, s]].astype(f32)
+        here = mix_o[tab[FROM_MIX, s]].astype(f32)
+        mixed[s] = jnp.where(moved > 0.5, away, here).astype(bf16)
+
+    unrolled(requests, 8, unpack)
     for k in range(rows - 1):
         pltpu.make_async_copy(ss, ss, ss_s.at[k]).wait()
         pltpu.make_async_copy(part_o.at[0], part_o.at[0], yo_s.at[k + 1]).wait()
-        for j in range(pieces):
-            pltpu.make_async_copy(part_c.at[0, j], part_c.at[0, j], yc_s.at[j, k + 1]).wait()
-    for j in range(pieces):
-        pltpu.make_async_copy(gots[j].at[others], gots[j].at[others], a2a_s.at[j]).wait()
+        for i in range(held // GROUP):
+            spot = part_c.at[0, pl.ds(i * TOK, TOK)]
+            pltpu.make_async_copy(spot, spot, yc_s.at[k + 1, i]).wait()
+    pltpu.make_async_copy(got.at[others], got.at[others], a2a_s).wait()
     keep_x.wait()
     keep_e.wait()
 
@@ -823,7 +803,6 @@
     tokens = requests * LEN
     inner = fa.shape[1] // 2
     width = model // rows
-    pieces = width // 128
     slots = cols * cap
     rest = requests - held
     dt = hidden.dtype
@@ -836,8 +815,6 @@
         mixer_kernel(rows, cols, cap, held, *refs)
 
     wide = inner + 2 * STATE
-    mix = pltpu.VMEM((held, LEN, 128), dt)
-    got = pltpu.VMEM((slots, LEN, 128), dt)
     return pl.pallas_call(
         body,
         out_shape=(
@@ -877,19 +854,19 @@
             pltpu.VMEM((slots, LEN, inner + STATE), dt),
             pltpu.VMEM((slots, 4, wide), dt),
             pltpu.VMEM((rows, rest * LEN, width), dt),
-            pltpu.VMEM((rows, pieces, held * LEN, 128), dt),
+            pltpu.VMEM((rows, held * LEN, width), dt),
             pltpu.VMEM((rows, rest * LEN, width), dt),
-            pltpu.VMEM((rows, pieces, held * LEN, 128), dt),
+            pltpu.VMEM((rows, held * LEN, width), dt),
             pltpu.VMEM((rows, 8, 128), f32),
             pltpu.VMEM((tokens, 128), f32),
-            pltpu.VMEM((pieces, rest, LEN, 128), dt),
-            mix, mix, mix,
-            pltpu.VMEM((pieces, slots, LEN, 128), dt),
-            got, got, got,
+            pltpu.VMEM((rest, LEN, width), dt),
+            pltpu.VMEM((held, LEN, width), dt),
+            pltpu.VMEM((slots, LEN, width), dt),
+            pltpu.VMEM((slots, LEN, width), dt),
             dma(()), dma(()), dma((fa.shape[1] // 256 + 3,)), dma((held,)),
-            dma((len(vectors) + 3,)), dma((2 + pieces,)), dma((3,)), dma((rows,)),
-            dma((rows,)), dma((rows,)), dma((pieces, rows)), dma((rows, pieces)),
-            dma((pieces,)), dma((pieces,)),
+            dma((len(vectors) + 3,)), dma((3,)), dma((3,)), dma((rows,)),
+            dma((rows,)), dma((rows,)), dma((rows, held // GROUP)), dma((rows, held // GROUP)),
+            dma(()), dma(()),
             dma(()), dma(()), dma(()), dma(()),
         ],
         compiler_params=pltpu.CompilerParams(

time: 108 us -> 105 us (0.972); the launches traced: 108 us -> 103 us
  Pallas kernels: 105 us -> 100 us
    pallas_call x1, Pallas kernels: 57.9 us -> 53.6 us  [mixer(): pl.pallas_call(body, out_shape=(jax.ShapeDtypeStruct((requests, LEN, widt...]
where the time goes in v7:
time: 105 us; the launch traced here: 103 us
  Pallas kernels  100 us (95%)
  local copies, waits for them, and re-layouts  1.5 us (1%)
    pallas_call x1, Pallas kernels, mixer(): pl.pallas_call(body, out_shape=(jax.ShapeDtypeStruct((requests, LEN, widt...  53.6 us
    pallas_call x1, Pallas kernels, gather_all(): pl.pallas_call(body, out_shape=(jax.ShapeDtypeStruct((held, LEN, model),...  38.8 us
    pallas_call x1, Pallas kernels, arrive(): pl.pallas_call(arrive_kernel, out_shape=(jax.ShapeDtypeStruct((requests,...  6.11 us

profile of v7, /device:TPU:1, one launch (start us, length us, event | category | flops | bytes accessed | tf_op | source)
XLA Modules:
  0.0 103.3 jit_solution(4468761446324584092)
XLA Ops:
  0.6 0.7 multiply_add_fusion
  1.4 0.7 reshape.23.refs_0_
  2.1 1.8 %route.1.refs_0_.tab_in = s32[16,128]{1,0:T(8,128)} custom-call(s32[32,48]{1,0:T(8,128)} %reshape.23.refs_0_), custom_call_target="tpu_custom_call" | custom-call | tf_op jit(solution)/shard_map/route/pallas_call | solution.py:123
  3.8 38.8 %gather_all.1 = (bf16[24,16,1536]{2,1,0:T(8,128)(2,1)}, bf16[1536,1024]{1,0:T(8,128)(2,1)}, bf16[1536,896]{1,0:T(8,128)(2,1)}) custom-call(s32[16,128]{1,0:T(8,128)} %route.1.refs_0_.tab_in, bf16[48,16,1536]{2,1,0:T(8,128)(2,1)} %bitcast.15, bf16[48,1024]{1,0:T(8,128)(2,1)} %refs_2_.1, bf16[48,512]{1,0:T(8,128)(2,1)} %refs_3_.1, bf16[48,256]{1,0:T(8,128)(2,1)} %refs_4_.1, ...), custom_call_target="tpu_custom_call" | custom-call | tf_op jit(solution)/shard_map/gather_all/pallas_call | solution.py:361
  42.7 53.6 %mixer.1 = (bf16[48,16,384]{2,1,0:T(8,128)(2,1)}, bf16[24,512,128]{2,1,0:T(8,128)(2,1)}, bf16[24,4,768]{2,1,0:T(4,128)(2,1)}, bf16[64,16,640]{2,1,0:T(8,128)(2,1)}, bf16[64,4,768]{2,1,0:T(4,128)(2,1)}) custom-call(s32[16,128]{1,0:T(8,128)} %route.1.refs_0_.tab_in, bf16[24,16,1536]{2,1,0:T(8,128)(2,1)} %get-tuple-element.15.refs_1_, ...), custom_call_target="tpu_custom_call" | custom-call | tf_op jit(solution)/shard_map/mixer/pallas_call | solution.py:818
  96.3 0.0 copy-start
  96.3 6.1 %arrive.1 = (bf16[48,512,128]{2,1,0:T(8,128)(2,1)}, bf16[3,48,512]{2,1,0:T(8,128)(2,1)}, bf16[3,48,256]{2,1,0:T(8,128)(2,1)}) custom-call(s32[16,128]{1,0:T(8,128)} %route.1.refs_0_.tab_in, bf16[64,16,640]{2,1,0:T(8,128)(2,1)} %get-tuple-element.19.xgot_in, bf16[64,4,768]{2,1,0:T(4,128)(2,1)} %get-tuple-element.20.egot_in, ...), custom_call_target="tpu_custom_call" | custom-call | tf_op jit(solution)/shard_map/arrive/pallas_call | solution.py:962
  102.4 0.0 copy-done
  102.4 0.8 copy.24
Async XLA Ops:
  96.3 6.1 %copy-start = (bf16[48,16,384]{2,1,0:T(8,128)(2,1)S(1)}, bf16[48,16,384]{2,1,0:T(8,128)(2,1)}, u32[]{:S(2)}) copy-start(bf16[48,16,384]{2,1,0:T(8,128)(2,1)} %get-tuple-element.18) | copy-start | bytes 1769476

commit v8 on v7

--- a/solution.py
+++ b/solution.py
@@ -157,203 +157,254 @@
     return barrier
 
 
+def torus_ring(row, me, depth, block, own, span, gone, twin, came):
+    core = me % 2
+    x = (me // 2) % SIDE
+    z = me // (2 * SIDE)
+    a = x + core * (z - x)
+    b = z + core * (x - z)
+
+    def at(pa, pb):
+        pa, pb = (pa + SIDE) % SIDE, (pb + SIDE) % SIDE
+        px = pa + core * (pb - pa)
+        pz = pb + core * (pa - pb)
+        return (pz * SIDE + px) * 2 + core
+
+    sibling = me + 1 - 2 * core
+    sent = [0, 0]
+
+    def send(h, source, c, dest):
+        sent[h] += 1
+        arrival = twin.at[h] if dest is sibling else came.at[h, c]
+        pltpu.make_async_remote_copy(
+            source, block(h, c), gone.at[h], arrival,
+            device_id=(row, dest), device_id_type=MESH,
+        ).start()
+
+    def forward(h, c, dest):
+        send(h, block(h, c), c, dest)
+
+    def arrived(h, c):
+        pltpu.make_async_copy(block(h, c), block(h, c), came.at[h, c]).wait()
+
+    up, down, far = at(a + 1, b), at(a - 1, b), at(a + 2, b)
+    over, under = at(a, b + 1), at(a, b - 1)
+
+    def begin():
+        for dest in (up, down, over, under, sibling):
+            for h in (0, 1):
+                send(h, own(h), me, dest)
+
+    def near():
+        arrived(0, down)
+        forward(0, down, up)
+        arrived(1, up)
+        forward(1, up, down)
+        arrived(1, down)
+        arrived(0, up)
+        for c in (down, up):
+            for h in (0, 1):
+                for dest in (over, under, sibling):
+                    forward(h, c, dest)
+
+    def beyond():
+        for h in (0, 1):
+            arrived(h, far)
+            for dest in (over, under, sibling):
+                forward(h, far, dest)
+
+    def beside():
+        for k in (0, 1, -1, 2):
+            low, high = at(a + k, b - 1), at(a + k, b + 1)
+            arrived(0, low)
+            forward(0, low, over)
+            arrived(1, high)
+            forward(1, high, under)
+            arrived(1, low)
+            arrived(0, high)
+            for h in (0, 1):
+                forward(h, low, sibling)
+                forward(h, high, sibling)
+
+    def opposite():
+        for k in (0, 1, -1, 2):
+            c = at(a + k, b + 2)
+            for h in (0, 1):
+                arrived(h, c)
+                forward(h, c, sibling)
+
+    def finish():
+        for h in (0, 1):
+            half = span(h, 16 * depth)
+            pltpu.make_async_copy(half, half, twin.at[h]).wait()
+        for h in (0, 1):
+            part = span(h, sent[h] * depth)
+            pltpu.make_async_copy(part, part, gone.at[h]).wait()
+
+    return begin, near, beyond, beside, opposite, finish
+
+
 def gather_kernel(
-    rows, cols, cap, tab_in, hidden, wa, w_out, w_bc, w_dt_in, hid_full, fa, fb,
-    tab, w_dt, wb, sl, packed, got, own, loc, a2a_s, a2a_r, gone, twin, war, wbr, y_s, y_r,
+    rows, cols, cap, tab_in, hidden, w_zx, w_bc, w_dt_in, hid_full, fw,
+    tab, w_dt, ws, sl, packed0, packed1, got0, got1, own0, own1, loc, a2a_s, a2a_r, gone, twin, arr, y_s, y_r,
 ):
     row, me = lax.axis_index("row"), lax.axis_index("col")
     barrier = greet(row, me, rows, cols)
     width = sl.shape[2]
-    half = own.shape[0] // 2
-    depth = wa.shape[0]
+    half = own0.shape[0] // 2
+    packs, gots, owns = (packed0, packed1), (got0, got1), (own0, own1)
+    lows = (0, packed0.shape[2])
+    depth = w_zx.shape[0]
 
     def cols_of(r):
         return pl.ds(pl.multiple_of(r * width, 128), width)
 
-    def block(ref, c):
-        return ref.at[pl.ds(pl.multiple_of(c * depth, 16), depth), :]
+    cut = 128 * (ws.shape[1] // 256)
+    lanes_of = (pl.ds(0, cut), pl.ds(cut, ws.shape[1] - cut))
+
+    def lines(c):
+        return pl.ds(pl.multiple_of(c * depth, 16), depth)
+
+    ring = torus_ring(
+        row, me, depth,
+        lambda h, c: fw.at[lines(c), lanes_of[h]],
+        lambda h: ws.at[:, lanes_of[h]],
+        lambda h, count: fw.at[pl.ds(0, count), lanes_of[h]],
+        gone, twin, arr,
+    )
+    begin, near, beyond, beside, opposite, finish = ring
 
     load = pltpu.make_async_copy(hidden.at[:, :, cols_of(row)], sl, loc.at[0])
     load.start()
-    inner = w_out.shape[1]
+    inner = w_zx.shape[1]
     states = w_bc.shape[1]
     heads = w_dt_in.shape[0]
     loads = (
         pltpu.make_async_copy(tab_in, tab, loc.at[5]),
         pltpu.make_async_copy(w_dt_in, w_dt, loc.at[6]),
-        pltpu.make_async_copy(w_out, wb.at[:, pl.ds(0, inner)], loc.at[7]),
-        pltpu.make_async_copy(w_bc, wb.at[:, pl.ds(inner, states)], loc.at[8]),
+        pltpu.make_async_copy(w_zx, ws.at[:, pl.ds(0, inner)], loc.at[7]),
+        pltpu.make_async_copy(w_bc, ws.at[:, pl.ds(inner, states)], loc.at[8]),
     )
     for copy in loads:
         copy.start()
     for copy in loads:
         copy.wait()
-    square = jnp.concatenate([w_dt[...].astype(jnp.float32), jnp.zeros((heads, 128 - depth), jnp.float32)], axis=1)
+    square = jnp.concatenate(
+        [w_dt[...].astype(jnp.float32), jnp.zeros((heads, 128 - depth), jnp.float32)], axis=1
+    )
     square = jnp.concatenate([square, jnp.zeros((128 - heads, 128), jnp.float32)], axis=0).T
-    wb[:, inner + states :] = square[:depth, :].astype(wb.dtype)
-    keep_a = pltpu.make_async_copy(wa, block(fa, me), loc.at[1])
-    keep_b = pltpu.make_async_copy(wb, block(fb, me), loc.at[2])
-    keep_a.start()
-    keep_b.start()
+    ws[:, inner + states :] = square[:depth, :].astype(ws.dtype)
+    keep_w = pltpu.make_async_copy(ws, fw.at[lines(me), :], loc.at[1])
+    keep_w.start()
     load.wait()
-
-    def pack(s):
-        packed[s] = sl[tab[SEND, s]]
-
-    unrolled(cols * cap, 8, pack)
-    pl.semaphore_wait(barrier, cols - 1 + rows - 1)
 
     def piece(ref, c):
         return ref.at[pl.ds(c * cap, cap)]
 
-    def push(d, carry):
-        peer = (me + d) % cols
-        pltpu.make_async_remote_copy(
-            piece(packed, peer), piece(got, me), a2a_s, a2a_r,
-            device_id=(row, peer), device_id_type=MESH,
-        ).start()
-        return carry
-
-    lax.fori_loop(1, cols, push, 0)
-    keep_m = pltpu.make_async_copy(piece(packed, me), piece(got, me), loc.at[3])
-    keep_m.start()
-
-    core = me % 2
-    x = (me // 2) % SIDE
-    z = me // (2 * SIDE)
-    a = x + core * (z - x)
-    b = z + core * (x - z)
-
-    def at(pa, pb):
-        pa, pb = (pa + SIDE) % SIDE, (pb + SIDE) % SIDE
-        px = pa + core * (pb - pa)
-        pz = pb + core * (pa - pb)
-        return (pz * SIDE + px) * 2 + core
-
-    sibling = me + 1 - 2 * core
-    sent = [0, 0]
-
-    def send(which, src, c, dest):
-        full, rs = ((fa, war), (fb, wbr))[which]
-        sent[which] += 1
-        rs = twin.at[which] if dest is sibling else rs.at[c]
-        pltpu.make_async_remote_copy(
-            src, block(full, c), gone.at[which], rs,
-            device_id=(row, dest), device_id_type=MESH,
-        ).start()
-
-    def forward(which, c, dest):
-        send(which, block((fa, fb)[which], c), c, dest)
-
-    def arrived(which, c):
-        full, rs = ((fa, war), (fb, wbr))[which]
-        pltpu.make_async_copy(block(full, c), block(full, c), rs.at[c]).wait()
-
-    up, down = at(a + 1, b), at(a - 1, b)
-    far = at(a + 2, b)
-    over, under = at(a, b + 1), at(a, b - 1)
-    for dest in (up, down, over, under, sibling):
-        for which, src in ((0, wa), (1, wb)):
-            send(which, src, me, dest)
-    arrived(0, down)
-    forward(0, down, up)
-    arrived(1, up)
-    forward(1, up, down)
-    arrived(1, down)
-    arrived(0, up)
-    for c in (down, up):
-        for which in (0, 1):
-            for dest in (over, under, sibling):
-                forward(which, c, dest)
-    keep_m.wait()
-
+    keeps = []
+    for k in (0, 1):
+        packed, got, low = packs[k], gots[k], lows[k]
+
+        def pack(s):
+            packed[s] = sl[tab[SEND, s], :, low : low + packed.shape[2]]
+
+        unrolled(cols * cap, 8, pack)
+        if k == 0:
+            pl.semaphore_wait(barrier, cols - 1 + rows - 1)
+
+        def push(d, carry):
+            peer = (me + d) % cols
+            pltpu.make_async_remote_copy(
+                piece(packed, peer), piece(got, me), a2a_s.at[k], a2a_r.at[k],
+                device_id=(row, peer), device_id_type=MESH,
+            ).start()
+            return carry
+
+        lax.fori_loop(1, cols, push, 0)
+        keeps.append(pltpu.make_async_copy(piece(packed, me), piece(got, me), loc.at[3 + 6 * k]))
+        keeps[k].start()
+
+    begin()
+    near()
     others = pl.ds(0, (cols - 1) * cap)
-    pltpu.make_async_copy(got.at[others], got.at[others], a2a_r).wait()
-
-    def unpack(s):
-        own[s] = got[tab[PICK, s]]
-
-    unrolled(own.shape[0], 8, unpack)
-
-    def part(ref, h, r):
-        return ref.at[pl.ds(h * half, half), :, cols_of(r)]
-
     right, left = (row + 1) % rows, (row + rows - 1) % rows
     far_row = (row + 2) % rows
-    for k, dest in ((0, right), (1, left)):
-        for h in (0, 1):
-            pltpu.make_async_remote_copy(
-                own.at[pl.ds(h * half, half)], part(hid_full, h, row),
-                y_s.at[2 * k + h], y_r.at[row, h],
-                device_id=(dest, me), device_id_type=MESH,
-            ).start()
-    keep_y = pltpu.make_async_copy(own, hid_full.at[:, :, cols_of(row)], loc.at[4])
-    keep_y.start()
-
-    for which in (0, 1):
-        arrived(which, far)
-        for dest in (over, under, sibling):
-            forward(which, far, dest)
-    for k in (0, 1, -1, 2):
-        low, high = at(a + k, b - 1), at(a + k, b + 1)
-        arrived(0, low)
-        forward(0, low, over)
-        arrived(1, high)
-        forward(1, high, under)
-        arrived(1, low)
-        arrived(0, high)
-        for which in (0, 1):
-            forward(which, low, sibling)
-            forward(which, high, sibling)
-
-    def y_here(h, r):
-        pltpu.make_async_copy(part(hid_full, h, r), part(hid_full, h, r), y_r.at[r, h]).wait()
-
-    y_here(0, left)
-    pltpu.make_async_remote_copy(
-        part(hid_full, 0, left), part(hid_full, 0, left), y_s.at[4], y_r.at[left, 0],
-        device_id=(right, me), device_id_type=MESH,
-    ).start()
-    y_here(1, right)
-    pltpu.make_async_remote_copy(
-        part(hid_full, 1, right), part(hid_full, 1, right), y_s.at[5], y_r.at[right, 1],
-        device_id=(left, me), device_id_type=MESH,
-    ).start()
-    y_here(1, left)
-    y_here(0, right)
-    for k in (0, 1, -1, 2):
-        opposite = at(a + k, b + 2)
-        for which in (0, 1):
-            arrived(which, opposite)
-            forward(which, opposite, sibling)
-    y_here(0, far_row)
-    y_here(1, far_row)
-
-    for which, ref in ((0, fa), (1, fb)):
-        lines = pl.ds(0, (cols // 2) * depth)
-        pltpu.make_async_copy(ref.at[lines, :], ref.at[lines, :], twin.at[which]).wait()
-    keep_a.wait()
-    keep_b.wait()
-    keep_y.wait()
-
-    pltpu.make_async_copy(packed.at[others], packed.at[others], a2a_s).wait()
-
-    for which, ref in ((0, fa), (1, fb)):
-        lines = pl.ds(0, sent[which] * depth)
-        pltpu.make_async_copy(ref.at[lines, :], ref.at[lines, :], gone.at[which]).wait()
-    for k in range(6):
-        h = (0, 1, 0, 1, 0, 1)[k]
-        pltpu.make_async_copy(part(hid_full, h, row), part(hid_full, h, row), y_s.at[k]).wait()
-
-
-def gather_all(tab, hidden, wa, w_out, w_bc, w_dt, rows, cols, cap, held):
+
+    def part(ref, k, h, r):
+        low, size = lows[k], owns[k].shape[2]
+        lanes = pl.ds(pl.multiple_of(r * width + low, 128), size)
+        return ref.at[pl.ds(h * half, half), :, lanes]
+
+    def y_here(k, h, r):
+        spot = part(hid_full, k, h, r)
+        pltpu.make_async_copy(spot, spot, y_r.at[k, r, h]).wait()
+
+    def pass_on(k, h, source, dest):
+        spot = part(hid_full, k, h, source)
+        pltpu.make_async_remote_copy(
+            spot, spot, y_s.at[k, 4 + h], y_r.at[k, source, h],
+            device_id=(dest, me), device_id_type=MESH,
+        ).start()
+
+    for k in (0, 1):
+        got, own = gots[k], owns[k]
+        keeps[k].wait()
+        pltpu.make_async_copy(got.at[others], got.at[others], a2a_r.at[k]).wait()
+
+        def unpack(s):
+            own[s] = got[tab[PICK, s]]
+
+        unrolled(own.shape[0], 8, unpack)
+        for n, dest in ((0, right), (1, left)):
+            for h in (n, 1 - n):
+                pltpu.make_async_remote_copy(
+                    own.at[pl.ds(h * half, half)], part(hid_full, k, h, row),
+                    y_s.at[k, 2 * n + h], y_r.at[k, row, h],
+                    device_id=(dest, me), device_id_type=MESH,
+                ).start()
+        lanes = pl.ds(pl.multiple_of(row * width + lows[k], 128), own.shape[2])
+        keeps.append(pltpu.make_async_copy(own, hid_full.at[:, :, lanes], loc.at[4 + 6 * k]))
+        keeps[2 + k].start()
+
+    beyond()
+    y_here(0, 0, left)
+    pass_on(0, 0, left, right)
+    y_here(0, 1, right)
+    pass_on(0, 1, right, left)
+    beside()
+    y_here(1, 0, left)
+    pass_on(1, 0, left, right)
+    y_here(1, 1, right)
+    pass_on(1, 1, right, left)
+    opposite()
+    for k in (0, 1):
+        y_here(k, 1, left)
+        y_here(k, 0, right)
+        y_here(k, 0, far_row)
+        y_here(k, 1, far_row)
+
+    finish()
+    keep_w.wait()
+    keeps[2].wait()
+    keeps[3].wait()
+
+    for k in (0, 1):
+        pltpu.make_async_copy(packs[k].at[others], packs[k].at[others], a2a_s.at[k]).wait()
+
+    for k in (0, 1):
+        for n in range(6):
+            spot = part(hid_full, k, n % 2, row)
+            pltpu.make_async_copy(spot, spot, y_s.at[k, n]).wait()
+
+
+def gather_all(tab, hidden, w_zx, w_bc, w_dt, rows, cols, cap, held):
     requests, _, model = hidden.shape
     width = model // rows
     dt = hidden.dtype
     hbm = pl.BlockSpec(memory_space=pltpu.HBM)
     dma = pltpu.SemaphoreType.DMA
-    depth = wa.shape[0]
-    rest = w_out.shape[1] + w_bc.shape[1] + 128
+    depth = w_zx.shape[0]
+    wide = w_zx.shape[1] + w_bc.shape[1] + 128
 
     def body(*refs):
         gather_kernel(rows, cols, cap, *refs)
@@ -362,28 +413,30 @@
         body,
         out_shape=(
             jax.ShapeDtypeStruct((held, LEN, model), dt),
-            jax.ShapeDtypeStruct((depth * cols, wa.shape[1]), dt),
-            jax.ShapeDtypeStruct((depth * cols, rest), dt),
+            jax.ShapeDtypeStruct((depth * cols, wide), dt),
         ),
-        in_specs=[hbm] * 6,
-        out_specs=(hbm, hbm, hbm),
+        in_specs=[hbm] * 5,
+        out_specs=(hbm, hbm),
         scratch_shapes=[
             pltpu.SMEM(tab.shape, jnp.int32),
             pltpu.VMEM(w_dt.shape, dt),
-            pltpu.VMEM((depth, rest), dt),
+            pltpu.VMEM((depth, wide), dt),
             pltpu.VMEM((requests, LEN, width), dt),
-            pltpu.VMEM((cols * cap, LEN, width), dt),
-            pltpu.VMEM((cols * cap, LEN, width), dt),
-            pltpu.VMEM((held, LEN, width), dt),
-            dma((9,)), dma(()), dma(()),
-            dma((2,)), dma((2,)), dma((cols,)), dma((cols,)),
-            dma((6,)), dma((rows, 2)),
+            pltpu.VMEM((cols * cap, LEN, 128), dt),
+            pltpu.VMEM((cols * cap, LEN, width - 128), dt),
+            pltpu.VMEM((cols * cap, LEN, 128), dt),
+            pltpu.VMEM((cols * cap, LEN, width - 128), dt),
+            pltpu.VMEM((held, LEN, 128), dt),
+            pltpu.VMEM((held, LEN, width - 128), dt),
+            dma((11,)), dma((2,)), dma((2,)),
+            dma((2,)), dma((2,)), dma((2, cols)),
+            dma((2, 6)), dma((2, rows, 2)),
         ],
         compiler_params=pltpu.CompilerParams(
             collective_id=0, has_side_effects=True, vmem_limit_bytes=60 << 20
         ),
         name="gather_all",
-    )(tab, hidden, wa, w_out, w_bc, w_dt)
+    )(tab, hidden, w_zx, w_bc, w_dt)
 
 
 def silu(v):
@@ -397,7 +450,7 @@
 
 
 def mixer_kernel(
-    rows, cols, cap, held, tab_in, hid_c, hidden, fa, fb, *refs,
+    rows, cols, cap, held, tab_in, hid_c, hidden, fw, w_out, *refs,
 ):
     sources, refs = refs[:8], refs[8:]
     prev, pex_in, peb_in, mixed, nst, edge_c, xgot, egot, tab, *refs = refs
@@ -408,10 +461,13 @@
         new, sent, edge_o, xmsg, emsg, part_o, part_c, came_o, came_c, ss_in, scale, mix_o,
         mix, packed, got,
         h_sem, o_sem, w_sem, n_sem, v_sem, loc, ss_s, ss_r, yo_s, yo_r, yc_s, yc_r,
-        a2a_s, a2a_r, x_s, x_r, e_s, e_r,
+        a2a_s, a2a_r, x_s, x_r, e_s, e_r, mine, gone, twin, arr,
     ) = refs
     row, me = lax.axis_index("row"), lax.axis_index("col")
     barrier = greet(row, me, rows, cols)
+    depth = w_out.shape[0]
+    load_mine = pltpu.make_async_copy(w_out, mine, loc.at[3])
+    load_mine.start()
     f32, bf16 = jnp.float32, jnp.bfloat16
     inner = gain.shape[1]
     requests = hid.shape[0]
@@ -419,6 +475,7 @@
     model = hid.shape[2]
     heads = inner // HEAD_DIM
     blocks = wa.shape[1] // 256
+    assert blocks == 4
 
     load_h = pltpu.make_async_copy(hid_c, hid.at[pl.ds(0, held)], h_sem)
     load_h.start()
@@ -431,7 +488,7 @@
 
     def wa_load(n):
         at = pl.ds(n * 256, 256)
-        return pltpu.make_async_copy(fa.at[:, at], wa.at[:, at], w_sem.at[n])
+        return pltpu.make_async_copy(fw.at[:, at], wa.at[:, at], w_sem.at[n])
 
     wa_load(0).start()
 
@@ -439,13 +496,26 @@
     load_home.start()
     for n in range(1, blocks):
         wa_load(n).start()
-    late = pl.ds(inner, wb.shape[1])
-    load_bc = pltpu.make_async_copy(fb.at[:, late], wb, w_sem.at[blocks])
-    load_out = pltpu.make_async_copy(fb.at[:, pl.ds(0, inner)], wo, w_sem.at[blocks + 2])
+    late = pl.ds(2 * inner, wb.shape[1])
+    load_bc = pltpu.make_async_copy(fw.at[:, late], wb, w_sem.at[blocks])
     load_old = pltpu.make_async_copy(prev, old, w_sem.at[blocks + 1])
     load_bc.start()
-    load_out.start()
     load_old.start()
+    load_mine.wait()
+    cut = inner // 2
+
+    def lines_of(c):
+        return pl.ds(pl.multiple_of(c * depth, 16), depth)
+
+    begin, near, beyond, beside, opposite, finish = torus_ring(
+        row, me, depth,
+        lambda h, c: wo.at[lines_of(c), pl.ds(h * cut, cut)],
+        lambda h: mine.at[:, pl.ds(h * cut, cut)],
+        lambda h, count: wo.at[pl.ds(0, count), pl.ds(h * cut, cut)],
+        gone, twin, arr,
+    )
+    keep_mine = pltpu.make_async_copy(mine, wo.at[lines_of(me), :], loc.at[4])
+    keep_mine.start()
     for copy in small[:-1]:
         copy.wait()
     pexf[...] = pex[...].astype(f32)
@@ -491,10 +561,16 @@
         at = slice(n * 128, (n + 1) * 128)
         gate[:, at] = jnp.where(left, z0, pltpu.roll(z1, HEAD_DIM, 1)).astype(bf16)
         xin[:, at] = jnp.where(left, pltpu.roll(z0, HEAD_DIM, 1), z1).astype(bf16)
+        if n == 0:
+            pl.semaphore_wait(barrier, cols - 1 + rows - 1)
+            begin()
+        if n == 2:
+            near()
     load_bc.wait()
     z = jnp.dot(hid[...].reshape(tokens, model), wb[...], preferred_element_type=f32)
     bc[...] = z[:, : 2 * STATE].astype(bf16)
     dts[...] = z[:, 2 * STATE :]
+    beyond()
     load_old.wait()
 
     def store(s):
@@ -629,11 +705,15 @@
                 new[s] = now.reshape(inner, STATE).astype(bf16)
                 store(s).start()
 
-    @pl.loop(held // GROUP, requests // GROUP)
+    group(held // GROUP, False)
+    beside()
+
+    @pl.loop(held // GROUP + 1, requests // GROUP)
     def _(i):
         group(i, False)
 
-    load_out.wait()
+    opposite()
+
     moving = held * LEN
     resting = tokens - moving
     width = part_c.shape[2]
@@ -663,7 +743,6 @@
 
     unrolled(cols * cap, 8, to_slots)
     others = pl.ds(0, (cols - 1) * cap)
-    pl.semaphore_wait(barrier, cols - 1 + rows - 1)
 
     def push_factors(d, carry):
         peer = (me + d) % cols
@@ -679,6 +758,9 @@
     keep_e = pltpu.make_async_copy(piece(emsg, me), piece(egot, me), loc.at[1])
     keep_x.start()
     keep_e.start()
+
+    finish()
+    keep_mine.wait()
 
     @pl.loop(0, held // GROUP)
     def _(i):
@@ -797,11 +879,11 @@
         store(s).wait()
 
 
-def mixer(tab, hid_c, hidden, fa, fb, vectors, prev, pex, peb, rows, cols, cap):
+def mixer(tab, hid_c, hidden, fw, w_out, vectors, prev, pex, peb, rows, cols, cap):
     requests, _, model = hidden.shape
     held = hid_c.shape[0]
     tokens = requests * LEN
-    inner = fa.shape[1] // 2
+    depth, inner = w_out.shape
     width = model // rows
     slots = cols * cap
     rest = requests - held
@@ -833,9 +915,9 @@
             pltpu.VMEM(peb.shape, dt),
             pltpu.VMEM((requests, LEN, model), dt),
             pltpu.VMEM((requests, LEN, model), dt),
-            pltpu.VMEM(fa.shape, dt),
-            pltpu.VMEM((fb.shape[0], fb.shape[1] - inner), dt),
-            pltpu.VMEM((fb.shape[0], inner), dt),
+            pltpu.VMEM((model, 2 * inner), dt),
+            pltpu.VMEM((model, fw.shape[1] - 2 * inner), dt),
+            pltpu.VMEM((model, inner), dt),
             pltpu.VMEM((held, inner, STATE), dt),
             pltpu.VMEM((tokens, inner), dt),
             pltpu.VMEM((tokens, inner), dt),
@@ -863,17 +945,18 @@
             pltpu.VMEM((held, LEN, width), dt),
             pltpu.VMEM((slots, LEN, width), dt),
             pltpu.VMEM((slots, LEN, width), dt),
-            dma(()), dma(()), dma((fa.shape[1] // 256 + 3,)), dma((held,)),
-            dma((len(vectors) + 3,)), dma((3,)), dma((3,)), dma((rows,)),
+            dma(()), dma(()), dma((2 * inner // 256 + 2,)), dma((held,)),
+            dma((len(vectors) + 3,)), dma((5,)), dma((3,)), dma((rows,)),
             dma((rows,)), dma((rows,)), dma((rows, held // GROUP)), dma((rows, held // GROUP)),
             dma(()), dma(()),
             dma(()), dma(()), dma(()), dma(()),
+            pltpu.VMEM(w_out.shape, dt), dma((2,)), dma((2,)), dma((2, cols)),
         ],
         compiler_params=pltpu.CompilerParams(
             collective_id=1, has_side_effects=True, vmem_limit_bytes=60 << 20
         ),
         name="mixer",
-    )(tab, hid_c, hidden, fa, fb, *vectors, prev, pex, peb)
+    )(tab, hid_c, hidden, fw, w_out, *vectors, prev, pex, peb)
 
 
 def arrive_kernel(
@@ -1003,13 +1086,13 @@
     code = owner + 64 * (continued == 1).astype(jnp.int32) + 128 * accepted
     tab = route(code.reshape(cols, requests), held)
     hidden = hidden.reshape(requests, LEN, model)
-    hid_c, fa, fb = gather_all(tab, hidden, w_zx, w_out, w_bc, w_dt.T, rows, cols, cap, held)
+    hid_c, fw = gather_all(tab, hidden, w_zx, w_bc, w_dt.T, rows, cols, cap, held)
     vectors = (
         dt_bias[None, :], a_log[None, :], d_skip[None, :],
         conv_x_w, conv_x_b[None, :], conv_bc_w, conv_bc_b[None, :], norm_gain[None, :],
     )
     mixed, moved, edge, xgot, egot = mixer(
-        tab, hid_c, hidden, fa, fb, vectors, prev_state.reshape(held, inner, STATE),
+        tab, hid_c, hidden, fw, w_out, vectors, prev_state.reshape(held, inner, STATE),
         prev_edge_x.transpose(1, 0, 2), prev_edge_bc.transpose(1, 0, 2),
         rows, cols, cap,
     )

time: 105 us -> 104 us (level); the launches traced: 103 us -> 104 us
    pallas_call x1, Pallas kernels: 53.6 us -> 57.3 us  [mixer(): pl.pallas_call(body, out_shape=(jax.ShapeDtypeStruct((requests, LEN, widt...]
    pallas_call x1, Pallas kernels: 38.8 us -> 35.5 us  [gather_all(): pl.pallas_call(body, out_shape=(jax.ShapeDtypeStruct((held, LEN, model),...]
where the time goes in v8:
time: 104 us
  Pallas kernels  101 us (97%)
  local copies, waits for them, and re-layouts  1.5 us (1%)
    pallas_call x1, Pallas kernels, mixer(): pl.pallas_call(body, out_shape=(jax.ShapeDtypeStruct((requests, LEN, widt...  57.3 us
    pallas_call x1, Pallas kernels, gather_all(): pl.pallas_call(body, out_shape=(jax.ShapeDtypeStruct((held, LEN, model),...  35.5 us
    pallas_call x1, Pallas kernels, arrive(): pl.pallas_call(arrive_kernel, out_shape=(jax.ShapeDtypeStruct((requests,...  6.11 us

profile of v8, /device:TPU:1, one launch (start us, length us, event | category | flops | bytes accessed | tf_op | source)
XLA Modules:
  0.0 103.6 jit_solution(2711092131792383659)
XLA Ops:
  0.6 0.7 multiply_add_fusion
  1.4 0.7 reshape.23.refs_0_
  2.1 1.8 %route.1.refs_0_.tab_in = s32[16,128]{1,0:T(8,128)} custom-call(s32[32,48]{1,0:T(8,128)} %reshape.23.refs_0_), custom_call_target="tpu_custom_call" | custom-call | tf_op jit(solution)/shard_map/route/pallas_call | solution.py:123
  3.8 35.5 %gather_all.1 = (bf16[24,16,1536]{2,1,0:T(8,128)(2,1)}, bf16[1536,1408]{1,0:T(8,128)(2,1)}) custom-call(s32[16,128]{1,0:T(8,128)} %route.1.refs_0_.tab_in, bf16[48,16,1536]{2,1,0:T(8,128)(2,1)} %bitcast.15, bf16[48,1024]{1,0:T(8,128)(2,1)} %refs_2_.1, bf16[48,256]{1,0:T(8,128)(2,1)} %refs_3_.1, bf16[8,48]{1,0:T(8,128)(2,1)} %bitcast.23), custom_call_target="tpu_custom_call" | custom-call | tf_op jit(solution)/shard_map/gather_all/pallas_call | solution.py:412
  39.3 57.3 %mixer.1 = (bf16[48,16,384]{2,1,0:T(8,128)(2,1)}, bf16[24,512,128]{2,1,0:T(8,128)(2,1)}, bf16[24,4,768]{2,1,0:T(4,128)(2,1)}, bf16[64,16,640]{2,1,0:T(8,128)(2,1)}, bf16[64,4,768]{2,1,0:T(4,128)(2,1)}) custom-call(s32[16,128]{1,0:T(8,128)} %route.1.refs_0_.tab_in, bf16[24,16,1536]{2,1,0:T(8,128)(2,1)} %get-tuple-element.14.refs_1_, ...), custom_call_target="tpu_custom_call" | custom-call | tf_op jit(solution)/shard_map/mixer/pallas_call | solution.py:900
  96.6 0.0 copy-start
  96.6 6.1 %arrive.1 = (bf16[48,512,128]{2,1,0:T(8,128)(2,1)}, bf16[3,48,512]{2,1,0:T(8,128)(2,1)}, bf16[3,48,256]{2,1,0:T(8,128)(2,1)}) custom-call(s32[16,128]{1,0:T(8,128)} %route.1.refs_0_.tab_in, bf16[64,16,640]{2,1,0:T(8,128)(2,1)} %get-tuple-element.17.xgot_in, bf16[64,4,768]{2,1,0:T(4,128)(2,1)} %get-tuple-element.18.egot_in, ...), custom_call_target="tpu_custom_call" | custom-call | tf_op jit(solution)/shard_map/arrive/pallas_call | solution.py:1045
  102.7 0.0 copy-done
  102.8 0.8 copy.24
Async XLA Ops:
  96.6 6.1 %copy-start = (bf16[48,16,384]{2,1,0:T(8,128)(2,1)S(1)}, bf16[48,16,384]{2,1,0:T(8,128)(2,1)}, u32[]{:S(2)}) copy-start(bf16[48,16,384]{2,1,0:T(8,128)(2,1)} %get-tuple-element.16) | copy-start | bytes 1769476

commit v9 on v8

--- a/solution.py
+++ b/solution.py
@@ -114,19 +114,6 @@
 SEND, PICK, BACK, FROM_MSG, FROM_MIX, MOVED, STAY, STAY_KEY, STAY_ACC, ACC, POS, PICK_O, POS_O, LEAVE = range(14)
 
 
-def route(code, held):
-    vmem = pl.BlockSpec(memory_space=pltpu.VMEM)
-
-    def body(*refs):
-        route_kernel(held, *refs)
-
-    return pl.pallas_call(
-        body, out_shape=jax.ShapeDtypeStruct((16, 128), jnp.int32),
-        in_specs=[vmem], out_specs=vmem, name="route",
-        compiler_params=pltpu.CompilerParams(vmem_limit_bytes=60 << 20),
-    )(code)
-
-
 def unrolled(count, step, body):
     def some(i, carry):
         for k in range(step):
@@ -245,8 +232,8 @@
 
 
 def gather_kernel(
-    rows, cols, cap, tab_in, hidden, w_zx, w_bc, w_dt_in, hid_full, fw,
-    tab, w_dt, ws, sl, packed0, packed1, got0, got1, own0, own1, loc, a2a_s, a2a_r, gone, twin, arr, y_s, y_r,
+    rows, cols, cap, code, hidden, w_zx, w_bc, w_dt_in, hid_full, fw, tab_out,
+    table, tab, w_dt, ws, sl, packed0, packed1, got0, got1, own0, own1, loc, a2a_s, a2a_r, gone, twin, arr, y_s, y_r,
 ):
     row, me = lax.axis_index("row"), lax.axis_index("col")
     barrier = greet(row, me, rows, cols)
@@ -280,13 +267,17 @@
     states = w_bc.shape[1]
     heads = w_dt_in.shape[0]
     loads = (
-        pltpu.make_async_copy(tab_in, tab, loc.at[5]),
         pltpu.make_async_copy(w_dt_in, w_dt, loc.at[6]),
         pltpu.make_async_copy(w_zx, ws.at[:, pl.ds(0, inner)], loc.at[7]),
         pltpu.make_async_copy(w_bc, ws.at[:, pl.ds(inner, states)], loc.at[8]),
     )
     for copy in loads:
         copy.start()
+    route_kernel(own0.shape[0], code, table)
+    to_scalars = pltpu.make_async_copy(table, tab, loc.at[5])
+    to_scalars.start()
+    keep_t = pltpu.make_async_copy(table, tab_out, loc.at[2])
+    keep_t.start()
     for copy in loads:
         copy.wait()
     square = jnp.concatenate(
@@ -297,6 +288,7 @@
     keep_w = pltpu.make_async_copy(ws, fw.at[lines(me), :], loc.at[1])
     keep_w.start()
     load.wait()
+    to_scalars.wait()
 
     def piece(ref, c):
         return ref.at[pl.ds(c * cap, cap)]
@@ -306,7 +298,8 @@
         packed, got, low = packs[k], gots[k], lows[k]
 
         def pack(s):
-            packed[s] = sl[tab[SEND, s], :, low : low + packed.shape[2]]
+            j = jnp.clip(tab[SEND, s], 0, sl.shape[0] - 1)
+            packed[s] = sl[j, :, low : low + packed.shape[2]]
 
         unrolled(cols * cap, 8, pack)
         if k == 0:
@@ -352,7 +345,7 @@
         pltpu.make_async_copy(got.at[others], got.at[others], a2a_r.at[k]).wait()
 
         def unpack(s):
-            own[s] = got[tab[PICK, s]]
+            own[s] = got[jnp.clip(tab[PICK, s], 0, got.shape[0] - 1)]
 
         unrolled(own.shape[0], 8, unpack)
         for n, dest in ((0, right), (1, left)):
@@ -385,6 +378,7 @@
 
     finish()
     keep_w.wait()
+    keep_t.wait()
     keeps[2].wait()
     keeps[3].wait()
 
@@ -397,7 +391,7 @@
             pltpu.make_async_copy(spot, spot, y_s.at[k, n]).wait()
 
 
-def gather_all(tab, hidden, w_zx, w_bc, w_dt, rows, cols, cap, held):
+def gather_all(code, hidden, w_zx, w_bc, w_dt, rows, cols, cap, held):
     requests, _, model = hidden.shape
     width = model // rows
     dt = hidden.dtype
@@ -414,11 +408,13 @@
         out_shape=(
             jax.ShapeDtypeStruct((held, LEN, model), dt),
             jax.ShapeDtypeStruct((depth * cols, wide), dt),
+            jax.ShapeDtypeStruct((16, 128), jnp.int32),
         ),
-        in_specs=[hbm] * 5,
-        out_specs=(hbm, hbm),
+        in_specs=[pl.BlockSpec(memory_space=pltpu.VMEM)] + [hbm] * 4,
+        out_specs=(hbm, hbm, hbm),
         scratch_shapes=[
-            pltpu.SMEM(tab.shape, jnp.int32),
+            pltpu.VMEM((16, 128), jnp.int32),
+            pltpu.SMEM((16, 128), jnp.int32),
             pltpu.VMEM(w_dt.shape, dt),
             pltpu.VMEM((depth, wide), dt),
             pltpu.VMEM((requests, LEN, width), dt),
@@ -436,7 +432,7 @@
             collective_id=0, has_side_effects=True, vmem_limit_bytes=60 << 20
         ),
         name="gather_all",
-    )(tab, hidden, w_zx, w_bc, w_dt)
+    )(code, hidden, w_zx, w_bc, w_dt)
 
 
 def silu(v):
@@ -979,12 +975,6 @@
         return pltpu.make_async_copy(was.at[s], nst.at[tab[POS, s]], m_sem.at[s])
 
     loads[1].wait()
-    loads[2].wait()
-
-    @pl.loop(0, count)
-    def _(s):
-        place(s).start()
-
     t_ids, _ = token_masks()
     none = jnp.zeros((TOK, STATE), bf16)
 
@@ -1012,6 +1002,12 @@
                 u = i * GROUP + 2 * pair + k
                 new[u] = out[:, k * STATE : (k + 1) * STATE]
                 store(u).start()
+
+    loads[2].wait()
+
+    @pl.loop(0, count)
+    def _(s):
+        place(s).start()
 
     for copy in loads[3:]:
         copy.wait()
@@ -1084,9 +1080,9 @@
     held = prev_state.shape[0]
     cap = 2 * ((requests // 4 + cols - 1) // cols)
     code = owner + 64 * (continued == 1).astype(jnp.int32) + 128 * accepted
-    tab = route(code.reshape(cols, requests), held)
+    code = code.reshape(cols, requests)
     hidden = hidden.reshape(requests, LEN, model)
-    hid_c, fw = gather_all(tab, hidden, w_zx, w_bc, w_dt.T, rows, cols, cap, held)
+    hid_c, fw, tab = gather_all(code, hidden, w_zx, w_bc, w_dt.T, rows, cols, cap, held)
     vectors = (
         dt_bias[None, :], a_log[None, :], d_skip[None, :],
         conv_x_w, conv_x_b[None, :], conv_bc_w, conv_bc_b[None, :], norm_gain[None, :],

time: 104 us -> 103 us (level)
  Pallas kernels: 101 us -> 99.5 us
    pallas_call x1 -> x0, Pallas kernels: 1.79 us -> none  [route(): pl.pallas_call(body, out_shape=jax.ShapeDtypeStruct((16, 128), jnp.int32)...]
where the time goes in v9:
time: 103 us; the launch traced here: 102 us
  Pallas kernels  99.5 us (97%)
  local copies, waits for them, and re-layouts  1.5 us (1%)
    pallas_call x1, Pallas kernels, mixer(): pl.pallas_call(body, out_shape=(jax.ShapeDtypeStruct((requests, LEN, widt...  57.4 us
    pallas_call x1, Pallas kernels, gather_all(): pl.pallas_call(body, out_shape=(jax.ShapeDtypeStruct((held, LEN, model),...  36.1 us
    pallas_call x1, Pallas kernels, arrive(): pl.pallas_call(arrive_kernel, out_shape=(jax.ShapeDtypeStruct((requests,...  5.97 us

profile of v9, /device:TPU:1, one launch (start us, length us, event | category | flops | bytes accessed | tf_op | source)
XLA Modules:
  0.0 102.4 jit_solution(12561961103501058406)
XLA Ops:
  0.6 0.7 multiply_add_fusion
  1.4 0.7 reshape.23.refs_0_
  2.1 36.1 %gather_all.1 = (bf16[24,16,1536]{2,1,0:T(8,128)(2,1)}, bf16[1536,1408]{1,0:T(8,128)(2,1)}, s32[16,128]{1,0:T(8,128)}) custom-call(s32[32,48]{1,0:T(8,128)} %reshape.23.refs_0_, bf16[48,16,1536]{2,1,0:T(8,128)(2,1)} %bitcast.15, bf16[48,1024]{1,0:T(8,128)(2,1)} %refs_2_.1, bf16[48,256]{1,0:T(8,128)(2,1)} %refs_3_.1, bf16[8,48]{1,0:T(8,128)(2,1)} %bitcast.23), custom_call_target="tpu_custom_call" | custom-call | tf_op jit(solution)/shard_map/gather_all/pallas_call | solution.py:406
  38.2 57.4 %mixer.1 = (bf16[48,16,384]{2,1,0:T(8,128)(2,1)}, bf16[24,512,128]{2,1,0:T(8,128)(2,1)}, bf16[24,4,768]{2,1,0:T(4,128)(2,1)}, bf16[64,16,640]{2,1,0:T(8,128)(2,1)}, bf16[64,4,768]{2,1,0:T(4,128)(2,1)}) custom-call(s32[16,128]{1,0:T(8,128)} %get-tuple-element.15.refs_0_.tab_in, bf16[24,16,1536]{2,1,0:T(8,128)(2,1)} %get-tuple-element.16.refs_1_, ...), custom_call_target="tpu_custom_call" | custom-call | tf_op jit(solution)/shard_map/mixer/pallas_call | solution.py:896
  95.6 0.0 copy-start
  95.6 6.0 %arrive.1 = (bf16[48,512,128]{2,1,0:T(8,128)(2,1)}, bf16[3,48,512]{2,1,0:T(8,128)(2,1)}, bf16[3,48,256]{2,1,0:T(8,128)(2,1)}) custom-call(s32[16,128]{1,0:T(8,128)} %get-tuple-element.15.refs_0_.tab_in, bf16[64,16,640]{2,1,0:T(8,128)(2,1)} %get-tuple-element.19.xgot_in, bf16[64,4,768]{2,1,0:T(4,128)(2,1)} %get-tuple-element.20.egot_in, ...), custom_call_target="tpu_custom_call" | custom-call | tf_op jit(solution)/shard_map/arrive/pallas_call | solution.py:1041
  101.5 0.0 copy-done
  101.6 0.8 copy.24
Async XLA Ops:
  95.6 6.0 %copy-start = (bf16[48,16,384]{2,1,0:T(8,128)(2,1)S(1)}, bf16[48,16,384]{2,1,0:T(8,128)(2,1)}, u32[]{:S(2)}) copy-start(bf16[48,16,384]{2,1,0:T(8,128)(2,1)} %get-tuple-element.18) | copy-start | bytes 1769476

commit v10 on v9

--- a/solution.py
+++ b/solution.py
@@ -737,7 +737,7 @@
         xmsg[q] = sent[n]
         emsg[q] = edge_o[n]
 
-    unrolled(cols * cap, 8, to_slots)
+    unrolled(cols * cap, 16, to_slots)
     others = pl.ds(0, (cols - 1) * cap)
 
     def push_factors(d, carry):
@@ -1012,8 +1012,7 @@
     for copy in loads[3:]:
         copy.wait()
 
-    @pl.loop(0, count)
-    def _(u):
+    def edges(u):
         for source, k, spot in (
             (egot, tab[PICK_O, u], tab[POS_O, u]), (edge, u, tab[POS, u])
         ):
@@ -1023,6 +1022,7 @@
                 ex[q, at, :] = lines[q : q + 1, :inner]
                 eb[q, at, :] = lines[q : q + 1, inner:]
 
+    unrolled(count, 8, edges)
     nex[...] = ex[...].astype(bf16)
     neb[...] = eb[...].astype(bf16)
 

time: 103 us -> 103 us (level)
  no operation moved by 1% of the time
where the time goes in v10:
time: 103 us; the launch traced here: 102 us
  Pallas kernels  99.5 us (97%)
  local copies, waits for them, and re-layouts  1.5 us (1%)
    pallas_call x1, Pallas kernels, mixer(): pl.pallas_call(body, out_shape=(jax.ShapeDtypeStruct((requests, LEN, widt...  57.4 us
    pallas_call x1, Pallas kernels, gather_all(): pl.pallas_call(body, out_shape=(jax.ShapeDtypeStruct((held, LEN, model),...  36.1 us
    pallas_call x1, Pallas kernels, arrive(): pl.pallas_call(arrive_kernel, out_shape=(jax.ShapeDtypeStruct((requests,...  5.96 us

profile of v10, /device:TPU:1, one launch (start us, length us, event | category | flops | bytes accessed | tf_op | source)
XLA Modules:
  0.0 102.4 jit_solution(7563449242448435941)
XLA Ops:
  0.6 0.7 multiply_add_fusion
  1.4 0.7 reshape.23.refs_0_
  2.1 36.1 %gather_all.1 = (bf16[24,16,1536]{2,1,0:T(8,128)(2,1)}, bf16[1536,1408]{1,0:T(8,128)(2,1)}, s32[16,128]{1,0:T(8,128)}) custom-call(s32[32,48]{1,0:T(8,128)} %reshape.23.refs_0_, bf16[48,16,1536]{2,1,0:T(8,128)(2,1)} %bitcast.15, bf16[48,1024]{1,0:T(8,128)(2,1)} %refs_2_.1, bf16[48,256]{1,0:T(8,128)(2,1)} %refs_3_.1, bf16[8,48]{1,0:T(8,128)(2,1)} %bitcast.23), custom_call_target="tpu_custom_call" | custom-call | tf_op jit(solution)/shard_map/gather_all/pallas_call | solution.py:406
  38.2 57.4 %mixer.1 = (bf16[48,16,384]{2,1,0:T(8,128)(2,1)}, bf16[24,512,128]{2,1,0:T(8,128)(2,1)}, bf16[24,4,768]{2,1,0:T(4,128)(2,1)}, bf16[64,16,640]{2,1,0:T(8,128)(2,1)}, bf16[64,4,768]{2,1,0:T(4,128)(2,1)}) custom-call(s32[16,128]{1,0:T(8,128)} %get-tuple-element.15.refs_0_.tab_in, bf16[24,16,1536]{2,1,0:T(8,128)(2,1)} %get-tuple-element.16.refs_1_, ...), custom_call_target="tpu_custom_call" | custom-call | tf_op jit(solution)/shard_map/mixer/pallas_call | solution.py:896
  95.6 0.0 copy-start
  95.6 6.0 %arrive.1 = (bf16[48,512,128]{2,1,0:T(8,128)(2,1)}, bf16[3,48,512]{2,1,0:T(8,128)(2,1)}, bf16[3,48,256]{2,1,0:T(8,128)(2,1)}) custom-call(s32[16,128]{1,0:T(8,128)} %get-tuple-element.15.refs_0_.tab_in, bf16[64,16,640]{2,1,0:T(8,128)(2,1)} %get-tuple-element.19.xgot_in, bf16[64,4,768]{2,1,0:T(4,128)(2,1)} %get-tuple-element.20.egot_in, ...), custom_call_target="tpu_custom_call" | custom-call | tf_op jit(solution)/shard_map/arrive/pallas_call | solution.py:1041
  101.6 0.0 copy-done
  101.6 0.8 copy.24
Async XLA Ops:
  95.6 6.0 %copy-start = (bf16[48,16,384]{2,1,0:T(8,128)(2,1)S(1)}, bf16[48,16,384]{2,1,0:T(8,128)(2,1)}, u32[]{:S(2)}) copy-start(bf16[48,16,384]{2,1,0:T(8,128)(2,1)} %get-tuple-element.18) | copy-start | bytes 1769476
